TPU v7x, 256 devices: a whole 4x4x8 slice. The times are simulated.
256 devices in a mesh: row: 16 (over z_lo, x, core), col: 16 (over y, z_hi).
Axes of the slice: x: 4, y: 4, z: 8 (z_hi: 4, z_lo: 2; z = z_hi * 2 + z_lo), core: 2. Of those that a mesh axis runs over, the one named last changes fastest.
Arguments:
- object_field: float32 [2, 8192, 8192], P(None, 'row', 'col'), may hold values from -5 to 5
- probe: float32 [2, 256, 256], replicated, may hold values from -5 to 5
- amplitude: float32 [16, 16, 8, 256, 256], P('row', 'col'), may hold values from 0.2 to 3
- offsets: int32 [16, 16, 8, 2], P('row', 'col'), may hold values from 0 to 511
Outputs:
- object_grad: float32 [2, 8192, 8192], P(None, 'row', 'col')
- probe_grad: float32 [2, 256, 256], replicated
All inputs are finite; a program needn't handle non-finite values.
Results may differ from a plain program's by a relative error of at most 0.0003.
Values sent between devices are 32-bit elements; how exact they have to be, the bound alone decides.
No kernel may reach another device: no remote copies, remote signals or barrier semaphores. Data moves between devices by JAX's collectives and lax.ppermute only.
A program may use at most 64 MiB of HBM per device.

v0:
```python
import math

import jax
import jax.numpy as jnp
from jax import lax
from jax.sharding import PartitionSpec as P


def passed_along(value, axis, steps):
    count = lax.axis_size(axis)
    first, last = (max(0, -steps), min(count, count - steps))
    return lax.ppermute(value, axis, [(source, source + steps) for source in range(first, last)])


def tables(size):
    index = jnp.arange(size, dtype=jnp.int32)
    product = index[:, None] * index[None, :] % size
    angle = product.astype(jnp.float32) * (2.0 * math.pi / size)
    scale = 1.0 / math.sqrt(size)
    return (jnp.cos(angle) * scale, jnp.sin(angle) * scale)


def matmul(left, right):
    return jnp.dot(left, right, precision=lax.Precision.HIGHEST, preferred_element_type=jnp.float32)


def transform(real_part, imag_part, cosine, sine, sign):
    left_r = matmul(cosine, real_part) - sign * matmul(sine, imag_part)
    left_i = matmul(cosine, imag_part) + sign * matmul(sine, real_part)
    out_r = matmul(left_r, cosine) - sign * matmul(left_i, sine)
    out_i = matmul(left_i, cosine) + sign * matmul(left_r, sine)
    return (out_r, out_i)


def patch_terms(view, probe, amp, cosine, sine):
    probe_r, probe_i = (probe[0], probe[1])
    view_r, view_i = (view[0], view[1])
    wave_r = probe_r * view_r - probe_i * view_i
    wave_i = probe_r * view_i + probe_i * view_r
    far_r, far_i = transform(wave_r, wave_i, cosine, sine, -1.0)
    modulus = jnp.sqrt(far_r * far_r + far_i * far_i)
    keep = 1.0 - amp / jnp.maximum(modulus, 0.5)
    chi_r, chi_i = transform(far_r * keep, far_i * keep, cosine, sine, 1.0)
    obj_term = jnp.stack([probe_r * chi_r + probe_i * chi_i, probe_r * chi_i - probe_i * chi_r])
    probe_term = jnp.stack([view_r * chi_r + view_i * chi_i, view_r * chi_i - view_i * chi_r])
    return (obj_term, probe_term)


def shards(object_field, probe, amplitude, offsets):
    tile_rows = object_field.shape[1]
    tile_cols = object_field.shape[2]
    side = probe.shape[1]
    positions = offsets.shape[2]
    cosine, sine = tables(side)
    below = passed_along(object_field[:, :side, :], "row", -1)
    tall = jnp.concatenate([object_field, below], axis=1)
    right = passed_along(tall[:, :, :side], "col", -1)
    extended = jnp.concatenate([tall, right], axis=2)

    def step(number, carry):
        grad, probe_acc = carry
        off = offsets[0, 0, number]
        top = off[0]
        left = off[1]
        zero = jnp.zeros((), jnp.int32)
        view = lax.dynamic_slice(extended, (zero, top, left), (2, side, side))
        obj_term, probe_term = patch_terms(view, probe, amplitude[0, 0, number], cosine, sine)
        old = lax.dynamic_slice(grad, (zero, top, left), (2, side, side))
        grad = lax.dynamic_update_slice(grad, old + obj_term, (zero, top, left))
        return (grad, probe_acc + probe_term)

    start = (jnp.zeros(extended.shape, jnp.float32), jnp.zeros((2, side, side), jnp.float32))
    grad, probe_acc = lax.fori_loop(0, positions, step, start)
    returned = passed_along(grad[:, :, tile_cols:], "col", 1)
    tall_grad = grad[:, :, :tile_cols].at[:, :, :side].add(returned)
    returned_rows = passed_along(tall_grad[:, tile_rows:, :], "row", 1)
    object_grad = tall_grad[:, :tile_rows, :].at[:, :side, :].add(returned_rows)
    probe_total = lax.psum(probe_acc, ("row", "col"))
    count = positions * lax.axis_size("row") * lax.axis_size("col")
    return (object_grad, probe_total / count)


def solution(mesh):
    placed = (
        P(None, "row", "col"),
        P(),
        P("row", "col", None, None, None),
        P("row", "col", None, None),
    )
    return jax.shard_map(
        shards, mesh=mesh, in_specs=placed, out_specs=(P(None, "row", "col"), P()), check_vma=False
    )
```

profile of v0, /device:TPU:31, one launch (start us, length us, event | category | flops | bytes accessed | tf_op | source)
XLA Modules:
  0.0 772.3 jit_solution(15942112181140656353)
XLA Ops:
  8.7 2.6 collective-permute-start
  11.4 53.6 %collective-permute-done = f32[2,256,512]{2,1,0:T(8,128)S(1)} collective-permute-done((f32[2,256,512]{2,1,0:T(8,128)S(1)}, f32[2,256,512]{2,1,0:T(8,128)S(1)}, u32[]{:S(2)}, u32[]{:S(2)}) %collective-permute-start) | collective-permute-done | bytes 1048608 | tf_op jit(solution)/shard_map/ppermute | solution.py:12
  67.3 7.7 collective-permute-start.1
  75.0 20.1 %collective-permute-done.1 = f32[2,768,256]{2,1,0:T(8,128)S(1)} collective-permute-done((f32[2,768,256]{2,1,0:T(8,128)}, f32[2,768,256]{2,1,0:T(8,128)S(1)}, u32[]{:S(2)}, u32[]{:S(2)}) %collective-permute-start.1) | collective-permute-done | bytes 1572896 | tf_op jit(solution)/shard_map/ppermute | solution.py:12
  95.1 4.4 pad_maximum_fusion
  102.0 316.3 %while.19 = (s32[]{:T(128)}, f32[2,768,768]{2,1,0:T(8,128)}, f32[2,256,256]{2,1,0:T(8,128)S(1)}, s32[1,1,8,2]{2,3,1,0:T(2,128)S(1)}, f32[2,256,256]{2,1,0:T(8,12...) while((s32[]{:T(128)}, f32[2,768,768]{2,1,0:T(8,128)}, ...), condition=%wide.region_1.2_spmd.clone.clone, body=%wide.region_0.1_spmd.clone.clone.sunk | while | flops 3240099840 | bytes 19136796 | solution.py:73
  117.9 2.5 fusion.184
  130.8 2.7 add_bitcast_fusion.2
  135.0 6.8 dynamic_update_slice.10
  157.7 2.5 fusion.184
  170.6 2.7 add_bitcast_fusion.2
  174.8 6.8 dynamic_update_slice.10
  197.5 2.5 fusion.184
  210.4 2.7 add_bitcast_fusion.2
  214.6 6.4 dynamic_update_slice.10
  236.9 2.5 fusion.184
  249.8 2.7 add_bitcast_fusion.2
  254.0 6.1 dynamic_update_slice.10
  276.0 2.5 fusion.184
  288.9 2.7 add_bitcast_fusion.2
  293.1 6.8 dynamic_update_slice.10
  315.8 2.5 fusion.184
  328.7 2.7 add_bitcast_fusion.2
  332.9 6.5 dynamic_update_slice.10
  355.3 2.5 fusion.184
  368.3 2.7 add_bitcast_fusion.2
  372.5 6.8 dynamic_update_slice.10
  395.1 2.5 fusion.184
  408.1 2.7 add_bitcast_fusion.2
  412.3 6.1 dynamic_update_slice.10
  424.2 37.8 %collective-permute-done.2 = f32[2,768,256]{2,1,0:T(8,128)S(1)} collective-permute-done((f32[2,768,256]{2,1,0:T(8,128)S(1)}, f32[2,768,256]{2,1,0:T(8,128)S(1)}, u32[]{:S(2)}, u32[]{:S(2)}) %collective-permute-start.2) | collective-permute-done | bytes 1572896 | tf_op jit(solution)/shard_map/ppermute | solution.py:12
  467.4 291.7 %all-reduce.2.cloned.1.call-done = f32[2,256,256]{2,1,0:T(8,128)} async-done(((f32[2,256,256]{2,1,0:T(8,128)}), f32[2,256,256]{2,1,0:T(8,128)}) %all-reduce.2.cloned.1.call-update) | async-done | bytes 524304 | tf_op jit(solution)/shard_map/psum | solution.py:78
  (176 shorter events, 216.4 us)
Async XLA Ops:
  7.2 4.1 copy-start.4
  7.2 751.9 %all-reduce.2.cloned.1.call-start = ((), (), s32[]{:S(2)}) async-start(), calls=%async_computation | async-start | bytes 1048576 | tf_op jit(solution)/shard_map/psum | solution.py:78
  8.7 56.4 %collective-permute-start = (f32[2,256,512]{2,1,0:T(8,128)S(1)}, f32[2,256,512]{2,1,0:T(8,128)S(1)}, u32[]{:S(2)}, u32[]{:S(2)}) collective-permute-start(f32[2,256,512]{2,1,0:T(8,128)S(1)} %slice.112), channel_id=1, source_target_pairs={{16,0},{32,16},{48,32},{64,48},{80,64},{96,80},{112,96},{128,112},... | collective-permute-start | bytes 3145736 | tf_op jit(solution)/shard_map/ppermute | solution.py:12
  65.2 2.2 copy-start.3
  67.3 27.8 %collective-permute-start.1 = (f32[2,768,256]{2,1,0:T(8,128)}, f32[2,768,256]{2,1,0:T(8,128)S(1)}, u32[]{:S(2)}, u32[]{:S(2)}) collective-permute-start(f32[2,768,256]{2,1,0:T(8,128)} %slice.132), channel_id=1, source_target_pairs={{1,0},{2,1},{3,2},{4,3},{5,4},{6,5},{7,6},{8,7},{9,8},{10,9},{11,1... | collective-permute-start | bytes 4718600 | tf_op jit(solution)/shard_map/ppermute | solution.py:12
  99.6 2.5 copy-start
  99.6 2.5 copy-start.6
  418.4 5.8 copy-start.1
  420.1 41.9 %collective-permute-start.2 = (f32[2,768,256]{2,1,0:T(8,128)S(1)}, f32[2,768,256]{2,1,0:T(8,128)S(1)}, u32[]{:S(2)}, u32[]{:S(2)}) collective-permute-start(f32[2,768,256]{2,1,0:T(8,128)S(1)} %slice.116), channel_id=1, source_target_pairs={{0,1},{1,2},{2,3},{3,4},{4,5},{5,6},{6,7},{7,8},{8,9},{9,10},{10,1... | collective-permute-start | bytes 4718600 | tf_op jit(solution)/shard_map/ppermute | solution.py:12
  463.7 1.7 copy-start.2
  465.4 297.3 %collective-permute-start.3 = (f32[2,256,512]{2,1,0:T(8,128)S(1)}, f32[2,256,512]{2,1,0:T(8,128)S(1)}, u32[]{:S(2)}, u32[]{:S(2)}) collective-permute-start(f32[2,256,512]{2,1,0:T(8,128)S(1)} %slice.135), channel_id=1, source_target_pairs={{0,16},{16,32},{32,48},{48,64},{64,80},{80,96},{96,112},{112,128},... | collective-permute-start | bytes 3145736 | tf_op jit(solution)/shard_map/ppermute | solution.py:12
  764.2 1.3 copy-start.5
Sparse Core Ops, SparseCore 0:
  467.5 291.5 all-reduce.1
where the time goes:
time: 778 us; the launch traced here: 772 us
  waiting for transfers between devices  403 us (52%)
  matrix products  207 us (27%)
  local copies, waits for them, and re-layouts  72.1 us (9%)
  other arithmetic  32.1 us (4%)
  loops' own time  29.7 us (4%)
  between operations  14.2 us (2%)
  starting transfers between devices  14.1 us (2%)
    psum x1, waiting for transfers between devices, shards(): probe_total = lax.psum(probe_acc, ('row', 'col'))  292 us
    dot_general x128, matrix products, matmul(): jnp.dot(left, right, precision=lax.Precision.HIGHEST, preferred_element_t...  207 us
    ppermute x4, waiting for transfers between devices, passed_along(): lax.ppermute(value, axis, [(source, source + steps) for source in range(f...  112 us
    dynamic_update_slice x8, local copies, waits for them, and re-layouts, step(): grad = lax.dynamic_update_slice(grad, old + obj_term, (zero, top, left))  52.3 us
    another operation x1, loops' own time, shards(): grad, probe_acc = lax.fori_loop(0, positions, step, start)  29.7 us
  transfers between devices with their start and end apart: 5, of which 4 were waited for; matrix products, arithmetic and copies ran while one was open for 1% of the time, Pallas kernels for 0%

commit v1 on v0

v1 whole, which is shorter than its diff:
```python
import functools
import math

import jax
import jax.numpy as jnp
import numpy as np
from jax import lax
from jax.experimental import pallas as pl
from jax.experimental.pallas import tpu as pltpu
from jax.sharding import PartitionSpec as P

F32 = jnp.float32
BF16 = jnp.bfloat16


def passed_along(value, axis, steps):
    count = lax.axis_size(axis)
    first, last = (max(0, -steps), min(count, count - steps))
    return lax.ppermute(value, axis, [(source, source + steps) for source in range(first, last)])


def split(value):
    high = value.astype(BF16)
    return high, (value - high.astype(F32)).astype(BF16)


def dft_tables(size):
    index = np.arange(size)
    angle = (index[:, None] * index[None, :] % size) * (2.0 * math.pi / size)
    cosine = (np.cos(angle) / math.sqrt(size)).astype(np.float32)
    sine = (np.sin(angle) / math.sqrt(size)).astype(np.float32)
    forward = np.concatenate([np.concatenate([cosine, -sine], 1), np.concatenate([sine, cosine], 1)], 0)
    backward = np.concatenate([np.concatenate([cosine, sine], 1), np.concatenate([-sine, cosine], 1)], 0)
    stacked = np.concatenate([cosine, sine], 0)
    return stacked, forward, backward


def dot(left, right):
    return jnp.dot(left, right, preferred_element_type=F32)


def dot3(left, right):
    return dot(left[0], right[0]) + (dot(left[0], right[1]) + dot(left[1], right[0]))


def both_sides(real_part, imag_part, stacked, wide, sign):
    side = real_part.shape[0]
    columns = split(jnp.concatenate([real_part, imag_part], axis=1))
    product = dot3(stacked, columns)
    cos_r, cos_i = product[:side, :side], product[:side, side:]
    sin_r, sin_i = product[side:, :side], product[side:, side:]
    left = split(jnp.concatenate([cos_r - sign * sin_i, cos_i + sign * sin_r], axis=1))
    out = dot3(left, wide)
    return out[:, :side], out[:, side:]


def patches_kernel(off, tile, right, bottom, corner, probe, amp, stacked, forward, backward,
                   main_out, right_out, bottom_out, corner_out, probe_out, ext, grad):
    side = probe.shape[1]
    rows, cols = tile.shape[1], tile.shape[2]
    ext[:, :rows, :cols] = tile[...]
    ext[:, :rows, cols:] = right[...]
    ext[:, rows:, :cols] = bottom[...]
    ext[:, rows:, cols:] = corner[...]
    grad[...] = jnp.zeros_like(grad)
    probe_out[...] = jnp.zeros_like(probe_out)

    def step(number, carry):
        top = off[number, 0]
        left = off[number, 1]
        row_base = pl.multiple_of(top // 8 * 8, 8)
        base = pl.multiple_of(left // 128 * 128, 128)
        row = top - row_base
        lane = left - base
        tall, span = side + 8, side + 128
        up = lax.rem(tall - row, tall)
        back = lax.rem(span - lane, span)
        pr, pi = probe[0], probe[1]

        def window(part):
            block = ext[part, pl.ds(row_base, tall), pl.ds(base, span)]
            return pltpu.roll(pltpu.roll(block, back, 1)[:, :side], up, 0)[:side]

        vr, vi = window(0), window(1)
        fr, fi = both_sides(pr * vr - pi * vi, pr * vi + pi * vr,
                            (stacked[0], stacked[1]), (forward[0], forward[1]), -1.0)
        keep = 1.0 - amp[number] * lax.rsqrt(jnp.maximum(fr * fr + fi * fi, 0.25))
        cr, ci = both_sides(fr * keep, fi * keep,
                            (stacked[0], stacked[1]), (backward[0], backward[1]), 1.0)
        vr, vi = window(0), window(1)
        probe_out[0] += vr * cr + vi * ci
        probe_out[1] += vr * ci - vi * cr
        below = jnp.zeros((8, side), F32)
        beside = jnp.zeros((tall, 128), F32)

        def add(part, term):
            moved = pltpu.roll(jnp.concatenate([term, below], axis=0), row, 0)
            moved = pltpu.roll(jnp.concatenate([moved, beside], axis=1), lane, 1)
            grad[part, pl.ds(row_base, tall), pl.ds(base, span)] += moved

        add(0, pr * cr + pi * ci)
        add(1, pr * ci - pi * cr)
        return carry

    lax.fori_loop(0, amp.shape[0], step, 0)
    main_out[...] = grad[:, :rows, :cols]
    right_out[...] = grad[:, :rows, cols:]
    bottom_out[...] = grad[:, rows:, :cols]
    corner_out[...] = grad[:, rows:, cols:]


def all_patches(off, tile, right, bottom, corner, probe, amp):
    side = probe.shape[1]
    rows, cols = tile.shape[1], tile.shape[2]
    tables = [jnp.stack(split(jnp.asarray(table))) for table in dft_tables(side)]
    vmem = pl.BlockSpec(memory_space=pltpu.VMEM)
    shape = lambda *dims: jax.ShapeDtypeStruct(dims, F32)
    return pl.pallas_call(
        patches_kernel,
        out_shape=(shape(2, rows, cols), shape(2, rows, side), shape(2, side, cols),
                   shape(2, side, side), shape(2, side, side)),
        in_specs=[pl.BlockSpec(memory_space=pltpu.SMEM)] + [vmem] * 9,
        out_specs=[vmem] * 5,
        scratch_shapes=[pltpu.VMEM((2, rows + side, cols + side), F32),
                        pltpu.VMEM((2, rows + side, cols + side), F32)],
        compiler_params=pltpu.CompilerParams(vmem_limit_bytes=60 * 1024 * 1024),
    )(off, tile, right, bottom, corner, probe, amp, *tables)


def halving_sum(value):
    shape = value.shape
    value = value.reshape(-1, 128)
    steps = [("row", bit) for bit in (1, 2, 4, 8)] + [("col", bit) for bit in (4, 8, 1, 2)]
    for axis, bit in steps:
        upper = (lax.axis_index(axis) & bit) != 0
        half = value.shape[0] // 2
        low, high = value[:half], value[half:]
        pairs = [(i, i ^ bit) for i in range(lax.axis_size(axis))]
        got = lax.ppermute(jnp.where(upper, low, high), axis, pairs)
        value = jnp.where(upper, high, low) + got
    for axis, bit in reversed(steps):
        upper = (lax.axis_index(axis) & bit) != 0
        pairs = [(i, i ^ bit) for i in range(lax.axis_size(axis))]
        got = lax.ppermute(value, axis, pairs)
        value = jnp.concatenate([jnp.where(upper, got, value), jnp.where(upper, value, got)], 0)
    return value.reshape(shape)


def shards(object_field, probe, amplitude, offsets):
    side = probe.shape[1]
    right = passed_along(object_field[:, :, :side], "col", -1)
    bottom = passed_along(object_field[:, :side, :], "row", -1)
    corner = passed_along(right[:, :side, :], "row", -1)
    main, right, bottom, corner, probe_acc = all_patches(
        offsets[0, 0], object_field, right, bottom, corner, probe, amplitude[0, 0])
    corner_back = passed_along(corner, "row", 1)
    bottom_back = passed_along(bottom, "row", 1)
    right = right.at[:, :side, :].add(corner_back)
    right_back = passed_along(right, "col", 1)
    count = amplitude.shape[2] * lax.axis_size("row") * lax.axis_size("col")
    probe_total = halving_sum(probe_acc) / count
    main = main.at[:, :side, :].add(bottom_back)
    object_grad = main.at[:, :, :side].add(right_back)
    return (object_grad, probe_total)


def solution(mesh):
    placed = (
        P(None, "row", "col"),
        P(),
        P("row", "col", None, None, None),
        P("row", "col", None, None),
    )
    return jax.shard_map(
        shards, mesh=mesh, in_specs=placed, out_specs=(P(None, "row", "col"), P()), check_vma=False
    )
```

time: 778 us -> 244 us (0.31)
  waiting for transfers between devices: 403 us -> 144 us
  matrix products: 207 us -> 0 us
  local copies, waits for them, and re-layouts: 72.1 us -> 6.29 us
  Pallas kernels: 0 us -> 36.8 us
  starting transfers between devices: 14.1 us -> 49.2 us
  loops' own time: 29.7 us -> 0 us
  other arithmetic: 32.1 us -> 6.32 us
  between operations: 14.2 us -> 1 us
    psum x1 -> x0, waiting for transfers between devices: 292 us -> none  [shards(): probe_total = lax.psum(probe_acc, ('row', 'col'))]
    dot_general x128 -> x0, matrix products: 207 us -> none  [matmul(): jnp.dot(left, right, precision=lax.Precision.HIGHEST, preferred_element_t...]
    ppermute x0 -> x16, waiting for transfers between devices: none -> 52.4 us  [the longest x8 27 us: halving_sum(): got = lax.ppermute(jnp.where(upper, low, high), axis, pairs)]
    dynamic_update_slice x8 -> x0, local copies, waits for them, and re-layouts: 52.3 us -> none  [step(): grad = lax.dynamic_update_slice(grad, old + obj_term, (zero, top, left))]
    pallas_call x0 -> x1, Pallas kernels: none -> 36.8 us  [all_patches(): pl.pallas_call(patches_kernel, out_shape=(shape(2, rows, cols), shape(2,...]
    another operation x1 -> x0, loops' own time: 29.7 us -> none  [shards(): grad, probe_acc = lax.fori_loop(0, positions, step, start)]
    ppermute x4 -> x6, starting transfers between devices: 14.1 us -> 37.2 us  [passed_along(): lax.ppermute(value, axis, [(source, source + steps) for source in range(f...]
    add x16 -> x8, other arithmetic: 22.7 us -> 0.09 us  [halving_sum(): value = jnp.where(upper, high, low) + got]
  transfers between devices with their start and end apart: 5 -> 22, of which waited for: 4 -> 18; matrix products, arithmetic and copies ran while one was open for 1% -> 3% of each run, Pallas kernels for 0% -> 0%
where the time goes in v1:
time: 244 us; the launch traced here: 243 us
  waiting for transfers between devices  144 us (59%)
  starting transfers between devices  49.2 us (20%)
  Pallas kernels  36.8 us (15%)
  other arithmetic  6.32 us (3%)
  local copies, waits for them, and re-layouts  6.29 us (3%)
    ppermute x6, waiting for transfers between devices, passed_along(): lax.ppermute(value, axis, [(source, source + steps) for source in range(f...  91.2 us
    ppermute x6, starting transfers between devices, passed_along(): lax.ppermute(value, axis, [(source, source + steps) for source in range(f...  37.2 us
    pallas_call x1, Pallas kernels, all_patches(): pl.pallas_call(patches_kernel, out_shape=(shape(2, rows, cols), shape(2,...  36.8 us
    ppermute x8, waiting for transfers between devices, halving_sum(): got = lax.ppermute(jnp.where(upper, low, high), axis, pairs)  27 us
    ppermute x8, waiting for transfers between devices, halving_sum(): got = lax.ppermute(value, axis, pairs)  25.4 us
    ppermute x8, starting transfers between devices, halving_sum(): got = lax.ppermute(value, axis, pairs)  8.12 us
  transfers between devices with their start and end apart: 22, of which 18 were waited for; matrix products, arithmetic and copies ran while one was open for 3% of the time, Pallas kernels for 0%

profile of v1, /device:TPU:31, one launch (start us, length us, event | category | flops | bytes accessed | tf_op | source)
XLA Modules:
  0.0 243.2 jit_solution(6090305210493028470)
XLA Ops:
  2.1 8.1 %collective-permute-start = (f32[2,512,256]{2,1,0:T(8,128)S(1)}, f32[2,512,256]{2,1,0:T(8,128)S(1)}, u32[]{:S(2)}, u32[]{:S(2)}) collective-permute-start(f32[2,512,256]{2,1,0:T(8,128)S(1)} %slice.131), channel_id=1, source_target_pairs={{1,0},{2,1},{3,2},{4,3},{5,4},{6,5},{7,6},{8,7},{9,8},{10,9},{11,1... | collective-permute-start | bytes 3145736 | tf_op jit(solution)/shard_map/ppermute | solution.py:19
  11.3 2.9 %collective-permute-start.1 = (f32[2,256,512]{2,1,0:T(8,128)}, f32[2,256,512]{2,1,0:T(8,128)S(1)}, u32[]{:S(2)}, u32[]{:S(2)}) collective-permute-start(f32[2,256,512]{2,1,0:T(8,128)} %slice.132), channel_id=1, source_target_pairs={{16,0},{32,16},{48,32},{64,48},{80,64},{96,80},{112,96},{128,112},... | collective-permute-start | bytes 3145736 | tf_op jit(solution)/shard_map/ppermute | solution.py:19
  14.1 38.2 %collective-permute-done.right = f32[2,512,256]{2,1,0:T(8,128)S(1)} collective-permute-done((f32[2,512,256]{2,1,0:T(8,128)S(1)}, f32[2,512,256]{2,1,0:T(8,128)S(1)}, u32[]{:S(2)}, u32[]{:S(2)}) %collective-permute-start) | collective-permute-done | bytes 1048608 | tf_op jit(solution)/shard_map/ppermute | solution.py:19
  52.4 5.6 %collective-permute-start.2 = (f32[2,256,256]{2,1,0:T(8,128)S(1)}, f32[2,256,256]{2,1,0:T(8,128)S(1)}, u32[]{:S(2)}, u32[]{:S(2)}) collective-permute-start(f32[2,256,256]{2,1,0:T(8,128)S(1)} %slice.153), channel_id=1, source_target_pairs={{16,0},{32,16},{48,32},{64,48},{80,64},{96,80},{112,96},{128,112},... | collective-permute-start | bytes 1572872 | tf_op jit(solution)/shard_map/ppermute | solution.py:19
  58.7 7.9 %collective-permute-done.1.bottom = f32[2,256,512]{2,1,0:T(8,128)S(1)} collective-permute-done((f32[2,256,512]{2,1,0:T(8,128)}, f32[2,256,512]{2,1,0:T(8,128)S(1)}, u32[]{:S(2)}, u32[]{:S(2)}) %collective-permute-start.1) | collective-permute-done | bytes 1048608 | tf_op jit(solution)/shard_map/ppermute | solution.py:19
  66.6 5.6 %collective-permute-done.2.corner = f32[2,256,256]{2,1,0:T(8,128)S(1)} collective-permute-done((f32[2,256,256]{2,1,0:T(8,128)S(1)}, f32[2,256,256]{2,1,0:T(8,128)S(1)}, u32[]{:S(2)}, u32[]{:S(2)}) %collective-permute-start.2) | collective-permute-done | bytes 524320 | tf_op jit(solution)/shard_map/ppermute | solution.py:19
  73.0 36.8 %shard_map.86 = (f32[2,512,512]{2,1,0:T(8,128)}, f32[2,512,256]{2,1,0:T(8,128)}, f32[2,256,512]{2,1,0:T(8,128)}, f32[2,256,256]{2,1,0:T(8,128)}, f32[2,256,256]{2,1,0:T(8,128)}) custom-call(s32[8,2]{1,0:T(8,128)} %copy.9.off, f32[2,512,512]{2,1,0:T(8,128)} %tile.1, f32[2,512,256]{2,1,0:T(8,128)} %copy-done.1, f32[2,256,512]{2,1,0:T(8,128)} %copy-done.4, ...), custom_call_target="tpu_custom_call" | custom-call | tf_op jit(solution)/shard_map/pallas_call | solution.py:118
  111.0 1.5 collective-permute-done.6
  112.6 4.9 %collective-permute-done.7 = f32[256,128]{1,0:T(8,128)S(1)} collective-permute-done((f32[256,128]{1,0:T(8,128)S(1)}, f32[256,128]{1,0:T(8,128)S(1)}, u32[]{:S(2)}, u32[]{:S(2)}) %collective-permute-start.7) | collective-permute-done | bytes 131104 | tf_op jit(solution)/shard_map/ppermute | solution.py:139
  117.7 4.6 %collective-permute-done.8 = f32[128,128]{1,0:T(8,128)S(1)} collective-permute-done((f32[128,128]{1,0:T(8,128)S(1)}, f32[128,128]{1,0:T(8,128)S(1)}, u32[]{:S(2)}, u32[]{:S(2)}) %collective-permute-start.8) | collective-permute-done | bytes 65568 | tf_op jit(solution)/shard_map/ppermute | solution.py:139
  122.4 2.7 %collective-permute-done.9 = f32[64,128]{1,0:T(8,128)S(1)} collective-permute-done((f32[64,128]{1,0:T(8,128)S(1)}, f32[64,128]{1,0:T(8,128)S(1)}, u32[]{:S(2)}, u32[]{:S(2)}) %collective-permute-start.9) | collective-permute-done | bytes 32800 | tf_op jit(solution)/shard_map/ppermute | solution.py:139
  125.4 2.6 %collective-permute-done.10 = f32[32,128]{1,0:T(8,128)S(1)} collective-permute-done((f32[32,128]{1,0:T(8,128)S(1)}, f32[32,128]{1,0:T(8,128)S(1)}, u32[]{:S(2)}, u32[]{:S(2)}) %collective-permute-start.10) | collective-permute-done | bytes 16416 | tf_op jit(solution)/shard_map/ppermute | solution.py:139
  128.8 3.4 %collective-permute-done.11 = f32[16,128]{1,0:T(8,128)S(1)} collective-permute-done((f32[16,128]{1,0:T(8,128)S(1)}, f32[16,128]{1,0:T(8,128)S(1)}, u32[]{:S(2)}, u32[]{:S(2)}) %collective-permute-start.11) | collective-permute-done | bytes 8224 | tf_op jit(solution)/shard_map/ppermute | solution.py:139
  132.3 3.3 %collective-permute-done.12 = f32[8,128]{1,0:T(8,128)S(1)} collective-permute-done((f32[8,128]{1,0:T(8,128)S(1)}, f32[8,128]{1,0:T(8,128)S(1)}, u32[]{:S(2)}, u32[]{:S(2)}) %collective-permute-start.12) | collective-permute-done | bytes 4128 | tf_op jit(solution)/shard_map/ppermute | solution.py:139
  135.7 2.5 %collective-permute-start.13 = (f32[4,128]{1,0:T(4,128)S(1)}, f32[4,128]{1,0:T(4,128)S(1)}, u32[]{:S(2)}, u32[]{:S(2)}) collective-permute-start(f32[4,128]{1,0:T(4,128)S(1)} %slice_select_fusion.8), channel_id=1, source_target_pairs={{0,2},{1,3},{2,0},{3,1},{4,6},{5,7},{6,4},{7,5},{8,10},{9,11},{10,... | collective-permute-start | bytes 6152 | tf_op jit(solution)/shard_map/ppermute | solution.py:139
  138.1 3.9 %collective-permute-done.13 = f32[4,128]{1,0:T(4,128)S(1)} collective-permute-done((f32[4,128]{1,0:T(4,128)S(1)}, f32[4,128]{1,0:T(4,128)S(1)}, u32[]{:S(2)}, u32[]{:S(2)}) %collective-permute-start.13) | collective-permute-done | bytes 2080 | tf_op jit(solution)/shard_map/ppermute | solution.py:139
  142.1 2.4 collective-permute-start.14
  144.5 3.9 %collective-permute-done.14 = f32[4,128]{1,0:T(4,128)S(1)} collective-permute-done((f32[4,128]{1,0:T(4,128)S(1)}, f32[4,128]{1,0:T(4,128)S(1)}, u32[]{:S(2)}, u32[]{:S(2)}) %collective-permute-start.14) | collective-permute-done | bytes 2080 | tf_op jit(solution)/shard_map/ppermute | solution.py:144
  148.8 3.1 %collective-permute-done.15 = f32[8,128]{1,0:T(8,128)S(1)} collective-permute-done((f32[8,128]{1,0:T(8,128)S(1)}, f32[8,128]{1,0:T(8,128)S(1)}, u32[]{:S(2)}, u32[]{:S(2)}) %collective-permute-start.15) | collective-permute-done | bytes 4128 | tf_op jit(solution)/shard_map/ppermute | solution.py:144
  152.6 3.7 %collective-permute-done.16 = f32[16,128]{1,0:T(8,128)S(1)} collective-permute-done((f32[16,128]{1,0:T(8,128)S(1)}, f32[16,128]{1,0:T(8,128)S(1)}, u32[]{:S(2)}, u32[]{:S(2)}) %collective-permute-start.16) | collective-permute-done | bytes 8224 | tf_op jit(solution)/shard_map/ppermute | solution.py:144
  156.5 2.4 collective-permute-done.17
  159.1 14.4 %collective-permute-start.4 = (f32[2,256,256]{2,1,0:T(8,128)S(1)}, f32[2,256,256]{2,1,0:T(8,128)S(1)}, u32[]{:S(2)}, u32[]{:S(2)}) collective-permute-start(f32[2,256,256]{2,1,0:T(8,128)S(1)} %copy-done.7), channel_id=1, source_target_pairs={{0,16},{16,32},{32,48},{48,64},{64,80},{80,96},{96,112},{112,128},... | collective-permute-start | bytes 1572872 | tf_op jit(solution)/shard_map/ppermute | solution.py:19
  173.5 1.5 collective-permute-start.19
  175.0 4.2 %collective-permute-start.3 = (f32[2,256,512]{2,1,0:T(8,128)}, f32[2,256,512]{2,1,0:T(8,128)}, u32[]{:S(2)}, u32[]{:S(2)}) collective-permute-start(f32[2,256,512]{2,1,0:T(8,128)} %get-tuple-element.44), channel_id=1, source_target_pairs={{0,16},{16,32},{32,48},{48,64},{64,80},{80,96},{96,112},{112,128},... | collective-permute-start | bytes 3145736 | tf_op jit(solution)/shard_map/ppermute | solution.py:19
  179.3 2.7 %collective-permute-start.20 = (f32[256,128]{1,0:T(8,128)S(1)}, f32[256,128]{1,0:T(8,128)S(1)}, u32[]{:S(2)}, u32[]{:S(2)}) collective-permute-start(f32[256,128]{1,0:T(8,128)S(1)} %pad_maximum_fusion.1), channel_id=1, source_target_pairs={{0,32},{16,48},{32,0},{48,16},{64,96},{80,112},{96,64},{112,80},{1... | collective-permute-start | bytes 393224 | tf_op jit(solution)/shard_map/ppermute | solution.py:144
  182.0 1.9 add_dynamic-update-slice_fusion.1
  183.9 2.0 collective-permute-start.5
  185.9 10.8 %collective-permute-done.20 = f32[256,128]{1,0:T(8,128)S(1)} collective-permute-done((f32[256,128]{1,0:T(8,128)S(1)}, f32[256,128]{1,0:T(8,128)S(1)}, u32[]{:S(2)}, u32[]{:S(2)}) %collective-permute-start.20) | collective-permute-done | bytes 131104 | tf_op jit(solution)/shard_map/ppermute | solution.py:144
  196.9 1.5 collective-permute-done.21
  199.5 1.5 add_dynamic-update-slice_fusion
  201.0 39.5 %collective-permute-done.5 = f32[2,512,256]{2,1,0:T(8,128)} collective-permute-done((f32[2,512,256]{2,1,0:T(8,128)}, f32[2,512,256]{2,1,0:T(8,128)}, u32[]{:S(2)}, u32[]{:S(2)}) %collective-permute-start.5) | collective-permute-done | bytes 1048608 | tf_op jit(solution)/shard_map/ppermute | solution.py:19
  240.4 1.5 fusion
  (71 shorter events, 10.7 us)
Async XLA Ops:
  0.6 9.6 %copy-start = (f32[2,512,512]{2,1,0:T(8,128)S(1)}, f32[2,512,512]{2,1,0:T(8,128)}, u32[]{:S(2)}) copy-start(f32[2,512,512]{2,1,0:T(8,128)} %tile.1) | copy-start | bytes 6291460
  2.1 55.9 %copy-start.6 = (s32[1,1,8,2]{2,3,1,0:T(2,128)S(1)}, s32[1,1,8,2]{2,3,1,0:T(2,128)}, u32[]{:S(2)}) copy-start(s32[1,1,8,2]{2,3,1,0:T(2,128)} %param.16) | copy-start | bytes 196
  2.1 50.3 %collective-permute-start = (f32[2,512,256]{2,1,0:T(8,128)S(1)}, f32[2,512,256]{2,1,0:T(8,128)S(1)}, u32[]{:S(2)}, u32[]{:S(2)}) collective-permute-start(f32[2,512,256]{2,1,0:T(8,128)S(1)} %slice.131), channel_id=1, source_target_pairs={{1,0},{2,1},{3,2},{4,3},{5,4},{6,5},{7,6},{8,7},{9,8},{10,9},{11,1... | collective-permute-start | bytes 3145736 | tf_op jit(solution)/shard_map/ppermute | solution.py:19
  11.3 55.3 %collective-permute-start.1 = (f32[2,256,512]{2,1,0:T(8,128)}, f32[2,256,512]{2,1,0:T(8,128)S(1)}, u32[]{:S(2)}, u32[]{:S(2)}) collective-permute-start(f32[2,256,512]{2,1,0:T(8,128)} %slice.132), channel_id=1, source_target_pairs={{16,0},{32,16},{48,32},{64,48},{80,64},{96,80},{112,96},{128,112},... | collective-permute-start | bytes 3145736 | tf_op jit(solution)/shard_map/ppermute | solution.py:19
  52.4 19.8 %copy-start.1 = (f32[2,512,256]{2,1,0:T(8,128)}, f32[2,512,256]{2,1,0:T(8,128)S(1)}, u32[]{:S(2)}) copy-start(f32[2,512,256]{2,1,0:T(8,128)S(1)} %collective-permute-done.right) | copy-start | bytes 3145732
  52.4 19.8 %collective-permute-start.2 = (f32[2,256,256]{2,1,0:T(8,128)S(1)}, f32[2,256,256]{2,1,0:T(8,128)S(1)}, u32[]{:S(2)}, u32[]{:S(2)}) collective-permute-start(f32[2,256,256]{2,1,0:T(8,128)S(1)} %slice.153), channel_id=1, source_target_pairs={{16,0},{32,16},{48,32},{64,48},{80,64},{96,80},{112,96},{128,112},... | collective-permute-start | bytes 1572872 | tf_op jit(solution)/shard_map/ppermute | solution.py:19
  66.6 5.6 %copy-start.4 = (f32[2,256,512]{2,1,0:T(8,128)}, f32[2,256,512]{2,1,0:T(8,128)S(1)}, u32[]{:S(2)}) copy-start(f32[2,256,512]{2,1,0:T(8,128)S(1)} %collective-permute-done.1.bottom) | copy-start | bytes 3145732
  72.2 0.8 copy-start.5
  110.8 48.3 %copy-start.7 = (f32[2,256,256]{2,1,0:T(8,128)S(1)}, f32[2,256,256]{2,1,0:T(8,128)}, u32[]{:S(2)}) copy-start(f32[2,256,256]{2,1,0:T(8,128)} %get-tuple-element.46) | copy-start | bytes 1572868
  110.9 1.6 collective-permute-start.6
  112.5 5.0 %collective-permute-start.7 = (f32[256,128]{1,0:T(8,128)S(1)}, f32[256,128]{1,0:T(8,128)S(1)}, u32[]{:S(2)}, u32[]{:S(2)}) collective-permute-start(f32[256,128]{1,0:T(8,128)S(1)} %slice_select_fusion.2), channel_id=1, source_target_pairs={{0,32},{16,48},{32,0},{48,16},{64,96},{80,112},{96,64},{112,80},{1... | collective-permute-start | bytes 393224 | tf_op jit(solution)/shard_map/ppermute | solution.py:139
  117.6 4.7 %collective-permute-start.8 = (f32[128,128]{1,0:T(8,128)S(1)}, f32[128,128]{1,0:T(8,128)S(1)}, u32[]{:S(2)}, u32[]{:S(2)}) collective-permute-start(f32[128,128]{1,0:T(8,128)S(1)} %slice_select_fusion.3), channel_id=1, source_target_pairs={{0,64},{16,80},{32,96},{48,112},{64,0},{80,16},{96,32},{112,48},{1... | collective-permute-start | bytes 196616 | tf_op jit(solution)/shard_map/ppermute | solution.py:139
  122.3 2.9 %collective-permute-start.9 = (f32[64,128]{1,0:T(8,128)S(1)}, f32[64,128]{1,0:T(8,128)S(1)}, u32[]{:S(2)}, u32[]{:S(2)}) collective-permute-start(f32[64,128]{1,0:T(8,128)S(1)} %slice_select_fusion.4), channel_id=1, source_target_pairs={{0,128},{16,144},{32,160},{48,176},{64,192},{80,208},{96,224},{112... | collective-permute-start | bytes 98312 | tf_op jit(solution)/shard_map/ppermute | solution.py:139
  125.2 2.9 %collective-permute-start.10 = (f32[32,128]{1,0:T(8,128)S(1)}, f32[32,128]{1,0:T(8,128)S(1)}, u32[]{:S(2)}, u32[]{:S(2)}) collective-permute-start(f32[32,128]{1,0:T(8,128)S(1)} %slice_select_fusion.5), channel_id=1, source_target_pairs={{0,4},{1,5},{2,6},{3,7},{4,0},{5,1},{6,2},{7,3},{8,12},{9,13},{10,... | collective-permute-start | bytes 49160 | tf_op jit(solution)/shard_map/ppermute | solution.py:139
  128.1 4.1 %collective-permute-start.11 = (f32[16,128]{1,0:T(8,128)S(1)}, f32[16,128]{1,0:T(8,128)S(1)}, u32[]{:S(2)}, u32[]{:S(2)}) collective-permute-start(f32[16,128]{1,0:T(8,128)S(1)} %slice_select_fusion.6), channel_id=1, source_target_pairs={{0,8},{1,9},{2,10},{3,11},{4,12},{5,13},{6,14},{7,15},{8,0},{9,1},... | collective-permute-start | bytes 24584 | tf_op jit(solution)/shard_map/ppermute | solution.py:139
  132.2 3.4 %collective-permute-start.12 = (f32[8,128]{1,0:T(8,128)S(1)}, f32[8,128]{1,0:T(8,128)S(1)}, u32[]{:S(2)}, u32[]{:S(2)}) collective-permute-start(f32[8,128]{1,0:T(8,128)S(1)} %slice_select_fusion.7), channel_id=1, source_target_pairs={{0,1},{1,0},{2,3},{3,2},{4,5},{5,4},{6,7},{7,6},{8,9},{9,8},{10,11... | collective-permute-start | bytes 12296 | tf_op jit(solution)/shard_map/ppermute | solution.py:139
  135.7 6.4 %collective-permute-start.13 = (f32[4,128]{1,0:T(4,128)S(1)}, f32[4,128]{1,0:T(4,128)S(1)}, u32[]{:S(2)}, u32[]{:S(2)}) collective-permute-start(f32[4,128]{1,0:T(4,128)S(1)} %slice_select_fusion.8), channel_id=1, source_target_pairs={{0,2},{1,3},{2,0},{3,1},{4,6},{5,7},{6,4},{7,5},{8,10},{9,11},{10,... | collective-permute-start | bytes 6152 | tf_op jit(solution)/shard_map/ppermute | solution.py:139
  142.1 6.3 %collective-permute-start.14 = (f32[4,128]{1,0:T(4,128)S(1)}, f32[4,128]{1,0:T(4,128)S(1)}, u32[]{:S(2)}, u32[]{:S(2)}) collective-permute-start(f32[4,128]{1,0:T(4,128)S(1)} %select_add_fusion.6), channel_id=1, source_target_pairs={{0,2},{1,3},{2,0},{3,1},{4,6},{5,7},{6,4},{7,5},{8,10},{9,11},{10,... | collective-permute-start | bytes 6152 | tf_op jit(solution)/shard_map/ppermute | solution.py:144
  148.4 3.4 %collective-permute-start.15 = (f32[8,128]{1,0:T(8,128)S(1)}, f32[8,128]{1,0:T(8,128)S(1)}, u32[]{:S(2)}, u32[]{:S(2)}) collective-permute-start(f32[8,128]{1,0:T(8,128)S(1)} %pad_maximum_fusion.6), channel_id=1, source_target_pairs={{0,1},{1,0},{2,3},{3,2},{4,5},{5,4},{6,7},{7,6},{8,9},{9,8},{10,11... | collective-permute-start | bytes 12296 | tf_op jit(solution)/shard_map/ppermute | solution.py:144
  151.9 4.4 %collective-permute-start.16 = (f32[16,128]{1,0:T(8,128)S(1)}, f32[16,128]{1,0:T(8,128)S(1)}, u32[]{:S(2)}, u32[]{:S(2)}) collective-permute-start(f32[16,128]{1,0:T(8,128)S(1)} %pad_maximum_fusion.5), channel_id=1, source_target_pairs={{0,8},{1,9},{2,10},{3,11},{4,12},{5,13},{6,14},{7,15},{8,0},{9,1},... | collective-permute-start | bytes 24584 | tf_op jit(solution)/shard_map/ppermute | solution.py:144
  156.3 2.7 %collective-permute-start.17 = (f32[32,128]{1,0:T(8,128)S(1)}, f32[32,128]{1,0:T(8,128)S(1)}, u32[]{:S(2)}, u32[]{:S(2)}) collective-permute-start(f32[32,128]{1,0:T(8,128)S(1)} %pad_maximum_fusion.4), channel_id=1, source_target_pairs={{0,4},{1,5},{2,6},{3,7},{4,0},{5,1},{6,2},{7,3},{8,12},{9,13},{10,... | collective-permute-start | bytes 49160 | tf_op jit(solution)/shard_map/ppermute | solution.py:144
  159.0 14.5 %collective-permute-start.18 = (f32[64,128]{1,0:T(8,128)S(1)}, f32[64,128]{1,0:T(8,128)S(1)}, u32[]{:S(2)}, u32[]{:S(2)}) collective-permute-start(f32[64,128]{1,0:T(8,128)S(1)} %pad_maximum_fusion.3), channel_id=1, source_target_pairs={{0,128},{16,144},{32,160},{48,176},{64,192},{80,208},{96,224},{112... | collective-permute-start | bytes 98312 | tf_op jit(solution)/shard_map/ppermute | solution.py:144
  159.1 22.9 %collective-permute-start.4 = (f32[2,256,256]{2,1,0:T(8,128)S(1)}, f32[2,256,256]{2,1,0:T(8,128)S(1)}, u32[]{:S(2)}, u32[]{:S(2)}) collective-permute-start(f32[2,256,256]{2,1,0:T(8,128)S(1)} %copy-done.7), channel_id=1, source_target_pairs={{0,16},{16,32},{32,48},{48,64},{64,80},{80,96},{96,112},{112,128},... | collective-permute-start | bytes 1572872 | tf_op jit(solution)/shard_map/ppermute | solution.py:19
  173.5 5.7 %collective-permute-start.19 = (f32[128,128]{1,0:T(8,128)S(1)}, f32[128,128]{1,0:T(8,128)S(1)}, u32[]{:S(2)}, u32[]{:S(2)}) collective-permute-start(f32[128,128]{1,0:T(8,128)S(1)} %pad_maximum_fusion.2), channel_id=1, source_target_pairs={{0,64},{16,80},{32,96},{48,112},{64,0},{80,16},{96,32},{112,48},{1... | collective-permute-start | bytes 196616 | tf_op jit(solution)/shard_map/ppermute | solution.py:144
  175.0 24.5 %collective-permute-start.3 = (f32[2,256,512]{2,1,0:T(8,128)}, f32[2,256,512]{2,1,0:T(8,128)}, u32[]{:S(2)}, u32[]{:S(2)}) collective-permute-start(f32[2,256,512]{2,1,0:T(8,128)} %get-tuple-element.44), channel_id=1, source_target_pairs={{0,16},{16,32},{32,48},{48,64},{64,80},{80,96},{96,112},{112,128},... | collective-permute-start | bytes 3145736 | tf_op jit(solution)/shard_map/ppermute | solution.py:19
  179.3 17.5 %collective-permute-start.20 = (f32[256,128]{1,0:T(8,128)S(1)}, f32[256,128]{1,0:T(8,128)S(1)}, u32[]{:S(2)}, u32[]{:S(2)}) collective-permute-start(f32[256,128]{1,0:T(8,128)S(1)} %pad_maximum_fusion.1), channel_id=1, source_target_pairs={{0,32},{16,48},{32,0},{48,16},{64,96},{80,112},{96,64},{112,80},{1... | collective-permute-start | bytes 393224 | tf_op jit(solution)/shard_map/ppermute | solution.py:144
  183.9 15.6 %copy-start.2 = (f32[2,512,512]{2,1,0:T(8,128)S(1)}, f32[2,512,512]{2,1,0:T(8,128)}, u32[]{:S(2)}) copy-start(f32[2,512,512]{2,1,0:T(8,128)} %get-tuple-element.43) | copy-start | bytes 6291460
  183.9 56.5 %collective-permute-start.5 = (f32[2,512,256]{2,1,0:T(8,128)}, f32[2,512,256]{2,1,0:T(8,128)}, u32[]{:S(2)}, u32[]{:S(2)}) collective-permute-start(f32[2,512,256]{2,1,0:T(8,128)} %add_dynamic-update-slice_fusion.1), channel_id=1, source_target_pairs={{0,1},{1,2},{2,3},{3,4},{4,5},{5,6},{6,7},{7,8},{8,9},{9,10},{10,1... | collective-permute-start | bytes 3145736 | tf_op jit(solution)/shard_map/ppermute | solution.py:19
  196.8 1.6 collective-permute-start.21
  241.9 1.3 copy-start.3

commit v2 on v1

--- a/solution.py
+++ b/solution.py
@@ -1,4 +1,3 @@
-import functools
 import math
 
 import jax
@@ -8,6 +7,7 @@
 from jax.experimental import pallas as pl
 from jax.experimental.pallas import tpu as pltpu
 from jax.sharding import PartitionSpec as P
+
 
 F32 = jnp.float32
 BF16 = jnp.bfloat16
@@ -55,7 +55,7 @@
 
 
 def patches_kernel(off, tile, right, bottom, corner, probe, amp, stacked, forward, backward,
-                   main_out, right_out, bottom_out, corner_out, probe_out, ext, grad):
+                   main_out, upper_out, lower_out, bottom_out, corner_out, probe_out, ext, grad):
     side = probe.shape[1]
     rows, cols = tile.shape[1], tile.shape[2]
     ext[:, :rows, :cols] = tile[...]
@@ -104,7 +104,8 @@
 
     lax.fori_loop(0, amp.shape[0], step, 0)
     main_out[...] = grad[:, :rows, :cols]
-    right_out[...] = grad[:, :rows, cols:]
+    upper_out[...] = grad[:, :side, cols:]
+    lower_out[...] = grad[:, side:rows, cols:]
     bottom_out[...] = grad[:, rows:, :cols]
     corner_out[...] = grad[:, rows:, cols:]
 
@@ -117,48 +118,56 @@
     shape = lambda *dims: jax.ShapeDtypeStruct(dims, F32)
     return pl.pallas_call(
         patches_kernel,
-        out_shape=(shape(2, rows, cols), shape(2, rows, side), shape(2, side, cols),
+        out_shape=(shape(2, rows, cols), shape(2, side, side), shape(2, rows - side, side), shape(2, side, cols),
                    shape(2, side, side), shape(2, side, side)),
         in_specs=[pl.BlockSpec(memory_space=pltpu.SMEM)] + [vmem] * 9,
-        out_specs=[vmem] * 5,
+        out_specs=[vmem] * 6,
         scratch_shapes=[pltpu.VMEM((2, rows + side, cols + side), F32),
                         pltpu.VMEM((2, rows + side, cols + side), F32)],
-        compiler_params=pltpu.CompilerParams(vmem_limit_bytes=60 * 1024 * 1024),
+        compiler_params=pltpu.CompilerParams(vmem_limit_bytes=26 * 1024 * 1024),
     )(off, tile, right, bottom, corner, probe, amp, *tables)
 
 
-def halving_sum(value):
+HALVED = (("row", 1), ("row", 2), ("row", 4), ("col", 4))
+WHOLE = (("col", 8), ("row", 8), ("col", 1), ("col", 2))
+
+
+def swapped(value, axis, bit):
+    return lax.ppermute(value, axis, [(i, i ^ bit) for i in range(lax.axis_size(axis))])
+
+
+def summed_everywhere(value):
     shape = value.shape
     value = value.reshape(-1, 128)
-    steps = [("row", bit) for bit in (1, 2, 4, 8)] + [("col", bit) for bit in (4, 8, 1, 2)]
-    for axis, bit in steps:
+    for axis, bit in HALVED:
         upper = (lax.axis_index(axis) & bit) != 0
         half = value.shape[0] // 2
         low, high = value[:half], value[half:]
-        pairs = [(i, i ^ bit) for i in range(lax.axis_size(axis))]
-        got = lax.ppermute(jnp.where(upper, low, high), axis, pairs)
+        got = swapped(jnp.where(upper, low, high), axis, bit)
         value = jnp.where(upper, high, low) + got
-    for axis, bit in reversed(steps):
+    for axis, bit in WHOLE:
+        value = value + swapped(value, axis, bit)
+    for axis, bit in reversed(HALVED):
         upper = (lax.axis_index(axis) & bit) != 0
-        pairs = [(i, i ^ bit) for i in range(lax.axis_size(axis))]
-        got = lax.ppermute(value, axis, pairs)
+        got = swapped(value, axis, bit)
         value = jnp.concatenate([jnp.where(upper, got, value), jnp.where(upper, value, got)], 0)
     return value.reshape(shape)
 
 
-def shards(object_field, probe, amplitude, offsets):
+def shards_body(object_field, probe, amplitude, offsets):
     side = probe.shape[1]
     right = passed_along(object_field[:, :, :side], "col", -1)
     bottom = passed_along(object_field[:, :side, :], "row", -1)
     corner = passed_along(right[:, :side, :], "row", -1)
-    main, right, bottom, corner, probe_acc = all_patches(
+    main, upper, lower, bottom, corner, probe_acc = all_patches(
         offsets[0, 0], object_field, right, bottom, corner, probe, amplitude[0, 0])
     corner_back = passed_along(corner, "row", 1)
+    lower_back = passed_along(lower, "col", 1)
     bottom_back = passed_along(bottom, "row", 1)
-    right = right.at[:, :side, :].add(corner_back)
-    right_back = passed_along(right, "col", 1)
+    upper_back = passed_along(upper + corner_back, "col", 1)
     count = amplitude.shape[2] * lax.axis_size("row") * lax.axis_size("col")
-    probe_total = halving_sum(probe_acc) / count
+    probe_total = summed_everywhere(probe_acc) / count
+    right_back = jnp.concatenate([upper_back, lower_back], axis=1)
     main = main.at[:, :side, :].add(bottom_back)
     object_grad = main.at[:, :, :side].add(right_back)
     return (object_grad, probe_total)
@@ -172,5 +181,5 @@
         P("row", "col", None, None),
     )
     return jax.shard_map(
-        shards, mesh=mesh, in_specs=placed, out_specs=(P(None, "row", "col"), P()), check_vma=False
+        shards_body, mesh=mesh, in_specs=placed, out_specs=(P(None, "row", "col"), P()), check_vma=False
     )

time: 244 us -> 229 us (0.939)
  waiting for transfers between devices: 144 us -> 117 us
  local copies, waits for them, and re-layouts: 6.29 us -> 14.5 us
  starting transfers between devices: 49.2 us -> 57.2 us
  Pallas kernels: 36.8 us -> 34.1 us
    ppermute x16 -> x12, waiting for transfers between devices: 52.4 us -> 28.5 us  [swapped(): lax.ppermute(value, axis, [(i, i ^ bit) for i in range(lax.axis_size(axis...]
    unnamed x16 -> x30, local copies, waits for them, and re-layouts: 2.13 us -> 9.47 us
    ppermute x16 -> x12, starting transfers between devices: 12 us -> 16.9 us  [swapped(): lax.ppermute(value, axis, [(i, i ^ bit) for i in range(lax.axis_size(axis...]
    ppermute x6 -> x7, starting transfers between devices: 37.2 us -> 40.4 us  [passed_along(): lax.ppermute(value, axis, [(source, source + steps) for source in range(f...]
    ppermute x6 -> x7, waiting for transfers between devices: 91.2 us -> 88.1 us  [passed_along(): lax.ppermute(value, axis, [(source, source + steps) for source in range(f...]
    pallas_call x1, Pallas kernels: 36.8 us -> 34.1 us  [all_patches(): pl.pallas_call(patches_kernel, out_shape=(shape(2, rows, cols), shape(2,...]
    scatter-add x3 -> x2, other arithmetic: 4.9 us -> 4.74 us  [the longest x1 2.41 us: shards_body(): main = main.at[:, :side, :].add(bottom_back)]
  transfers between devices with their start and end apart: 22 -> 19, of which waited for: 18 -> 14; matrix products, arithmetic and copies ran while one was open for 3% -> 3% of each run, Pallas kernels for 0% -> 0%
where the time goes in v2:
time: 229 us
  waiting for transfers between devices  117 us (51%)
  starting transfers between devices  57.2 us (25%)
  Pallas kernels  34.1 us (15%)
  local copies, waits for them, and re-layouts  14.5 us (6%)
  other arithmetic  5.14 us (2%)
    ppermute x7, waiting for transfers between devices, passed_along(): lax.ppermute(value, axis, [(source, source + steps) for source in range(f...  88.1 us
    ppermute x7, starting transfers between devices, passed_along(): lax.ppermute(value, axis, [(source, source + steps) for source in range(f...  40.4 us
    pallas_call x1, Pallas kernels, all_patches(): pl.pallas_call(patches_kernel, out_shape=(shape(2, rows, cols), shape(2,...  34.1 us
    ppermute x12, waiting for transfers between devices, swapped(): lax.ppermute(value, axis, [(i, i ^ bit) for i in range(lax.axis_size(axis...  28.5 us
    ppermute x12, starting transfers between devices, swapped(): lax.ppermute(value, axis, [(i, i ^ bit) for i in range(lax.axis_size(axis...  16.9 us
    unnamed x30, local copies, waits for them, and re-layouts  9.47 us
  transfers between devices with their start and end apart: 19, of which 14 were waited for; matrix products, arithmetic and copies ran while one was open for 3% of the time, Pallas kernels for 0%

profile of v2, /device:TPU:31, one launch (start us, length us, event | category | flops | bytes accessed | tf_op | source)
XLA Modules:
  0.0 228.6 jit_solution(8482065409568606638)
XLA Ops:
  0.6 1.4 slice.83
  2.1 8.1 %collective-permute-start = (f32[2,512,256]{2,1,0:T(8,128)S(1)}, f32[2,512,256]{2,1,0:T(8,128)S(1)}, u32[]{:S(2)}, u32[]{:S(2)}) collective-permute-start(f32[2,512,256]{2,1,0:T(8,128)S(1)} %slice.83), channel_id=1, source_target_pairs={{1,0},{2,1},{3,2},{4,3},{5,4},{6,5},{7,6},{8,7},{9,8},{10,9},{11,1... | collective-permute-start | bytes 3145736 | tf_op jit(solution)/shard_map/ppermute | solution.py:19
  11.3 2.9 %collective-permute-start.1 = (f32[2,256,512]{2,1,0:T(8,128)}, f32[2,256,512]{2,1,0:T(8,128)}, u32[]{:S(2)}, u32[]{:S(2)}) collective-permute-start(f32[2,256,512]{2,1,0:T(8,128)} %slice.84), channel_id=1, source_target_pairs={{16,0},{32,16},{48,32},{64,48},{80,64},{96,80},{112,96},{128,112},... | collective-permute-start | bytes 3145736 | tf_op jit(solution)/shard_map/ppermute | solution.py:19
  14.1 38.2 %collective-permute-done.right = f32[2,512,256]{2,1,0:T(8,128)S(1)} collective-permute-done((f32[2,512,256]{2,1,0:T(8,128)S(1)}, f32[2,512,256]{2,1,0:T(8,128)S(1)}, u32[]{:S(2)}, u32[]{:S(2)}) %collective-permute-start) | collective-permute-done | bytes 1048608 | tf_op jit(solution)/shard_map/ppermute | solution.py:19
  53.2 5.6 %collective-permute-start.2 = (f32[2,256,256]{2,1,0:T(8,128)}, f32[2,256,256]{2,1,0:T(8,128)}, u32[]{:S(2)}, u32[]{:S(2)}) collective-permute-start(f32[2,256,256]{2,1,0:T(8,128)} %slice.96), channel_id=1, source_target_pairs={{16,0},{32,16},{48,32},{64,48},{80,64},{96,80},{112,96},{128,112},... | collective-permute-start | bytes 1572872 | tf_op jit(solution)/shard_map/ppermute | solution.py:19
  58.9 7.8 %collective-permute-done.1.bottom = f32[2,256,512]{2,1,0:T(8,128)} collective-permute-done((f32[2,256,512]{2,1,0:T(8,128)}, f32[2,256,512]{2,1,0:T(8,128)}, u32[]{:S(2)}, u32[]{:S(2)}) %collective-permute-start.1) | collective-permute-done | bytes 1048608 | tf_op jit(solution)/shard_map/ppermute | solution.py:19
  66.7 5.6 %collective-permute-done.2.corner = f32[2,256,256]{2,1,0:T(8,128)} collective-permute-done((f32[2,256,256]{2,1,0:T(8,128)}, f32[2,256,256]{2,1,0:T(8,128)}, u32[]{:S(2)}, u32[]{:S(2)}) %collective-permute-start.2) | collective-permute-done | bytes 524320 | tf_op jit(solution)/shard_map/ppermute | solution.py:19
  72.3 1.6 copy-done.1
  73.9 1.2 copy-done.2
  75.1 1.2 copy-done.3
  77.4 1.0 copy-done.7
  78.4 34.1 %shard_map.86 = (f32[2,512,512]{2,1,0:T(8,128)}, f32[2,256,256]{2,1,0:T(8,128)S(1)}, f32[2,256,256]{2,1,0:T(8,128)S(1)}, f32[2,256,512]{2,1,0:T(8,128)S(1)}, f32...) custom-call(s32[8,2]{1,0:T(8,128)S(1)} %copy.9.off, f32[2,512,512]{2,1,0:T(8,128)S(1)} %copy-done, ...), custom_call_target="tpu_custom_call" | custom-call | tf_op jit(solution)/shard_map/pallas_call | solution.py:119
  116.7 1.7 collective-permute-done.7
  118.5 4.9 %collective-permute-done.8 = f32[256,128]{1,0:T(8,128)S(1)} collective-permute-done((f32[256,128]{1,0:T(8,128)S(1)}, f32[256,128]{1,0:T(8,128)S(1)}, u32[]{:S(2)}, u32[]{:S(2)}) %collective-permute-start.8) | collective-permute-done | bytes 131104 | tf_op jit(solution)/shard_map/ppermute | solution.py:136
  123.6 4.6 %collective-permute-done.9 = f32[128,128]{1,0:T(8,128)S(1)} collective-permute-done((f32[128,128]{1,0:T(8,128)S(1)}, f32[128,128]{1,0:T(8,128)S(1)}, u32[]{:S(2)}, u32[]{:S(2)}) %collective-permute-start.9) | collective-permute-done | bytes 65568 | tf_op jit(solution)/shard_map/ppermute | solution.py:136
  128.5 2.6 %collective-permute-done.10 = f32[64,128]{1,0:T(8,128)S(1)} collective-permute-done((f32[64,128]{1,0:T(8,128)S(1)}, f32[64,128]{1,0:T(8,128)S(1)}, u32[]{:S(2)}, u32[]{:S(2)}) %collective-permute-start.10) | collective-permute-done | bytes 32800 | tf_op jit(solution)/shard_map/ppermute | solution.py:136
  131.7 3.6 %collective-permute-done.11 = f32[64,128]{1,0:T(8,128)S(1)} collective-permute-done((f32[64,128]{1,0:T(8,128)S(1)}, f32[64,128]{1,0:T(8,128)S(1)}, u32[]{:S(2)}, u32[]{:S(2)}) %collective-permute-start.11) | collective-permute-done | bytes 32800 | tf_op jit(solution)/shard_map/ppermute | solution.py:136
  135.4 3.1 %collective-permute-done.12 = f32[64,128]{1,0:T(8,128)S(1)} collective-permute-done((f32[64,128]{1,0:T(8,128)S(1)}, f32[64,128]{1,0:T(8,128)S(1)}, u32[]{:S(2)}, u32[]{:S(2)}) %collective-permute-start.12) | collective-permute-done | bytes 32800 | tf_op jit(solution)/shard_map/ppermute | solution.py:136
  138.4 3.7 %collective-permute-done.13 = f32[64,128]{1,0:T(8,128)S(1)} collective-permute-done((f32[64,128]{1,0:T(8,128)S(1)}, f32[64,128]{1,0:T(8,128)S(1)}, u32[]{:S(2)}, u32[]{:S(2)}) %collective-permute-start.13) | collective-permute-done | bytes 32800 | tf_op jit(solution)/shard_map/ppermute | solution.py:136
  142.1 2.4 %collective-permute-start.14 = (f32[64,128]{1,0:T(8,128)S(1)}, f32[64,128]{1,0:T(8,128)S(1)}, u32[]{:S(2)}, u32[]{:S(2)}) collective-permute-start(f32[64,128]{1,0:T(8,128)S(1)} %add.50), channel_id=1, source_target_pairs={{0,2},{1,3},{2,0},{3,1},{4,6},{5,7},{6,4},{7,5},{8,10},{9,11},{10,... | collective-permute-start | bytes 98312 | tf_op jit(solution)/shard_map/ppermute | solution.py:136
  144.5 4.3 %collective-permute-done.14 = f32[64,128]{1,0:T(8,128)S(1)} collective-permute-done((f32[64,128]{1,0:T(8,128)S(1)}, f32[64,128]{1,0:T(8,128)S(1)}, u32[]{:S(2)}, u32[]{:S(2)}) %collective-permute-start.14) | collective-permute-done | bytes 32800 | tf_op jit(solution)/shard_map/ppermute | solution.py:136
  148.9 9.6 %collective-permute-start.3 = (f32[2,256,512]{2,1,0:T(8,128)S(1)}, f32[2,256,512]{2,1,0:T(8,128)S(1)}, u32[]{:S(2)}, u32[]{:S(2)}) collective-permute-start(f32[2,256,512]{2,1,0:T(8,128)S(1)} %copy-done.9), channel_id=1, source_target_pairs={{0,16},{16,32},{32,48},{48,64},{64,80},{80,96},{96,112},{112,128},... | collective-permute-start | bytes 3145736 | tf_op jit(solution)/shard_map/ppermute | solution.py:19
  158.6 2.3 %collective-permute-start.16 = (f32[128,128]{1,0:T(8,128)S(1)}, f32[128,128]{1,0:T(8,128)S(1)}, u32[]{:S(2)}, u32[]{:S(2)}) collective-permute-start(f32[128,128]{1,0:T(8,128)S(1)} %pad_maximum_fusion.2), channel_id=1, source_target_pairs={{0,64},{16,80},{32,96},{48,112},{64,0},{80,16},{96,32},{112,48},{1... | collective-permute-start | bytes 196616 | tf_op jit(solution)/shard_map/ppermute | solution.py:136
  160.9 3.4 %collective-permute-start.4 = (f32[2,256,256]{2,1,0:T(8,128)S(1)}, f32[2,256,256]{2,1,0:T(8,128)S(1)}, u32[]{:S(2)}, u32[]{:S(2)}) collective-permute-start(f32[2,256,256]{2,1,0:T(8,128)S(1)} %copy-done.13), channel_id=1, source_target_pairs={{0,16},{16,32},{32,48},{48,64},{64,80},{80,96},{96,112},{112,128},... | collective-permute-start | bytes 1572872 | tf_op jit(solution)/shard_map/ppermute | solution.py:19
  164.4 10.9 %collective-permute-start.17 = (f32[256,128]{1,0:T(8,128)S(1)}, f32[256,128]{1,0:T(8,128)S(1)}, u32[]{:S(2)}, u32[]{:S(2)}) collective-permute-start(f32[256,128]{1,0:T(8,128)S(1)} %pad_maximum_fusion.1), channel_id=1, source_target_pairs={{0,32},{16,48},{32,0},{48,16},{64,96},{80,112},{96,64},{112,80},{1... | collective-permute-start | bytes 393224 | tf_op jit(solution)/shard_map/ppermute | solution.py:136
  175.3 1.9 collective-permute-start.6
  177.2 4.9 %collective-permute-done.4 = f32[2,256,256]{2,1,0:T(8,128)S(1)} collective-permute-done((f32[2,256,256]{2,1,0:T(8,128)S(1)}, f32[2,256,256]{2,1,0:T(8,128)S(1)}, u32[]{:S(2)}, u32[]{:S(2)}) %collective-permute-start.4) | collective-permute-done | bytes 524320 | tf_op jit(solution)/shard_map/ppermute | solution.py:19
  182.2 8.9 %collective-permute-start.5 = (f32[2,256,256]{2,1,0:T(8,128)S(1)}, f32[2,256,256]{2,1,0:T(8,128)S(1)}, u32[]{:S(2)}, u32[]{:S(2)}) collective-permute-start(f32[2,256,256]{2,1,0:T(8,128)S(1)} %add.42), channel_id=1, source_target_pairs={{0,1},{1,2},{2,3},{3,4},{4,5},{5,6},{6,7},{7,8},{8,9},{9,10},{10,1... | collective-permute-start | bytes 1572872 | tf_op jit(solution)/shard_map/ppermute | solution.py:19
  191.3 2.4 %add_dynamic-update-slice_fusion = f32[2,512,512]{2,1,0:T(8,128)} fusion(f32[2,512,512]{2,1,0:T(8,128)} %get-tuple-element.32, f32[2,256,512]{2,1,0:T(8,128)S(1)} %collective-permute-done.3), kind=kLoop, calls=%fused_computation.2 | loop fusion | flops 262144 | bytes 3145728 | tf_op jit(solution)/shard_map/scatter-add | solution.py:171
  193.7 26.2 %collective-permute-done.6 = f32[2,256,256]{2,1,0:T(8,128)S(1)} collective-permute-done((f32[2,256,256]{2,1,0:T(8,128)S(1)}, f32[2,256,256]{2,1,0:T(8,128)S(1)}, u32[]{:S(2)}, u32[]{:S(2)}) %collective-permute-start.6) | collective-permute-done | bytes 524320 | tf_op jit(solution)/shard_map/ppermute | solution.py:19
  219.8 5.4 %collective-permute-done.5 = f32[2,256,256]{2,1,0:T(8,128)S(1)} collective-permute-done((f32[2,256,256]{2,1,0:T(8,128)S(1)}, f32[2,256,256]{2,1,0:T(8,128)S(1)}, u32[]{:S(2)}, u32[]{:S(2)}) %collective-permute-start.5) | collective-permute-done | bytes 524320 | tf_op jit(solution)/shard_map/ppermute | solution.py:19
  225.2 2.3 %fusion = f32[2,512,512]{2,1,0:T(8,128)} fusion(f32[2,512,512]{2,1,0:T(8,128)} %add_dynamic-update-slice_fusion, f32[2,256,256]{2,1,0:T(8,128)S(1)} %collective-permute-done.6, f32[2,256,256]{2,1,0:T(8,128)S(1)} %collective-permute-done.5), kind=kLoop, calls=%fused_computation.1 | loop fusion | flops 524288 | bytes 3145728 | tf_op jit(solution)/shard_map/scatter-add | solution.py:172
  (67 shorter events, 9.6 us)
Async XLA Ops:
  0.6 9.6 %copy-start = (f32[2,512,512]{2,1,0:T(8,128)S(1)}, f32[2,512,512]{2,1,0:T(8,128)}, u32[]{:S(2)}) copy-start(f32[2,512,512]{2,1,0:T(8,128)} %tile.1) | copy-start | bytes 6291460
  2.1 56.7 %copy-start.14 = (s32[1,1,8,2]{2,3,1,0:T(2,128)S(1)}, s32[1,1,8,2]{2,3,1,0:T(2,128)}, u32[]{:S(2)}) copy-start(s32[1,1,8,2]{2,3,1,0:T(2,128)} %param.14) | copy-start | bytes 196
  2.1 50.3 %collective-permute-start = (f32[2,512,256]{2,1,0:T(8,128)S(1)}, f32[2,512,256]{2,1,0:T(8,128)S(1)}, u32[]{:S(2)}, u32[]{:S(2)}) collective-permute-start(f32[2,512,256]{2,1,0:T(8,128)S(1)} %slice.83), channel_id=1, source_target_pairs={{1,0},{2,1},{3,2},{4,3},{5,4},{6,5},{7,6},{8,7},{9,8},{10,9},{11,1... | collective-permute-start | bytes 3145736 | tf_op jit(solution)/shard_map/ppermute | solution.py:19
  11.3 55.4 %collective-permute-start.1 = (f32[2,256,512]{2,1,0:T(8,128)}, f32[2,256,512]{2,1,0:T(8,128)}, u32[]{:S(2)}, u32[]{:S(2)}) collective-permute-start(f32[2,256,512]{2,1,0:T(8,128)} %slice.84), channel_id=1, source_target_pairs={{16,0},{32,16},{48,32},{64,48},{80,64},{96,80},{112,96},{128,112},... | collective-permute-start | bytes 3145736 | tf_op jit(solution)/shard_map/ppermute | solution.py:19
  53.2 19.1 %collective-permute-start.2 = (f32[2,256,256]{2,1,0:T(8,128)}, f32[2,256,256]{2,1,0:T(8,128)}, u32[]{:S(2)}, u32[]{:S(2)}) collective-permute-start(f32[2,256,256]{2,1,0:T(8,128)} %slice.96), channel_id=1, source_target_pairs={{16,0},{32,16},{48,32},{64,48},{80,64},{96,80},{112,96},{128,112},... | collective-permute-start | bytes 1572872 | tf_op jit(solution)/shard_map/ppermute | solution.py:19
  72.3 1.6 copy-start.1
  73.9 1.2 copy-start.2
  75.1 1.2 copy-start.3
  76.3 1.0 copy-start.4
  77.4 1.0 copy-start.7
  114.1 0.8 copy-start.12
  114.9 1.0 copy-start.8
  115.9 45.0 %copy-start.13 = (f32[2,256,256]{2,1,0:T(8,128)S(1)}, f32[2,256,256]{2,1,0:T(8,128)}, u32[]{:S(2)}) copy-start(f32[2,256,256]{2,1,0:T(8,128)} %copy-done.12) | copy-start | bytes 1572868
  115.9 33.0 %copy-start.9 = (f32[2,256,512]{2,1,0:T(8,128)S(1)}, f32[2,256,512]{2,1,0:T(8,128)}, u32[]{:S(2)}) copy-start(f32[2,256,512]{2,1,0:T(8,128)} %copy-done.8) | copy-start | bytes 3145732
  116.6 58.7 %copy-start.11 = (f32[2,256,256]{2,1,0:T(8,128)S(1)}, f32[2,256,256]{2,1,0:T(8,128)}, u32[]{:S(2)}) copy-start(f32[2,256,256]{2,1,0:T(8,128)} %copy-done.10) | copy-start | bytes 1572868
  116.6 65.5 %copy-start.6 = (f32[2,256,256]{2,1,0:T(8,128)S(1)}, f32[2,256,256]{2,1,0:T(8,128)}, u32[]{:S(2)}) copy-start(f32[2,256,256]{2,1,0:T(8,128)} %copy-done.5) | copy-start | bytes 1572868
  116.6 1.7 collective-permute-start.7
  118.4 5.0 %collective-permute-start.8 = (f32[256,128]{1,0:T(8,128)S(1)}, f32[256,128]{1,0:T(8,128)S(1)}, u32[]{:S(2)}, u32[]{:S(2)}) collective-permute-start(f32[256,128]{1,0:T(8,128)S(1)} %slice_select_fusion.2), channel_id=1, source_target_pairs={{0,32},{16,48},{32,0},{48,16},{64,96},{80,112},{96,64},{112,80},{1... | collective-permute-start | bytes 393224 | tf_op jit(solution)/shard_map/ppermute | solution.py:136
  123.5 4.7 %collective-permute-start.9 = (f32[128,128]{1,0:T(8,128)S(1)}, f32[128,128]{1,0:T(8,128)S(1)}, u32[]{:S(2)}, u32[]{:S(2)}) collective-permute-start(f32[128,128]{1,0:T(8,128)S(1)} %slice_select_fusion.3), channel_id=1, source_target_pairs={{0,64},{16,80},{32,96},{48,112},{64,0},{80,16},{96,32},{112,48},{1... | collective-permute-start | bytes 196616 | tf_op jit(solution)/shard_map/ppermute | solution.py:136
  128.2 2.9 %collective-permute-start.10 = (f32[64,128]{1,0:T(8,128)S(1)}, f32[64,128]{1,0:T(8,128)S(1)}, u32[]{:S(2)}, u32[]{:S(2)}) collective-permute-start(f32[64,128]{1,0:T(8,128)S(1)} %slice_select_fusion.4), channel_id=1, source_target_pairs={{0,4},{1,5},{2,6},{3,7},{4,0},{5,1},{6,2},{7,3},{8,12},{9,13},{10,... | collective-permute-start | bytes 98312 | tf_op jit(solution)/shard_map/ppermute | solution.py:136
  131.1 4.3 %collective-permute-start.11 = (f32[64,128]{1,0:T(8,128)S(1)}, f32[64,128]{1,0:T(8,128)S(1)}, u32[]{:S(2)}, u32[]{:S(2)}) collective-permute-start(f32[64,128]{1,0:T(8,128)S(1)} %select_add_fusion.2), channel_id=1, source_target_pairs={{0,8},{1,9},{2,10},{3,11},{4,12},{5,13},{6,14},{7,15},{8,0},{9,1},... | collective-permute-start | bytes 98312 | tf_op jit(solution)/shard_map/ppermute | solution.py:136
  135.4 3.1 %collective-permute-start.12 = (f32[64,128]{1,0:T(8,128)S(1)}, f32[64,128]{1,0:T(8,128)S(1)}, u32[]{:S(2)}, u32[]{:S(2)}) collective-permute-start(f32[64,128]{1,0:T(8,128)S(1)} %add.48), channel_id=1, source_target_pairs={{0,128},{16,144},{32,160},{48,176},{64,192},{80,208},{96,224},{112... | collective-permute-start | bytes 98312 | tf_op jit(solution)/shard_map/ppermute | solution.py:136
  138.4 3.7 %collective-permute-start.13 = (f32[64,128]{1,0:T(8,128)S(1)}, f32[64,128]{1,0:T(8,128)S(1)}, u32[]{:S(2)}, u32[]{:S(2)}) collective-permute-start(f32[64,128]{1,0:T(8,128)S(1)} %add.49), channel_id=1, source_target_pairs={{0,1},{1,0},{2,3},{3,2},{4,5},{5,4},{6,7},{7,6},{8,9},{9,8},{10,11... | collective-permute-start | bytes 98312 | tf_op jit(solution)/shard_map/ppermute | solution.py:136
  142.1 6.8 %collective-permute-start.14 = (f32[64,128]{1,0:T(8,128)S(1)}, f32[64,128]{1,0:T(8,128)S(1)}, u32[]{:S(2)}, u32[]{:S(2)}) collective-permute-start(f32[64,128]{1,0:T(8,128)S(1)} %add.50), channel_id=1, source_target_pairs={{0,2},{1,3},{2,0},{3,1},{4,6},{5,7},{6,4},{7,5},{8,10},{9,11},{10,... | collective-permute-start | bytes 98312 | tf_op jit(solution)/shard_map/ppermute | solution.py:136
  148.9 9.7 %collective-permute-start.15 = (f32[64,128]{1,0:T(8,128)S(1)}, f32[64,128]{1,0:T(8,128)S(1)}, u32[]{:S(2)}, u32[]{:S(2)}) collective-permute-start(f32[64,128]{1,0:T(8,128)S(1)} %add.51), channel_id=1, source_target_pairs={{0,4},{1,5},{2,6},{3,7},{4,0},{5,1},{6,2},{7,3},{8,12},{9,13},{10,... | collective-permute-start | bytes 98312 | tf_op jit(solution)/shard_map/ppermute | solution.py:136
  148.9 42.4 %collective-permute-start.3 = (f32[2,256,512]{2,1,0:T(8,128)S(1)}, f32[2,256,512]{2,1,0:T(8,128)S(1)}, u32[]{:S(2)}, u32[]{:S(2)}) collective-permute-start(f32[2,256,512]{2,1,0:T(8,128)S(1)} %copy-done.9), channel_id=1, source_target_pairs={{0,16},{16,32},{32,48},{48,64},{64,80},{80,96},{96,112},{112,128},... | collective-permute-start | bytes 3145736 | tf_op jit(solution)/shard_map/ppermute | solution.py:19
  158.6 5.7 %collective-permute-start.16 = (f32[128,128]{1,0:T(8,128)S(1)}, f32[128,128]{1,0:T(8,128)S(1)}, u32[]{:S(2)}, u32[]{:S(2)}) collective-permute-start(f32[128,128]{1,0:T(8,128)S(1)} %pad_maximum_fusion.2), channel_id=1, source_target_pairs={{0,64},{16,80},{32,96},{48,112},{64,0},{80,16},{96,32},{112,48},{1... | collective-permute-start | bytes 196616 | tf_op jit(solution)/shard_map/ppermute | solution.py:136
  160.9 21.3 %collective-permute-start.4 = (f32[2,256,256]{2,1,0:T(8,128)S(1)}, f32[2,256,256]{2,1,0:T(8,128)S(1)}, u32[]{:S(2)}, u32[]{:S(2)}) collective-permute-start(f32[2,256,256]{2,1,0:T(8,128)S(1)} %copy-done.13), channel_id=1, source_target_pairs={{0,16},{16,32},{32,48},{48,64},{64,80},{80,96},{96,112},{112,128},... | collective-permute-start | bytes 1572872 | tf_op jit(solution)/shard_map/ppermute | solution.py:19
  164.4 26.7 %collective-permute-start.17 = (f32[256,128]{1,0:T(8,128)S(1)}, f32[256,128]{1,0:T(8,128)S(1)}, u32[]{:S(2)}, u32[]{:S(2)}) collective-permute-start(f32[256,128]{1,0:T(8,128)S(1)} %pad_maximum_fusion.1), channel_id=1, source_target_pairs={{0,32},{16,48},{32,0},{48,16},{64,96},{80,112},{96,64},{112,80},{1... | collective-permute-start | bytes 393224 | tf_op jit(solution)/shard_map/ppermute | solution.py:136
  175.3 44.5 %collective-permute-start.6 = (f32[2,256,256]{2,1,0:T(8,128)S(1)}, f32[2,256,256]{2,1,0:T(8,128)S(1)}, u32[]{:S(2)}, u32[]{:S(2)}) collective-permute-start(f32[2,256,256]{2,1,0:T(8,128)S(1)} %copy-done.11), channel_id=1, source_target_pairs={{0,1},{1,2},{2,3},{3,4},{4,5},{5,6},{6,7},{7,8},{8,9},{9,10},{10,1... | collective-permute-start | bytes 1572872 | tf_op jit(solution)/shard_map/ppermute | solution.py:19
  182.2 43.0 %collective-permute-start.5 = (f32[2,256,256]{2,1,0:T(8,128)S(1)}, f32[2,256,256]{2,1,0:T(8,128)S(1)}, u32[]{:S(2)}, u32[]{:S(2)}) collective-permute-start(f32[2,256,256]{2,1,0:T(8,128)S(1)} %add.42), channel_id=1, source_target_pairs={{0,1},{1,2},{2,3},{3,4},{4,5},{5,6},{6,7},{7,8},{8,9},{9,10},{10,1... | collective-permute-start | bytes 1572872 | tf_op jit(solution)/shard_map/ppermute | solution.py:19
  191.2 36.4 %collective-permute-start.18 = (f32[512,128]{1,0:T(8,128)S(1)}, f32[512,128]{1,0:T(8,128)S(1)}, u32[]{:S(2)}, u32[]{:S(2)}) collective-permute-start(f32[512,128]{1,0:T(8,128)S(1)} %pad_maximum_fusion), channel_id=1, source_target_pairs={{0,16},{16,0},{32,48},{48,32},{64,80},{80,64},{96,112},{112,96},{1... | collective-permute-start | bytes 786440 | tf_op jit(solution)/shard_map/ppermute | solution.py:136
  (2 other events, 1.6 us)

commit v3 on v2

v3 whole, which is shorter than its diff:
```python
import math

import jax
import jax.numpy as jnp
import numpy as np
from jax import lax
from jax.experimental import pallas as pl
from jax.experimental.pallas import tpu as pltpu
from jax.sharding import PartitionSpec as P


F32 = jnp.float32
BF16 = jnp.bfloat16


def passed_along(value, axis, steps):
    count = lax.axis_size(axis)
    first, last = (max(0, -steps), min(count, count - steps))
    return lax.ppermute(value, axis, [(source, source + steps) for source in range(first, last)])


def split(value):
    high = value.astype(BF16)
    return high, (value - high.astype(F32)).astype(BF16)


def half_tables(size):
    half = size // 2
    tables = []
    for odd in (0, 1):
        angle = ((2 * np.arange(half)[:, None] + odd) * np.arange(half)[None, :] % size) * (2.0 * math.pi / size)
        cosine, sine = np.cos(angle) / math.sqrt(size), np.sin(angle) / math.sqrt(size)
        tables.append(np.block([[cosine, sine], [-sine, cosine]]).astype(np.float32))
    return np.stack(tables)


def split_table(table):
    high = table.astype(BF16)
    return np.stack([high, (table - high.astype(np.float32)).astype(BF16)], axis=1)


def dot(left, right):
    return jnp.dot(left, right, preferred_element_type=F32)


def rolled(block, shift, axis):
    size = block.shape[axis]
    small = 8 if axis == 0 else 128
    count = size // small
    pieces = []
    for index in range(count):
        piece = block[index * small:(index + 1) * small] if axis == 0 else block[:, index * small:(index + 1) * small]
        pieces.append(pltpu.roll(piece, shift, axis))
    place = lax.broadcasted_iota(jnp.int32, pieces[0].shape, axis)
    inside = place >= shift
    out = [jnp.where(inside, pieces[index], pieces[index - 1]) for index in range(count)]
    return jnp.concatenate(out, axis=axis)


def unrolled(block, shift, axis):
    size = block.shape[axis]
    small = 8 if axis == 0 else 128
    count = size // small
    back = lax.rem(small - shift, small)
    pieces = []
    for index in range(count):
        piece = block[index * small:(index + 1) * small] if axis == 0 else block[:, index * small:(index + 1) * small]
        pieces.append(pltpu.roll(piece, back, axis))
    place = lax.broadcasted_iota(jnp.int32, pieces[0].shape, axis)
    inside = place < small - shift
    out = [jnp.where(inside, pieces[index], pieces[(index + 1) % count]) for index in range(count)]
    return jnp.concatenate(out, axis=axis)


def prepare_kernel(off, amp, probe, pick, amp_out, probe_out):
    number = pl.program_id(0)
    side = probe.shape[1]
    half = side // 2
    row, lane = lax.rem(off[number, 0], 8), lax.rem(off[number, 1], 128)
    high, low = split(amp[0])
    high, low = split(dot(high, pick[0]) + dot(low, pick[0]))
    both = dot(pick[1], high) + dot(pick[1], low)
    amp_out[0, 0] = both[:, :half]
    amp_out[0, 1] = both[:, half:]
    for part in (0, 1):
        probe_out[0, part] = rolled(rolled(probe[part], row, 0), lane, 1)


def prepare(off, amp, probe):
    count, side = amp.shape[0], amp.shape[1]
    half = side // 2
    pick = np.zeros((side, side), np.float32)
    pick[2 * np.arange(half), np.arange(half)] = 1.0
    pick[2 * np.arange(half) + 1, half + np.arange(half)] = 1.0
    return pl.pallas_call(
        prepare_kernel,
        grid=(count,),
        out_shape=(jax.ShapeDtypeStruct((count, 2, side, half), F32), jax.ShapeDtypeStruct((count, 2, side, side), F32)),
        in_specs=[pl.BlockSpec(memory_space=pltpu.SMEM),
                  pl.BlockSpec((1, side, side), lambda i: (i, 0, 0)),
                  pl.BlockSpec((2, side, side), lambda i: (0, 0, 0)),
                  pl.BlockSpec((2, side, side), lambda i: (0, 0, 0))],
        out_specs=(pl.BlockSpec((1, 2, side, half), lambda i: (i, 0, 0, 0)),
                   pl.BlockSpec((1, 2, side, side), lambda i: (i, 0, 0, 0))),
    )(off, amp, probe, jnp.asarray(np.stack([pick, pick.T]).astype(BF16)))


def one_patch(top, left, amp, probe, left_table, right_table, ext, grad, probe_acc,
              view, a_high, a_low, x_high, x_low):
    side = probe.shape[1]
    half, step = side // 2, 32
    base_row = pl.multiple_of(top // 8 * 8, 8)
    base_col = pl.multiple_of(left // 128 * 128, 128)
    row, lane = top - base_row, left - base_col
    lanes = lax.broadcasted_iota(jnp.int32, (8, 128), 1)
    in_lane = lanes >= lane
    in_row = lax.broadcasted_iota(jnp.int32, (8, 128), 0) >= row

    def wide(mask, rows):
        return jnp.concatenate([mask] * (rows // 8), axis=0) if rows > 8 else mask

    def tiles(part, offset, rows):
        start = pl.multiple_of(base_row + offset, 8)
        block = ext[part, pl.ds(start, rows), pl.ds(base_col, side + 128)]
        return jnp.where(wide(in_lane, rows), block[:, :128], block[:, side:]), block[:, 128:side]

    def window(part, offset, rows):
        near, far = tiles(part, offset, rows)
        if offset == 0:
            near_end, far_end = tiles(part, side, 8)
            near = jnp.concatenate([jnp.where(in_row, near[:8], near_end), near[8:]], axis=0)
            far = jnp.concatenate([jnp.where(in_row, far[:8], far_end), far[8:]], axis=0)
        out = jnp.concatenate([near, far], axis=1)
        view[part, offset:offset + rows] = out
        return out

    def put(high, low, which, rows, value):
        top_part, rest = split(value)
        high[which, rows] = top_part
        low[which, rows] = rest

    for at in range(0, half, step):
        def wave(offset):
            here = slice(offset, offset + step)
            vr, vi = window(0, offset, step), window(1, offset, step)
            pr, pi = probe[0, here], probe[1, here]
            return pr * vr - pi * vi, pr * vi + pi * vr

        upper_r, upper_i = wave(at)
        lower_r, lower_i = wave(half + at)
        put(a_high, a_low, 0, slice(at, at + step), upper_r + lower_r)
        put(a_high, a_low, 0, slice(half + at, half + at + step), upper_i + lower_i)
        put(a_high, a_low, 1, slice(at, at + step), upper_r - lower_r)
        put(a_high, a_low, 1, slice(half + at, half + at + step), upper_i - lower_i)

    def left_product(table, odd):
        fine, rough = table[odd, 1], table[odd, 0]
        return dot(jnp.concatenate([rough, rough, fine], axis=1),
                   jnp.concatenate([a_high[odd], a_low[odd], a_high[odd]], axis=0))

    def right_product(table, odd):
        fine, rough = table[odd, 1], table[odd, 0]
        return dot(jnp.concatenate([x_high[odd], x_low[odd], x_high[odd]], axis=1),
                   jnp.concatenate([rough, rough, fine], axis=0))

    for odd in (0, 1):
        out = left_product(left_table, odd)
        for at in range(0, half, step):
            real, imag = out[at:at + step], out[half + at:half + at + step]
            rows = slice(odd * half + at, odd * half + at + step)
            put(x_high, x_low, 0, rows, jnp.concatenate([real[:, :half] + real[:, half:], imag[:, :half] + imag[:, half:]], axis=1))
            put(x_high, x_low, 1, rows, jnp.concatenate([real[:, :half] - real[:, half:], imag[:, :half] - imag[:, half:]], axis=1))
    for odd in (0, 1):
        far = right_product(right_table, odd)
        for at in range(0, side, step):
            rows = slice(at, at + step)
            real, imag = far[rows, :half], far[rows, half:]
            keep = 1.0 - amp[odd, rows] * lax.rsqrt(jnp.maximum(real * real + imag * imag, 0.25))
            put(x_high, x_low, odd, rows, jnp.concatenate([real * keep, imag * keep], axis=1))
    even, odd_part = right_product(left_table, 0), right_product(left_table, 1)
    for at in range(0, side, step):
        rows = slice(at, at + step)
        total, difference = even[rows] + odd_part[rows], even[rows] - odd_part[rows]
        which, place = at // half, at % half
        put(a_high, a_low, which, slice(place, place + step), jnp.concatenate([total[:, :half], difference[:, :half]], axis=1))
        put(a_high, a_low, which, slice(half + place, half + place + step), jnp.concatenate([total[:, half:], difference[:, half:]], axis=1))
    even, odd_part = left_product(right_table, 0), left_product(right_table, 1)

    def add(part, offset, term):
        rows = term.shape[0]
        start = pl.multiple_of(base_row + offset, 8)
        here = wide(in_lane, rows)
        zero = jnp.zeros((rows, 128), F32)
        near, far = term[:, :128], term[:, 128:]
        grad[part, pl.ds(start, rows), pl.ds(base_col, side + 128)] += jnp.concatenate(
            [jnp.where(here, near, zero), far, jnp.where(here, zero, near)], axis=1)

    zero_row = jnp.zeros((8, side), F32)
    both_in_row = jnp.concatenate([in_row] * (side // 128), axis=1)
    for at in range(0, side, step):
        rows = slice(at, at + step)
        place = at % half
        if at < half:
            cr = even[place:place + step] + odd_part[place:place + step]
            ci = even[half + place:half + place + step] + odd_part[half + place:half + place + step]
        else:
            cr = even[place:place + step] - odd_part[place:place + step]
            ci = even[half + place:half + place + step] - odd_part[half + place:half + place + step]
        pr, pi = probe[0, rows], probe[1, rows]
        vr, vi = view[0, rows], view[1, rows]
        for part, term in enumerate((pr * cr + pi * ci, pr * ci - pi * cr)):
            if at == 0:
                add(part, side, jnp.where(both_in_row, zero_row, term[:8]))
                term = jnp.concatenate([jnp.where(both_in_row, term[:8], zero_row), term[8:]], axis=0)
            add(part, at, term)
        view[0, rows] = unrolled(vr * cr + vi * ci, lane, 1)
        view[1, rows] = unrolled(vr * ci - vi * cr, lane, 1)
    back = lax.rem(8 - row, 8)
    inside = lax.broadcasted_iota(jnp.int32, (8, side), 0) < 8 - row
    for part in (0, 1):
        opening = pltpu.roll(view[part, 0:8], back, 0)
        now = opening
        for at in range(0, side, 8):
            after = opening if at + 8 == side else pltpu.roll(view[part, at + 8:at + 16], back, 0)
            probe_acc[part, at:at + 8] += jnp.where(inside, now, after)
            now = after


def patches_kernel(off, tile, upper, lower, bottom, corner, probe, amp, left_table, right_table,
                   main_out, upper_out, lower_out, bottom_out, corner_out, probe_out, ext, grad, *scratch):
    side = upper.shape[2]
    rows, cols = tile.shape[1], tile.shape[2]
    ext[:, :rows, :cols] = tile[...]
    ext[:, :side, cols:] = upper[...]
    ext[:, side:rows, cols:] = lower[...]
    ext[:, rows:, :cols] = bottom[...]
    ext[:, rows:, cols:] = corner[...]
    grad[...] = jnp.zeros_like(grad)
    probe_out[...] = jnp.zeros_like(probe_out)

    def step(number, carry):
        one_patch(off[number, 0], off[number, 1], amp.at[number], probe.at[number], left_table, right_table,
                  ext, grad, probe_out, *scratch)
        return carry

    lax.fori_loop(0, amp.shape[0], step, 0)
    main_out[...] = grad[:, :rows, :cols]
    upper_out[...] = grad[:, :side, cols:]
    lower_out[...] = grad[:, side:rows, cols:]
    bottom_out[...] = grad[:, rows:, :cols]
    corner_out[...] = grad[:, rows:, cols:]


def all_patches(off, tile, upper, lower, bottom, corner, probe, amp):
    side = upper.shape[2]
    rows, cols = tile.shape[1], tile.shape[2]
    table = half_tables(side)
    tables = [jnp.asarray(split_table(table)), jnp.asarray(split_table(table.transpose(0, 2, 1)))]
    amps, probes = prepare(off, amp, probe)
    vmem = pl.BlockSpec(memory_space=pltpu.VMEM)
    shape = lambda *dims: jax.ShapeDtypeStruct(dims, F32)
    return pl.pallas_call(
        patches_kernel,
        out_shape=(shape(2, rows, cols), shape(2, side, side), shape(2, rows - side, side), shape(2, side, cols),
                   shape(2, side, side), shape(2, side, side)),
        in_specs=[pl.BlockSpec(memory_space=pltpu.SMEM)] + [vmem] * 9,
        out_specs=[vmem] * 6,
        scratch_shapes=[pltpu.VMEM((2, rows + side, cols + side), F32)] * 2
                     + [pltpu.VMEM((2, side, side), F32)] + [pltpu.VMEM((2, side, side), BF16)] * 4,
        compiler_params=pltpu.CompilerParams(vmem_limit_bytes=36 * 1024 * 1024),
    )(off, tile, upper, lower, bottom, corner, probes, amps, *tables)


ACROSS, LINES = (2, 4, 6), (4, 8, 12)


def exchanged(pieces, distances, axis):
    return [lax.ppermute(piece, axis, [(i, i ^ distance) for i in range(lax.axis_size(axis))])
            for piece, distance in zip(pieces, distances)]


def added(parts):
    while len(parts) > 1:
        parts = [parts[i] + parts[i + 1] for i in range(0, len(parts), 2)]
    return parts[0]


def scattered(value, me, distances, axis):
    rows = value.shape[0] // 4
    pieces = [lax.dynamic_slice_in_dim(value, (me ^ place) * rows, rows, 0) for place in range(4)]
    return added(pieces[:1] + exchanged(pieces[1:], distances, axis))


def everywhere(value, distances, axis):
    return added([value] + exchanged([value] * 3, distances, axis))


def gathered(value, me, distances, axis):
    rows = value.shape[0]
    whole = jnp.zeros((rows * 4, value.shape[1]), value.dtype)
    for place, part in enumerate([value] + exchanged([value] * 3, distances, axis)):
        whole = lax.dynamic_update_slice_in_dim(whole, part, (me ^ place) * rows, 0)
    return whole


def summed_everywhere(value):
    shape = value.shape
    value = value.reshape(-1, shape[-1])
    chip = (lax.axis_index("row") >> 1) & 3
    line = lax.axis_index("col") >> 2
    value = scattered(value, chip, ACROSS, "row")
    value = scattered(value, line, LINES, "col")
    value = everywhere(value, (1, 8, 9), "row")
    value = everywhere(value, (1, 2, 3), "col")
    value = gathered(value, line, LINES, "col")
    value = gathered(value, chip, ACROSS, "row")
    return value.reshape(shape)


def shards_body(object_field, probe, amplitude, offsets):
    side = probe.shape[1]
    upper = passed_along(object_field[:, :side, :side], "col", -1)
    lower = passed_along(object_field[:, side:, :side], "col", -1)
    bottom = passed_along(object_field[:, :side, :], "row", -1)
    corner = passed_along(upper, "row", -1)
    main, upper, lower, bottom, corner, probe_acc = all_patches(
        offsets[0, 0], object_field, upper, lower, bottom, corner, probe, amplitude[0, 0])
    corner_back = passed_along(corner, "row", 1)
    lower_back = passed_along(lower, "col", 1)
    bottom_back = passed_along(bottom, "row", 1)
    upper_back = passed_along(upper + corner_back, "col", 1)
    count = amplitude.shape[2] * lax.axis_size("row") * lax.axis_size("col")
    probe_total = summed_everywhere(probe_acc) / count
    right_back = jnp.concatenate([upper_back, lower_back], axis=1)
    main = main.at[:, :side, :].add(bottom_back)
    object_grad = main.at[:, :, :side].add(right_back)
    return (object_grad, probe_total)


def solution(mesh):
    placed = (
        P(None, "row", "col"),
        P(),
        P("row", "col", None, None, None),
        P("row", "col", None, None),
    )
    return jax.shard_map(
        shards_body, mesh=mesh, in_specs=placed, out_specs=(P(None, "row", "col"), P()), check_vma=False
    )
```

time: 229 us -> 202 us (0.88)
  waiting for transfers between devices: 117 us -> 94 us
  Pallas kernels: 34.1 us -> 26.4 us
  starting transfers between devices: 57.2 us -> 61.8 us
  other arithmetic: 5.14 us -> 2.42 us
    ppermute x7 -> x8, waiting for transfers between devices: 88.1 us -> 69.7 us  [passed_along(): lax.ppermute(value, axis, [(source, source + steps) for source in range(f...]
    pallas_call x1, Pallas kernels: 34.1 us -> 18.2 us  [all_patches(): pl.pallas_call(patches_kernel, out_shape=(shape(2, rows, cols), shape(2,...]
    pallas_call x0 -> x1, Pallas kernels: none -> 8.18 us  [prepare(): pl.pallas_call(prepare_kernel, grid=(count,), out_shape=(jax.ShapeDtypeSt...]
    ppermute x12 -> x18, waiting for transfers between devices: 28.5 us -> 24.3 us  [exchanged(): lax.ppermute(piece, axis, [(i, i ^ distance) for i in range(lax.axis_size...]
    ppermute x12 -> x18, starting transfers between devices: 16.9 us -> 21 us  [exchanged(): lax.ppermute(piece, axis, [(i, i ^ distance) for i in range(lax.axis_size...]
    unnamed x30 -> x32, local copies, waits for them, and re-layouts: 9.47 us -> 10.6 us
    ppermute x7 -> x8, starting transfers between devices: 40.4 us -> 40.8 us  [passed_along(): lax.ppermute(value, axis, [(source, source + steps) for source in range(f...]
  transfers between devices with their start and end apart: 19 -> 26, of which waited for: 14 -> 18; matrix products, arithmetic and copies ran while one was open for 3% -> 1% of each run, Pallas kernels for 0% -> 4%
where the time goes in v3:
time: 202 us
  waiting for transfers between devices  94 us (47%)
  starting transfers between devices  61.8 us (31%)
  Pallas kernels  26.4 us (13%)
  local copies, waits for them, and re-layouts  16 us (8%)
  other arithmetic  2.42 us (1%)
    ppermute x8, waiting for transfers between devices, passed_along(): lax.ppermute(value, axis, [(source, source + steps) for source in range(f...  69.7 us
    ppermute x8, starting transfers between devices, passed_along(): lax.ppermute(value, axis, [(source, source + steps) for source in range(f...  40.8 us
    ppermute x18, waiting for transfers between devices, exchanged(): lax.ppermute(piece, axis, [(i, i ^ distance) for i in range(lax.axis_size...  24.3 us
    ppermute x18, starting transfers between devices, exchanged(): lax.ppermute(piece, axis, [(i, i ^ distance) for i in range(lax.axis_size...  21 us
    pallas_call x1, Pallas kernels, all_patches(): pl.pallas_call(patches_kernel, out_shape=(shape(2, rows, cols), shape(2,...  18.2 us
    unnamed x32, local copies, waits for them, and re-layouts  10.6 us
    pallas_call x1, Pallas kernels, prepare(): pl.pallas_call(prepare_kernel, grid=(count,), out_shape=(jax.ShapeDtypeSt...  8.18 us
  transfers between devices with their start and end apart: 26, of which 18 were waited for; matrix products, arithmetic and copies ran while one was open for 1% of the time, Pallas kernels for 4%

profile of v3, /device:TPU:31, one launch (start us, length us, event | category | flops | bytes accessed | tf_op | source)
XLA Modules:
  0.0 201.5 jit_solution(1787144128935262071)
XLA Ops:
  0.6 2.2 %fusion.1 = (f32[2,256,256]{2,1,0:T(8,128)}, f32[2,256,256]{2,1,0:T(8,128)S(1)}) fusion(f32[2,512,512]{2,1,0:T(8,128)} %tile.1), kind=kLoop, calls=%fused_computation.22 | loop fusion | bytes 2097152 | tf_op jit(solution)/shard_map/slice | solution.py:323
  2.9 8.1 %collective-permute-start = (f32[2,256,256]{2,1,0:T(8,128)S(1)}, f32[2,256,256]{2,1,0:T(8,128)}, u32[]{:S(2)}, u32[]{:S(2)}) collective-permute-start(f32[2,256,256]{2,1,0:T(8,128)S(1)} %get-tuple-element.45), channel_id=1, source_target_pairs={{1,0},{2,1},{3,2},{4,3},{5,4},{6,5},{7,6},{8,7},{9,8},{10,9},{11,1... | collective-permute-start | bytes 1572872 | tf_op jit(solution)/shard_map/ppermute | solution.py:19
  12.1 2.9 %collective-permute-start.2 = (f32[2,256,512]{2,1,0:T(8,128)}, f32[2,256,512]{2,1,0:T(8,128)S(1)}, u32[]{:S(2)}, u32[]{:S(2)}) collective-permute-start(f32[2,256,512]{2,1,0:T(8,128)} %slice.59), channel_id=1, source_target_pairs={{16,0},{32,16},{48,32},{64,48},{80,64},{96,80},{112,96},{128,112},... | collective-permute-start | bytes 3145736 | tf_op jit(solution)/shard_map/ppermute | solution.py:19
  14.9 3.1 %collective-permute-start.1 = (f32[2,256,256]{2,1,0:T(8,128)}, f32[2,256,256]{2,1,0:T(8,128)}, u32[]{:S(2)}, u32[]{:S(2)}) collective-permute-start(f32[2,256,256]{2,1,0:T(8,128)} %get-tuple-element.44), channel_id=1, source_target_pairs={{1,0},{2,1},{3,2},{4,3},{5,4},{6,5},{7,6},{8,7},{9,8},{10,9},{11,1... | collective-permute-start | bytes 1572872 | tf_op jit(solution)/shard_map/ppermute | solution.py:19
  18.0 19.6 %collective-permute-done.upper = f32[2,256,256]{2,1,0:T(8,128)} collective-permute-done((f32[2,256,256]{2,1,0:T(8,128)S(1)}, f32[2,256,256]{2,1,0:T(8,128)}, u32[]{:S(2)}, u32[]{:S(2)}) %collective-permute-start) | collective-permute-done | bytes 524320 | tf_op jit(solution)/shard_map/ppermute | solution.py:19
  37.6 7.1 %collective-permute-start.3 = (f32[2,256,256]{2,1,0:T(8,128)}, f32[2,256,256]{2,1,0:T(8,128)}, u32[]{:S(2)}, u32[]{:S(2)}) collective-permute-start(f32[2,256,256]{2,1,0:T(8,128)} %collective-permute-done.upper), channel_id=1, source_target_pairs={{16,0},{32,16},{48,32},{64,48},{80,64},{96,80},{112,96},{128,112},... | collective-permute-start | bytes 1572872 | tf_op jit(solution)/shard_map/ppermute | solution.py:19
  45.4 8.2 %shard_map.86 = (f32[8,2,256,128]{3,2,1,0:T(8,128)}, f32[8,2,256,256]{3,2,1,0:T(8,128)}) custom-call(s32[8,2]{1,0:T(8,128)} %copy.10.off, f32[8,256,256]{2,1,0:T(8,128)} %bitcast.4, f32[2,256,256]{2,1,0:T(8,128)} %probe.1, bf16[2,256,256]{2,1,0:T(8,128)(2,1)} %constant.86.clone.pick), custom_call_target="tpu_custom_call" | custom-call | tf_op jit(solution)/shard_map/pallas_call | solution.py:95
  53.6 8.1 %collective-permute-done.2.bottom = f32[2,256,512]{2,1,0:T(8,128)S(1)} collective-permute-done((f32[2,256,512]{2,1,0:T(8,128)}, f32[2,256,512]{2,1,0:T(8,128)S(1)}, u32[]{:S(2)}, u32[]{:S(2)}) %collective-permute-start.2) | collective-permute-done | bytes 1048608 | tf_op jit(solution)/shard_map/ppermute | solution.py:19
  61.7 11.3 %collective-permute-done.3.corner = f32[2,256,256]{2,1,0:T(8,128)} collective-permute-done((f32[2,256,256]{2,1,0:T(8,128)}, f32[2,256,256]{2,1,0:T(8,128)}, u32[]{:S(2)}, u32[]{:S(2)}) %collective-permute-start.3) | collective-permute-done | bytes 524320 | tf_op jit(solution)/shard_map/ppermute | solution.py:19
  73.0 2.2 %copy-done.1 = f32[8,2,256,256]{3,2,1,0:T(8,128)S(1)} copy-done((f32[8,2,256,256]{3,2,1,0:T(8,128)S(1)}, f32[8,2,256,256]{3,2,1,0:T(8,128)}, u32[]{:S(2)}) %copy-start.1) | copy-done | bytes 4194328
  75.2 1.6 copy-done.2
  78.9 18.2 %shard_map.87 = (f32[2,512,512]{2,1,0:T(8,128)}, f32[2,256,256]{2,1,0:T(8,128)S(1)}, f32[2,256,256]{2,1,0:T(8,128)S(1)}, f32[2,256,512]{2,1,0:T(8,128)S(1)}, f32...) custom-call(s32[8,2]{1,0:T(8,128)S(1)} %copy-done.7, f32[2,512,512]{2,1,0:T(8,128)S(1)} %copy-done, ...), custom_call_target="tpu_custom_call" | custom-call | tf_op jit(solution)/shard_map/pallas_call | solution.py:262
  101.9 2.5 %collective-permute-start.8 = (f32[128,256]{1,0:T(8,128)S(1)}, f32[128,256]{1,0:T(8,128)S(1)}, u32[]{:S(2)}, u32[]{:S(2)}) collective-permute-start(f32[128,256]{1,0:T(8,128)S(1)} %get-tuple-element.46), channel_id=1, source_target_pairs={{0,32},{16,48},{32,0},{48,16},{64,96},{80,112},{96,64},{112,80},{1... | collective-permute-start | bytes 393224 | tf_op jit(solution)/shard_map/ppermute | solution.py:278
  104.5 2.8 %collective-permute-done.9 = f32[128,256]{1,0:T(8,128)S(1)} collective-permute-done((f32[128,256]{1,0:T(8,128)S(1)}, f32[128,256]{1,0:T(8,128)S(1)}, u32[]{:S(2)}, u32[]{:S(2)}) %collective-permute-start.9) | collective-permute-done | bytes 131104 | tf_op jit(solution)/shard_map/ppermute | solution.py:278
  110.1 2.0 collective-permute-start.13
  112.1 1.6 collective-permute-done.12
  118.4 2.8 %collective-permute-start.18 = (f32[32,256]{1,0:T(8,128)S(1)}, f32[32,256]{1,0:T(8,128)S(1)}, u32[]{:S(2)}, u32[]{:S(2)}) collective-permute-start(f32[32,256]{1,0:T(8,128)S(1)} %add_add_fusion.2), channel_id=1, source_target_pairs={{0,2},{1,3},{2,0},{3,1},{4,6},{5,7},{6,4},{7,5},{8,10},{9,11},{10,... | collective-permute-start | bytes 98312 | tf_op jit(solution)/shard_map/ppermute | solution.py:278
  121.7 2.4 %collective-permute-start.17 = (f32[32,256]{1,0:T(8,128)S(1)}, f32[32,256]{1,0:T(8,128)S(1)}, u32[]{:S(2)}, u32[]{:S(2)}) collective-permute-start(f32[32,256]{1,0:T(8,128)S(1)} %add_add_fusion.2), channel_id=1, source_target_pairs={{0,1},{1,0},{2,3},{3,2},{4,5},{5,4},{6,7},{7,6},{8,9},{9,8},{10,11... | collective-permute-start | bytes 98312 | tf_op jit(solution)/shard_map/ppermute | solution.py:278
  126.4 1.6 collective-permute-start.20
  128.0 5.0 %collective-permute-start.4 = (f32[2,256,512]{2,1,0:T(8,128)S(1)}, f32[2,256,512]{2,1,0:T(8,128)S(1)}, u32[]{:S(2)}, u32[]{:S(2)}) collective-permute-start(f32[2,256,512]{2,1,0:T(8,128)S(1)} %copy-done.9), channel_id=1, source_target_pairs={{0,16},{16,32},{32,48},{48,64},{64,80},{80,96},{96,112},{112,128},... | collective-permute-start | bytes 3145736 | tf_op jit(solution)/shard_map/ppermute | solution.py:19
  133.1 1.9 collective-permute-start.5
  135.0 2.2 %collective-permute-start.21 = (f32[32,256]{1,0:T(8,128)S(1)}, f32[32,256]{1,0:T(8,128)S(1)}, u32[]{:S(2)}, u32[]{:S(2)}) collective-permute-start(f32[32,256]{1,0:T(8,128)S(1)} %get-tuple-element.43), channel_id=1, source_target_pairs={{0,8},{1,9},{2,10},{3,11},{4,12},{5,13},{6,14},{7,15},{8,0},{9,1},... | collective-permute-start | bytes 98312 | tf_op jit(solution)/shard_map/ppermute | solution.py:278
  137.2 1.7 collective-permute-start.22
  139.3 1.8 collective-permute-done.22
  141.2 4.4 %collective-permute-start.7 = (f32[2,256,256]{2,1,0:T(8,128)S(1)}, f32[2,256,256]{2,1,0:T(8,128)S(1)}, u32[]{:S(2)}, u32[]{:S(2)}) collective-permute-start(f32[2,256,256]{2,1,0:T(8,128)S(1)} %copy-done.11), channel_id=1, source_target_pairs={{0,1},{1,2},{2,3},{3,4},{4,5},{5,6},{6,7},{7,8},{8,9},{9,10},{10,1... | collective-permute-start | bytes 1572872 | tf_op jit(solution)/shard_map/ppermute | solution.py:19
  145.5 1.9 collective-permute-start.24
  147.5 6.8 %collective-permute-done.23 = f32[128,256]{1,0:T(8,128)S(1)} collective-permute-done((f32[128,256]{1,0:T(8,128)S(1)}, f32[128,256]{1,0:T(8,128)S(1)}, u32[]{:S(2)}, u32[]{:S(2)}) %collective-permute-start.23) | collective-permute-done | bytes 131104 | tf_op jit(solution)/shard_map/ppermute | solution.py:278
  154.7 4.9 %collective-permute-done.25 = f32[128,256]{1,0:T(8,128)S(1)} collective-permute-done((f32[128,256]{1,0:T(8,128)S(1)}, f32[128,256]{1,0:T(8,128)S(1)}, u32[]{:S(2)}, u32[]{:S(2)}) %collective-permute-start.25) | collective-permute-done | bytes 131104 | tf_op jit(solution)/shard_map/ppermute | solution.py:278
  159.7 8.4 %collective-permute-start.6 = (f32[2,256,256]{2,1,0:T(8,128)S(1)}, f32[2,256,256]{2,1,0:T(8,128)S(1)}, u32[]{:S(2)}, u32[]{:S(2)}) collective-permute-start(f32[2,256,256]{2,1,0:T(8,128)S(1)} %add.86), channel_id=1, source_target_pairs={{0,1},{1,2},{2,3},{3,4},{4,5},{5,6},{6,7},{7,8},{8,9},{9,10},{10,1... | collective-permute-start | bytes 1572872 | tf_op jit(solution)/shard_map/ppermute | solution.py:19
  169.3 25.0 %collective-permute-done.7 = f32[2,256,256]{2,1,0:T(8,128)S(1)} collective-permute-done((f32[2,256,256]{2,1,0:T(8,128)S(1)}, f32[2,256,256]{2,1,0:T(8,128)S(1)}, u32[]{:S(2)}, u32[]{:S(2)}) %collective-permute-start.7) | collective-permute-done | bytes 524320 | tf_op jit(solution)/shard_map/ppermute | solution.py:19
  194.3 5.6 %collective-permute-done.6 = f32[2,256,256]{2,1,0:T(8,128)S(1)} collective-permute-done((f32[2,256,256]{2,1,0:T(8,128)S(1)}, f32[2,256,256]{2,1,0:T(8,128)S(1)}, u32[]{:S(2)}, u32[]{:S(2)}) %collective-permute-start.6) | collective-permute-done | bytes 524320 | tf_op jit(solution)/shard_map/ppermute | solution.py:19
  200.2 1.3 copy-done.14
  (76 shorter events, 21.3 us)
Async XLA Ops:
  0.6 44.1 %copy-start.15 = (s32[1,1,8,2]{2,3,1,0:T(2,128)S(1)}, s32[1,1,8,2]{2,3,1,0:T(2,128)}, u32[]{:S(2)}) copy-start(s32[1,1,8,2]{2,3,1,0:T(2,128)} %param.14) | copy-start | bytes 196
  2.9 34.7 %collective-permute-start = (f32[2,256,256]{2,1,0:T(8,128)S(1)}, f32[2,256,256]{2,1,0:T(8,128)}, u32[]{:S(2)}, u32[]{:S(2)}) collective-permute-start(f32[2,256,256]{2,1,0:T(8,128)S(1)} %get-tuple-element.45), channel_id=1, source_target_pairs={{1,0},{2,1},{3,2},{4,3},{5,4},{6,5},{7,6},{8,7},{9,8},{10,9},{11,1... | collective-permute-start | bytes 1572872 | tf_op jit(solution)/shard_map/ppermute | solution.py:19
  12.1 49.6 %collective-permute-start.2 = (f32[2,256,512]{2,1,0:T(8,128)}, f32[2,256,512]{2,1,0:T(8,128)S(1)}, u32[]{:S(2)}, u32[]{:S(2)}) collective-permute-start(f32[2,256,512]{2,1,0:T(8,128)} %slice.59), channel_id=1, source_target_pairs={{16,0},{32,16},{48,32},{64,48},{80,64},{96,80},{112,96},{128,112},... | collective-permute-start | bytes 3145736 | tf_op jit(solution)/shard_map/ppermute | solution.py:19
  14.9 38.6 %collective-permute-start.1 = (f32[2,256,256]{2,1,0:T(8,128)}, f32[2,256,256]{2,1,0:T(8,128)}, u32[]{:S(2)}, u32[]{:S(2)}) collective-permute-start(f32[2,256,256]{2,1,0:T(8,128)} %get-tuple-element.44), channel_id=1, source_target_pairs={{1,0},{2,1},{3,2},{4,3},{5,4},{6,5},{7,6},{8,7},{9,8},{10,9},{11,1... | collective-permute-start | bytes 1572872 | tf_op jit(solution)/shard_map/ppermute | solution.py:19
  37.6 35.4 %collective-permute-start.3 = (f32[2,256,256]{2,1,0:T(8,128)}, f32[2,256,256]{2,1,0:T(8,128)}, u32[]{:S(2)}, u32[]{:S(2)}) collective-permute-start(f32[2,256,256]{2,1,0:T(8,128)} %collective-permute-done.upper), channel_id=1, source_target_pairs={{16,0},{32,16},{48,32},{64,48},{80,64},{96,80},{112,96},{128,112},... | collective-permute-start | bytes 1572872 | tf_op jit(solution)/shard_map/ppermute | solution.py:19
  45.4 27.7 %copy-start.7 = (s32[8,2]{1,0:T(8,128)S(1)}, s32[8,2]{1,0:T(8,128)}, u32[]{:S(2)}) copy-start(s32[8,2]{1,0:T(8,128)} %copy.10.off) | copy-start | bytes 196
  100.5 27.5 %copy-start.9 = (f32[2,256,512]{2,1,0:T(8,128)S(1)}, f32[2,256,512]{2,1,0:T(8,128)}, u32[]{:S(2)}) copy-start(f32[2,256,512]{2,1,0:T(8,128)} %copy-done.8) | copy-start | bytes 3145732
  100.5 40.6 %copy-start.11 = (f32[2,256,256]{2,1,0:T(8,128)S(1)}, f32[2,256,256]{2,1,0:T(8,128)}, u32[]{:S(2)}) copy-start(f32[2,256,256]{2,1,0:T(8,128)} %copy-done.10) | copy-start | bytes 1572868
  100.5 59.1 %copy-start.4 = (f32[2,256,256]{2,1,0:T(8,128)S(1)}, f32[2,256,256]{2,1,0:T(8,128)}, u32[]{:S(2)}) copy-start(f32[2,256,256]{2,1,0:T(8,128)} %copy-done.3) | copy-start | bytes 1572868
  101.7 5.5 %collective-permute-start.9 = (f32[128,256]{1,0:T(8,128)S(1)}, f32[128,256]{1,0:T(8,128)S(1)}, u32[]{:S(2)}, u32[]{:S(2)}) collective-permute-start(f32[128,256]{1,0:T(8,128)S(1)} %get-tuple-element.48), channel_id=1, source_target_pairs={{0,64},{16,80},{32,96},{48,112},{64,0},{80,16},{96,32},{112,48},{1... | collective-permute-start | bytes 393224 | tf_op jit(solution)/shard_map/ppermute | solution.py:278
  101.8 6.5 %collective-permute-start.10 = (f32[128,256]{1,0:T(8,128)S(1)}, f32[128,256]{1,0:T(8,128)S(1)}, u32[]{:S(2)}, u32[]{:S(2)}) collective-permute-start(f32[128,256]{1,0:T(8,128)S(1)} %get-tuple-element.47), channel_id=1, source_target_pairs={{0,96},{16,112},{32,64},{48,80},{64,32},{80,48},{96,0},{112,16},{1... | collective-permute-start | bytes 393224 | tf_op jit(solution)/shard_map/ppermute | solution.py:278
  101.9 6.4 %collective-permute-start.8 = (f32[128,256]{1,0:T(8,128)S(1)}, f32[128,256]{1,0:T(8,128)S(1)}, u32[]{:S(2)}, u32[]{:S(2)}) collective-permute-start(f32[128,256]{1,0:T(8,128)S(1)} %get-tuple-element.46), channel_id=1, source_target_pairs={{0,32},{16,48},{32,0},{48,16},{64,96},{80,112},{96,64},{112,80},{1... | collective-permute-start | bytes 393224 | tf_op jit(solution)/shard_map/ppermute | solution.py:278
  109.3 4.4 %collective-permute-start.12 = (f32[32,256]{1,0:T(8,128)S(1)}, f32[32,256]{1,0:T(8,128)S(1)}, u32[]{:S(2)}, u32[]{:S(2)}) collective-permute-start(f32[32,256]{1,0:T(8,128)S(1)} %get-tuple-element.51), channel_id=1, source_target_pairs={{0,8},{1,9},{2,10},{3,11},{4,12},{5,13},{6,14},{7,15},{8,0},{9,1},... | collective-permute-start | bytes 98312 | tf_op jit(solution)/shard_map/ppermute | solution.py:278
  110.1 4.0 %collective-permute-start.13 = (f32[32,256]{1,0:T(8,128)S(1)}, f32[32,256]{1,0:T(8,128)S(1)}, u32[]{:S(2)}, u32[]{:S(2)}) collective-permute-start(f32[32,256]{1,0:T(8,128)S(1)} %get-tuple-element.50), channel_id=1, source_target_pairs={{0,12},{1,13},{2,14},{3,15},{4,8},{5,9},{6,10},{7,11},{8,4},{9,5},... | collective-permute-start | bytes 98312 | tf_op jit(solution)/shard_map/ppermute | solution.py:278
  112.1 2.8 %collective-permute-start.11 = (f32[32,256]{1,0:T(8,128)S(1)}, f32[32,256]{1,0:T(8,128)S(1)}, u32[]{:S(2)}, u32[]{:S(2)}) collective-permute-start(f32[32,256]{1,0:T(8,128)S(1)} %get-tuple-element.49), channel_id=1, source_target_pairs={{0,4},{1,5},{2,6},{3,7},{4,0},{5,1},{6,2},{7,3},{8,12},{9,13},{10,... | collective-permute-start | bytes 98312 | tf_op jit(solution)/shard_map/ppermute | solution.py:278
  114.8 2.9 %collective-permute-start.15 = (f32[32,256]{1,0:T(8,128)S(1)}, f32[32,256]{1,0:T(8,128)S(1)}, u32[]{:S(2)}, u32[]{:S(2)}) collective-permute-start(f32[32,256]{1,0:T(8,128)S(1)} %add_add_fusion.3), channel_id=1, source_target_pairs={{0,128},{16,144},{32,160},{48,176},{64,192},{80,208},{96,224},{112... | collective-permute-start | bytes 98312 | tf_op jit(solution)/shard_map/ppermute | solution.py:278
  114.9 3.4 %collective-permute-start.16 = (f32[32,256]{1,0:T(8,128)S(1)}, f32[32,256]{1,0:T(8,128)S(1)}, u32[]{:S(2)}, u32[]{:S(2)}) collective-permute-start(f32[32,256]{1,0:T(8,128)S(1)} %add_add_fusion.3), channel_id=1, source_target_pairs={{0,144},{16,128},{32,176},{48,160},{64,208},{80,192},{96,240},{112... | collective-permute-start | bytes 98312 | tf_op jit(solution)/shard_map/ppermute | solution.py:278
  115.9 2.5 %collective-permute-start.14 = (f32[32,256]{1,0:T(8,128)S(1)}, f32[32,256]{1,0:T(8,128)S(1)}, u32[]{:S(2)}, u32[]{:S(2)}) collective-permute-start(f32[32,256]{1,0:T(8,128)S(1)} %add_add_fusion.3), channel_id=1, source_target_pairs={{0,16},{16,0},{32,48},{48,32},{64,80},{80,64},{96,112},{112,96},{1... | collective-permute-start | bytes 98312 | tf_op jit(solution)/shard_map/ppermute | solution.py:278
  118.4 6.8 %collective-permute-start.18 = (f32[32,256]{1,0:T(8,128)S(1)}, f32[32,256]{1,0:T(8,128)S(1)}, u32[]{:S(2)}, u32[]{:S(2)}) collective-permute-start(f32[32,256]{1,0:T(8,128)S(1)} %add_add_fusion.2), channel_id=1, source_target_pairs={{0,2},{1,3},{2,0},{3,1},{4,6},{5,7},{6,4},{7,5},{8,10},{9,11},{10,... | collective-permute-start | bytes 98312 | tf_op jit(solution)/shard_map/ppermute | solution.py:278
  121.2 5.2 %collective-permute-start.19 = (f32[32,256]{1,0:T(8,128)S(1)}, f32[32,256]{1,0:T(8,128)S(1)}, u32[]{:S(2)}, u32[]{:S(2)}) collective-permute-start(f32[32,256]{1,0:T(8,128)S(1)} %add_add_fusion.2), channel_id=1, source_target_pairs={{0,3},{1,2},{2,1},{3,0},{4,7},{5,6},{6,5},{7,4},{8,11},{9,10},{10,... | collective-permute-start | bytes 98312 | tf_op jit(solution)/shard_map/ppermute | solution.py:278
  121.7 4.7 %collective-permute-start.17 = (f32[32,256]{1,0:T(8,128)S(1)}, f32[32,256]{1,0:T(8,128)S(1)}, u32[]{:S(2)}, u32[]{:S(2)}) collective-permute-start(f32[32,256]{1,0:T(8,128)S(1)} %add_add_fusion.2), channel_id=1, source_target_pairs={{0,1},{1,0},{2,3},{3,2},{4,5},{5,4},{6,7},{7,6},{8,9},{9,8},{10,11... | collective-permute-start | bytes 98312 | tf_op jit(solution)/shard_map/ppermute | solution.py:278
  126.4 12.5 %collective-permute-start.20 = (f32[32,256]{1,0:T(8,128)S(1)}, f32[32,256]{1,0:T(8,128)S(1)}, u32[]{:S(2)}, u32[]{:S(2)}) collective-permute-start(f32[32,256]{1,0:T(8,128)S(1)} %get-tuple-element.43), channel_id=1, source_target_pairs={{0,4},{1,5},{2,6},{3,7},{4,0},{5,1},{6,2},{7,3},{8,12},{9,13},{10,... | collective-permute-start | bytes 98312 | tf_op jit(solution)/shard_map/ppermute | solution.py:278
  128.0 41.0 %collective-permute-start.4 = (f32[2,256,512]{2,1,0:T(8,128)S(1)}, f32[2,256,512]{2,1,0:T(8,128)S(1)}, u32[]{:S(2)}, u32[]{:S(2)}) collective-permute-start(f32[2,256,512]{2,1,0:T(8,128)S(1)} %copy-done.9), channel_id=1, source_target_pairs={{0,16},{16,32},{32,48},{48,64},{64,80},{80,96},{96,112},{112,128},... | collective-permute-start | bytes 3145736 | tf_op jit(solution)/shard_map/ppermute | solution.py:19
  133.1 26.6 %collective-permute-start.5 = (f32[2,256,256]{2,1,0:T(8,128)}, f32[2,256,256]{2,1,0:T(8,128)S(1)}, u32[]{:S(2)}, u32[]{:S(2)}) collective-permute-start(f32[2,256,256]{2,1,0:T(8,128)} %copy-done.12), channel_id=1, source_target_pairs={{0,16},{16,32},{32,48},{48,64},{64,80},{80,96},{96,112},{112,128},... | collective-permute-start | bytes 1572872 | tf_op jit(solution)/shard_map/ppermute | solution.py:19
  135.0 4.4 %collective-permute-start.21 = (f32[32,256]{1,0:T(8,128)S(1)}, f32[32,256]{1,0:T(8,128)S(1)}, u32[]{:S(2)}, u32[]{:S(2)}) collective-permute-start(f32[32,256]{1,0:T(8,128)S(1)} %get-tuple-element.43), channel_id=1, source_target_pairs={{0,8},{1,9},{2,10},{3,11},{4,12},{5,13},{6,14},{7,15},{8,0},{9,1},... | collective-permute-start | bytes 98312 | tf_op jit(solution)/shard_map/ppermute | solution.py:278
  137.2 4.0 %collective-permute-start.22 = (f32[32,256]{1,0:T(8,128)S(1)}, f32[32,256]{1,0:T(8,128)S(1)}, u32[]{:S(2)}, u32[]{:S(2)}) collective-permute-start(f32[32,256]{1,0:T(8,128)S(1)} %get-tuple-element.43), channel_id=1, source_target_pairs={{0,12},{1,13},{2,14},{3,15},{4,8},{5,9},{6,10},{7,11},{8,4},{9,5},... | collective-permute-start | bytes 98312 | tf_op jit(solution)/shard_map/ppermute | solution.py:278
  141.2 13.1 %collective-permute-start.23 = (f32[128,256]{1,0:T(8,128)S(1)}, f32[128,256]{1,0:T(8,128)S(1)}, u32[]{:S(2)}, u32[]{:S(2)}) collective-permute-start(f32[128,256]{1,0:T(8,128)S(1)} %constant_dynamic-update-slice_fusion.4), channel_id=1, source_target_pairs={{0,32},{16,48},{32,0},{48,16},{64,96},{80,112},{96,64},{112,80},{1... | collective-permute-start | bytes 393224 | tf_op jit(solution)/shard_map/ppermute | solution.py:278
  141.2 27.8 %copy-start.13 = (f32[2,512,512]{2,1,0:T(8,128)S(1)}, f32[2,512,512]{2,1,0:T(8,128)}, u32[]{:S(2)}) copy-start(f32[2,512,512]{2,1,0:T(8,128)} %get-tuple-element.36) | copy-start | bytes 6291460
  141.2 53.1 %collective-permute-start.7 = (f32[2,256,256]{2,1,0:T(8,128)S(1)}, f32[2,256,256]{2,1,0:T(8,128)S(1)}, u32[]{:S(2)}, u32[]{:S(2)}) collective-permute-start(f32[2,256,256]{2,1,0:T(8,128)S(1)} %copy-done.11), channel_id=1, source_target_pairs={{0,1},{1,2},{2,3},{3,4},{4,5},{5,6},{6,7},{7,8},{8,9},{9,10},{10,1... | collective-permute-start | bytes 1572872 | tf_op jit(solution)/shard_map/ppermute | solution.py:19
  145.5 9.2 %collective-permute-start.24 = (f32[128,256]{1,0:T(8,128)S(1)}, f32[128,256]{1,0:T(8,128)S(1)}, u32[]{:S(2)}, u32[]{:S(2)}) collective-permute-start(f32[128,256]{1,0:T(8,128)S(1)} %constant_dynamic-update-slice_fusion.4), channel_id=1, source_target_pairs={{0,64},{16,80},{32,96},{48,112},{64,0},{80,16},{96,32},{112,48},{1... | collective-permute-start | bytes 393224 | tf_op jit(solution)/shard_map/ppermute | solution.py:278
  154.3 5.3 %collective-permute-start.25 = (f32[128,256]{1,0:T(8,128)S(1)}, f32[128,256]{1,0:T(8,128)S(1)}, u32[]{:S(2)}, u32[]{:S(2)}) collective-permute-start(f32[128,256]{1,0:T(8,128)S(1)} %constant_dynamic-update-slice_fusion.4), channel_id=1, source_target_pairs={{0,96},{16,112},{32,64},{48,80},{64,32},{80,48},{96,0},{112,16},{1... | collective-permute-start | bytes 393224 | tf_op jit(solution)/shard_map/ppermute | solution.py:278
  159.7 40.2 %collective-permute-start.6 = (f32[2,256,256]{2,1,0:T(8,128)S(1)}, f32[2,256,256]{2,1,0:T(8,128)S(1)}, u32[]{:S(2)}, u32[]{:S(2)}) collective-permute-start(f32[2,256,256]{2,1,0:T(8,128)S(1)} %add.86), channel_id=1, source_target_pairs={{0,1},{1,2},{2,3},{3,4},{4,5},{5,6},{6,7},{7,8},{8,9},{9,10},{10,1... | collective-permute-start | bytes 1572872 | tf_op jit(solution)/shard_map/ppermute | solution.py:19
  (10 other events, 21.0 us)

commit v4 on v3

--- a/solution.py
+++ b/solution.py
@@ -1,3 +1,4 @@
+import functools
 import math
 
 import jax
@@ -226,33 +227,39 @@
             now = after
 
 
-def patches_kernel(off, tile, upper, lower, bottom, corner, probe, amp, left_table, right_table,
-                   main_out, upper_out, lower_out, bottom_out, corner_out, probe_out, ext, grad, *scratch):
+def patches_kernel(off, tile, upper, middle, lower, bottom, corner, probe, amp, left_table, right_table,
+                   main_out, upper_out, lower_out, bottom_out, corner_out, probe_out, ext, grad, *scratch, scale):
     side = upper.shape[2]
     rows, cols = tile.shape[1], tile.shape[2]
-    ext[:, :rows, :cols] = tile[...]
-    ext[:, :side, cols:] = upper[...]
-    ext[:, side:rows, cols:] = lower[...]
-    ext[:, rows:, :cols] = bottom[...]
-    ext[:, rows:, cols:] = corner[...]
-    grad[...] = jnp.zeros_like(grad)
-    probe_out[...] = jnp.zeros_like(probe_out)
-
-    def step(number, carry):
-        one_patch(off[number, 0], off[number, 1], amp.at[number], probe.at[number], left_table, right_table,
-                  ext, grad, probe_out, *scratch)
-        return carry
-
-    lax.fori_loop(0, amp.shape[0], step, 0)
-    main_out[...] = grad[:, :rows, :cols]
-    upper_out[...] = grad[:, :side, cols:]
-    lower_out[...] = grad[:, side:rows, cols:]
-    bottom_out[...] = grad[:, rows:, :cols]
-    corner_out[...] = grad[:, rows:, cols:]
-
-
-def all_patches(off, tile, upper, lower, bottom, corner, probe, amp):
-    side = upper.shape[2]
+    cut = rows - lower.shape[1]
+    number = pl.program_id(0)
+
+    @pl.when(number == 0)
+    def opening():
+        ext[:, :rows, :cols] = tile[...]
+        ext[:, :side, cols:] = upper[...]
+        ext[:, side:cut, cols:] = middle[...]
+        ext[:, cut:rows, cols:] = lower[...]
+        ext[:, rows:, :cols] = bottom[...]
+        ext[:, rows:, cols:] = corner[...]
+        grad[...] = jnp.zeros_like(grad)
+        probe_out[...] = jnp.zeros_like(probe_out)
+
+    one_patch(off[number, 0], off[number, 1], amp.at[0], probe.at[0], left_table, right_table,
+              ext, grad, probe_out, *scratch)
+
+    @pl.when(number == pl.num_programs(0) - 1)
+    def closing():
+        main_out[...] = grad[:, :rows, :cols]
+        upper_out[...] = grad[:, :side, cols:]
+        lower_out[...] = grad[:, side:rows, cols:]
+        bottom_out[...] = grad[:, rows:, :cols]
+        corner_out[...] = grad[:, rows:, cols:]
+        probe_out[...] *= scale
+
+
+def all_patches(off, tile, upper, middle, lower, bottom, corner, probe, amp, scale):
+    count, side = amp.shape[0], upper.shape[2]
     rows, cols = tile.shape[1], tile.shape[2]
     table = half_tables(side)
     tables = [jnp.asarray(split_table(table)), jnp.asarray(split_table(table.transpose(0, 2, 1)))]
@@ -260,15 +267,18 @@
     vmem = pl.BlockSpec(memory_space=pltpu.VMEM)
     shape = lambda *dims: jax.ShapeDtypeStruct(dims, F32)
     return pl.pallas_call(
-        patches_kernel,
+        functools.partial(patches_kernel, scale=scale),
+        grid=(count,),
         out_shape=(shape(2, rows, cols), shape(2, side, side), shape(2, rows - side, side), shape(2, side, cols),
                    shape(2, side, side), shape(2, side, side)),
-        in_specs=[pl.BlockSpec(memory_space=pltpu.SMEM)] + [vmem] * 9,
+        in_specs=[pl.BlockSpec(memory_space=pltpu.SMEM)] + [vmem] * 6
+                 + [pl.BlockSpec((1, 2, side, side), lambda i: (i, 0, 0, 0)),
+                    pl.BlockSpec((1, 2, side, side // 2), lambda i: (i, 0, 0, 0))] + [vmem] * 2,
         out_specs=[vmem] * 6,
         scratch_shapes=[pltpu.VMEM((2, rows + side, cols + side), F32)] * 2
                      + [pltpu.VMEM((2, side, side), F32)] + [pltpu.VMEM((2, side, side), BF16)] * 4,
-        compiler_params=pltpu.CompilerParams(vmem_limit_bytes=36 * 1024 * 1024),
-    )(off, tile, upper, lower, bottom, corner, probes, amps, *tables)
+        compiler_params=pltpu.CompilerParams(vmem_limit_bytes=50 * 1024 * 1024),
+    )(off, tile, upper, middle, lower, bottom, corner, probes, amps, *tables)
 
 
 ACROSS, LINES = (2, 4, 6), (4, 8, 12)
@@ -303,34 +313,75 @@
     return whole
 
 
+def halved(value, distance, axis):
+    rows = value.shape[0] // 2
+    upper = (lax.axis_index(axis) & distance) != 0
+    low, high = value[:rows], value[rows:]
+    got, = exchanged([jnp.where(upper, low, high)], (distance,), axis)
+    return jnp.where(upper, high, low) + got
+
+
+def doubled(value, distance, axis):
+    upper = (lax.axis_index(axis) & distance) != 0
+    got, = exchanged([value], (distance,), axis)
+    return jnp.concatenate([jnp.where(upper, got, value), jnp.where(upper, value, got)], axis=0)
+
+
+def round_ring(value, step):
+    size = lax.axis_size("col")
+    return lax.ppermute(value, "col", [(i, i // 4 * 4 + (i + step) % 4) for i in range(size)])
+
+
+def ring_sum(value):
+    held = [value]
+    for _ in range(3):
+        held.append(round_ring(held[-1], -1))
+    return (held[0] + held[2]) + (held[1] + held[3])
+
+
 def summed_everywhere(value):
     shape = value.shape
     value = value.reshape(-1, shape[-1])
     chip = (lax.axis_index("row") >> 1) & 3
-    line = lax.axis_index("col") >> 2
+    value = halved(value, 1, "row")
     value = scattered(value, chip, ACROSS, "row")
-    value = scattered(value, line, LINES, "col")
-    value = everywhere(value, (1, 8, 9), "row")
-    value = everywhere(value, (1, 2, 3), "col")
-    value = gathered(value, line, LINES, "col")
+    value = everywhere(value, LINES, "col")
+    value = value + exchanged([value], (8,), "row")[0]
+    value = ring_sum(value)
     value = gathered(value, chip, ACROSS, "row")
+    value = doubled(value, 1, "row")
     return value.reshape(shape)
+
+
+def long_way(value):
+    value = round_ring(value, 1)
+    value = round_ring(value, 1)
+    pairs = []
+    for source in range(lax.axis_size("col")):
+        line, place = source // 4, source % 4
+        if place != 2:
+            pairs.append((source, line * 4 + (place + 1) % 4))
+        elif line > 0:
+            pairs.append((source, line * 4 - 1))
+    return lax.ppermute(value, "col", pairs)
 
 
 def shards_body(object_field, probe, amplitude, offsets):
     side = probe.shape[1]
+    cut = object_field.shape[1] - side // 2
+    lower = long_way(object_field[:, cut:, :side])
     upper = passed_along(object_field[:, :side, :side], "col", -1)
-    lower = passed_along(object_field[:, side:, :side], "col", -1)
+    middle = passed_along(object_field[:, side:cut, :side], "col", -1)
     bottom = passed_along(object_field[:, :side, :], "row", -1)
     corner = passed_along(upper, "row", -1)
+    count = amplitude.shape[2] * lax.axis_size("row") * lax.axis_size("col")
     main, upper, lower, bottom, corner, probe_acc = all_patches(
-        offsets[0, 0], object_field, upper, lower, bottom, corner, probe, amplitude[0, 0])
+        offsets[0, 0], object_field, upper, middle, lower, bottom, corner, probe, amplitude[0, 0], 1.0 / count)
     corner_back = passed_along(corner, "row", 1)
     lower_back = passed_along(lower, "col", 1)
     bottom_back = passed_along(bottom, "row", 1)
     upper_back = passed_along(upper + corner_back, "col", 1)
-    count = amplitude.shape[2] * lax.axis_size("row") * lax.axis_size("col")
-    probe_total = summed_everywhere(probe_acc) / count
+    probe_total = summed_everywhere(probe_acc)
     right_back = jnp.concatenate([upper_back, lower_back], axis=1)
     main = main.at[:, :side, :].add(bottom_back)
     object_grad = main.at[:, :, :side].add(right_back)

time: 202 us -> 203 us (level)
  the two profiles are of different devices: /device:TPU:31 before, /device:TPU:8 now
where the time goes in v4:
time: 203 us
  waiting for transfers between devices  98.9 us (49%)
  starting transfers between devices  66.9 us (33%)
  Pallas kernels  27.9 us (14%)
  local copies, waits for them, and re-layouts  6.33 us (3%)
    ppermute x8, waiting for transfers between devices, passed_along(): lax.ppermute(value, axis, [(source, source + steps) for source in range(f...  52.1 us
    ppermute x12, starting transfers between devices, exchanged(): lax.ppermute(piece, axis, [(i, i ^ distance) for i in range(lax.axis_size...  30.3 us
    ppermute x8, starting transfers between devices, passed_along(): lax.ppermute(value, axis, [(source, source + steps) for source in range(f...  27.4 us
    ppermute x5, waiting for transfers between devices, round_ring(): lax.ppermute(value, 'col', [(i, i // 4 * 4 + (i + step) % 4) for i in ran...  20.4 us
    pallas_call x1, Pallas kernels, all_patches(): pl.pallas_call(functools.partial(patches_kernel, scale=scale), grid=(coun...  19.7 us
    ppermute x12, waiting for transfers between devices, exchanged(): lax.ppermute(piece, axis, [(i, i ^ distance) for i in range(lax.axis_size...  19.1 us
    pallas_call x1, Pallas kernels, prepare(): pl.pallas_call(prepare_kernel, grid=(count,), out_shape=(jax.ShapeDtypeSt...  8.19 us
    ppermute x1, waiting for transfers between devices, long_way(): return lax.ppermute(value, 'col', pairs)  7.35 us
  transfers between devices with their start and end apart: 26, of which 17 were waited for; matrix products, arithmetic and copies ran while one was open for 2% of the time, Pallas kernels for 4%

profile of v4, /device:TPU:8, one launch (start us, length us, event | category | flops | bytes accessed | tf_op | source)
XLA Modules:
  0.0 202.6 jit_solution(11486253102796280772)
XLA Ops:
  1.7 8.1 %collective-permute-start = (f32[2,256,256]{2,1,0:T(8,128)S(1)}, f32[2,256,256]{2,1,0:T(8,128)S(1)}, u32[]{:S(2)}, u32[]{:S(2)}) collective-permute-start(f32[2,256,256]{2,1,0:T(8,128)S(1)} %slice.68), channel_id=1, source_target_pairs={{1,0},{2,1},{3,2},{4,3},{5,4},{6,5},{7,6},{8,7},{9,8},{10,9},{11,1... | collective-permute-start | bytes 1572872 | tf_op jit(solution)/shard_map/ppermute | solution.py:20
  13.6 11.5 %collective-permute-done.2 = f32[2,128,256]{2,1,0:T(8,128)S(1)} collective-permute-done((f32[2,128,256]{2,1,0:T(8,128)S(1)}, f32[2,128,256]{2,1,0:T(8,128)S(1)}, u32[]{:S(2)}, u32[]{:S(2)}) %collective-permute-start.2) | collective-permute-done | bytes 262176 | tf_op jit(solution)/shard_map/ppermute | solution.py:332
  25.2 7.1 %collective-permute-done.upper = f32[2,256,256]{2,1,0:T(8,128)S(1)} collective-permute-done((f32[2,256,256]{2,1,0:T(8,128)S(1)}, f32[2,256,256]{2,1,0:T(8,128)S(1)}, u32[]{:S(2)}, u32[]{:S(2)}) %collective-permute-start) | collective-permute-done | bytes 524320 | tf_op jit(solution)/shard_map/ppermute | solution.py:20
  33.6 7.5 %collective-permute-start.1 = (f32[2,128,256]{2,1,0:T(8,128)S(1)}, f32[2,128,256]{2,1,0:T(8,128)S(1)}, u32[]{:S(2)}, u32[]{:S(2)}) collective-permute-start(f32[2,128,256]{2,1,0:T(8,128)S(1)} %get-tuple-element.45), channel_id=1, source_target_pairs={{1,0},{2,1},{3,2},{4,3},{5,4},{6,5},{7,6},{8,7},{9,8},{10,9},{11,1... | collective-permute-start | bytes 786440 | tf_op jit(solution)/shard_map/ppermute | solution.py:20
  41.0 1.9 collective-permute-start.4
  43.7 8.2 %shard_map.86 = (f32[8,2,256,128]{3,2,1,0:T(8,128)}, f32[8,2,256,256]{3,2,1,0:T(8,128)}) custom-call(s32[8,2]{1,0:T(8,128)} %copy.10.off, f32[8,256,256]{2,1,0:T(8,128)} %bitcast.7, f32[2,256,256]{2,1,0:T(8,128)} %probe.1, bf16[2,256,256]{2,1,0:T(8,128)(2,1)} %constant.78.clone.pick), custom_call_target="tpu_custom_call" | custom-call | tf_op jit(solution)/shard_map/pallas_call | solution.py:96
  51.9 7.4 %collective-permute-done.4.lower = f32[2,128,256]{2,1,0:T(8,128)S(1)} collective-permute-done((f32[2,128,256]{2,1,0:T(8,128)S(1)}, f32[2,128,256]{2,1,0:T(8,128)S(1)}, u32[]{:S(2)}, u32[]{:S(2)}) %collective-permute-start.4) | collective-permute-done | bytes 262176 | tf_op jit(solution)/shard_map/ppermute | solution.py:366
  59.2 19.7 %shard_map.87 = (f32[2,512,512]{2,1,0:T(8,128)}, f32[2,256,256]{2,1,0:T(8,128)S(1)}, f32[2,256,256]{2,1,0:T(8,128)S(1)}, f32[2,256,512]{2,1,0:T(8,128)}, f32[2,2...) custom-call(s32[8,2]{1,0:T(8,128)S(1)} %copy-done, f32[2,512,512]{2,1,0:T(8,128)} %tile.1, ...), custom_call_target="tpu_custom_call" | custom-call | tf_op jit(solution)/shard_map/pallas_call | solution.py:269
  82.0 3.1 %collective-permute-start.13 = (f32[64,256]{1,0:T(8,128)S(1)}, f32[64,256]{1,0:T(8,128)S(1)}, u32[]{:S(2)}, u32[]{:S(2)}) collective-permute-start(f32[64,256]{1,0:T(8,128)S(1)} %get-tuple-element.50), channel_id=1, source_target_pairs={{0,64},{16,80},{32,96},{48,112},{64,0},{80,16},{96,32},{112,48},{1... | collective-permute-start | bytes 196616 | tf_op jit(solution)/shard_map/ppermute | solution.py:288
  86.3 2.2 %collective-permute-done.13 = f32[64,256]{1,0:T(8,128)S(1)} collective-permute-done((f32[64,256]{1,0:T(8,128)S(1)}, f32[64,256]{1,0:T(8,128)S(1)}, u32[]{:S(2)}, u32[]{:S(2)}) %collective-permute-start.13) | collective-permute-done | bytes 65568 | tf_op jit(solution)/shard_map/ppermute | solution.py:288
  88.6 2.0 collective-permute-done.14
  90.6 4.1 %collective-permute-start.16 = (f32[64,256]{1,0:T(8,128)S(1)}, f32[64,256]{1,0:T(8,128)S(1)}, u32[]{:S(2)}, u32[]{:S(2)}) collective-permute-start(f32[64,256]{1,0:T(8,128)S(1)} %add_add_fusion.2), channel_id=1, source_target_pairs={{0,8},{1,9},{2,10},{3,11},{4,12},{5,13},{6,14},{7,15},{8,0},{9,1},... | collective-permute-start | bytes 196616 | tf_op jit(solution)/shard_map/ppermute | solution.py:288
  95.0 2.7 %collective-permute-done.16 = f32[64,256]{1,0:T(8,128)S(1)} collective-permute-done((f32[64,256]{1,0:T(8,128)S(1)}, f32[64,256]{1,0:T(8,128)S(1)}, u32[]{:S(2)}, u32[]{:S(2)}) %collective-permute-start.16) | collective-permute-done | bytes 65568 | tf_op jit(solution)/shard_map/ppermute | solution.py:288
  97.7 1.3 collective-permute-done.17
  99.8 4.3 %collective-permute-done.18 = f32[64,256]{1,0:T(8,128)S(1)} collective-permute-done((f32[64,256]{1,0:T(8,128)S(1)}, f32[64,256]{1,0:T(8,128)S(1)}, u32[]{:S(2)}, u32[]{:S(2)}) %collective-permute-start.18) | collective-permute-done | bytes 65568 | tf_op jit(solution)/shard_map/ppermute | solution.py:288
  104.1 1.7 collective-permute-start.19
  105.8 3.6 %collective-permute-done.19 = f32[64,256]{1,0:T(8,128)S(1)} collective-permute-done((f32[64,256]{1,0:T(8,128)S(1)}, f32[64,256]{1,0:T(8,128)S(1)}, u32[]{:S(2)}, u32[]{:S(2)}) %collective-permute-start.19) | collective-permute-done | bytes 65568 | tf_op jit(solution)/shard_map/ppermute | solution.py:332
  109.4 2.7 %collective-permute-start.20 = (f32[64,256]{1,0:T(8,128)S(1)}, f32[64,256]{1,0:T(8,128)S(1)}, u32[]{:S(2)}, u32[]{:S(2)}) collective-permute-start(f32[64,256]{1,0:T(8,128)S(1)} %collective-permute-done.19), channel_id=1, source_target_pairs={{0,3},{1,0},{2,1},{3,2},{4,7},{5,4},{6,5},{7,6},{8,11},{9,8},{10,9... | collective-permute-start | bytes 196616 | tf_op jit(solution)/shard_map/ppermute | solution.py:332
  112.2 3.6 %collective-permute-done.20 = f32[64,256]{1,0:T(8,128)S(1)} collective-permute-done((f32[64,256]{1,0:T(8,128)S(1)}, f32[64,256]{1,0:T(8,128)S(1)}, u32[]{:S(2)}, u32[]{:S(2)}) %collective-permute-start.20) | collective-permute-done | bytes 65568 | tf_op jit(solution)/shard_map/ppermute | solution.py:332
  115.8 2.7 %collective-permute-start.21 = (f32[64,256]{1,0:T(8,128)S(1)}, f32[64,256]{1,0:T(8,128)S(1)}, u32[]{:S(2)}, u32[]{:S(2)}) collective-permute-start(f32[64,256]{1,0:T(8,128)S(1)} %collective-permute-done.20), channel_id=1, source_target_pairs={{0,3},{1,0},{2,1},{3,2},{4,7},{5,4},{6,5},{7,6},{8,11},{9,8},{10,9... | collective-permute-start | bytes 196616 | tf_op jit(solution)/shard_map/ppermute | solution.py:332
  118.5 1.5 collective-permute-start.7
  120.1 1.6 collective-permute-done.21
  121.9 1.7 collective-permute-start.8
  123.6 7.0 %collective-permute-start.23 = (f32[64,256]{1,0:T(8,128)S(1)}, f32[64,256]{1,0:T(8,128)S(1)}, u32[]{:S(2)}, u32[]{:S(2)}) collective-permute-start(f32[64,256]{1,0:T(8,128)S(1)} %get-tuple-element.43), channel_id=1, source_target_pairs={{0,64},{16,80},{32,96},{48,112},{64,0},{80,16},{96,32},{112,48},{1... | collective-permute-start | bytes 196616 | tf_op jit(solution)/shard_map/ppermute | solution.py:288
  130.8 2.7 %collective-permute-done.23 = f32[64,256]{1,0:T(8,128)S(1)} collective-permute-done((f32[64,256]{1,0:T(8,128)S(1)}, f32[64,256]{1,0:T(8,128)S(1)}, u32[]{:S(2)}, u32[]{:S(2)}) %collective-permute-start.23) | collective-permute-done | bytes 65568 | tf_op jit(solution)/shard_map/ppermute | solution.py:288
  133.6 2.5 %collective-permute-done.24 = f32[64,256]{1,0:T(8,128)S(1)} collective-permute-done((f32[64,256]{1,0:T(8,128)S(1)}, f32[64,256]{1,0:T(8,128)S(1)}, u32[]{:S(2)}, u32[]{:S(2)}) %collective-permute-start.24) | collective-permute-done | bytes 65568 | tf_op jit(solution)/shard_map/ppermute | solution.py:288
  136.1 12.7 %collective-permute-start.25 = (f32[256,256]{1,0:T(8,128)S(1)}, f32[256,256]{1,0:T(8,128)S(1)}, u32[]{:S(2)}, u32[]{:S(2)}) collective-permute-start(f32[256,256]{1,0:T(8,128)S(1)} %constant_dynamic-update-slice_fusion), channel_id=1, source_target_pairs={{0,16},{16,0},{32,48},{48,32},{64,80},{80,64},{96,112},{112,96},{1... | collective-permute-start | bytes 786440 | tf_op jit(solution)/shard_map/ppermute | solution.py:288
  148.7 1.9 collective-permute-start.10
  150.8 4.1 %collective-permute-start.9 = (f32[2,256,256]{2,1,0:T(8,128)S(1)}, f32[2,256,256]{2,1,0:T(8,128)S(1)}, u32[]{:S(2)}, u32[]{:S(2)}) collective-permute-start(f32[2,256,256]{2,1,0:T(8,128)S(1)} %add.67), channel_id=1, source_target_pairs={{0,1},{1,2},{2,3},{3,4},{4,5},{5,6},{6,7},{7,8},{8,9},{9,10},{10,1... | collective-permute-start | bytes 1572872 | tf_op jit(solution)/shard_map/ppermute | solution.py:20
  156.0 27.3 %collective-permute-done.10 = f32[2,256,256]{2,1,0:T(8,128)S(1)} collective-permute-done((f32[2,256,256]{2,1,0:T(8,128)S(1)}, f32[2,256,256]{2,1,0:T(8,128)S(1)}, u32[]{:S(2)}, u32[]{:S(2)}) %collective-permute-start.10) | collective-permute-done | bytes 524320 | tf_op jit(solution)/shard_map/ppermute | solution.py:20
  183.3 17.7 %collective-permute-done.9 = f32[2,256,256]{2,1,0:T(8,128)S(1)} collective-permute-done((f32[2,256,256]{2,1,0:T(8,128)S(1)}, f32[2,256,256]{2,1,0:T(8,128)S(1)}, u32[]{:S(2)}, u32[]{:S(2)}) %collective-permute-start.9) | collective-permute-done | bytes 524320 | tf_op jit(solution)/shard_map/ppermute | solution.py:20
  201.3 1.3 copy-done.4
  (54 shorter events, 14.1 us)
Async XLA Ops:
  0.6 42.3 %copy-start.5 = (s32[1,1,8,2]{2,3,1,0:T(2,128)S(1)}, s32[1,1,8,2]{2,3,1,0:T(2,128)}, u32[]{:S(2)}) copy-start(s32[1,1,8,2]{2,3,1,0:T(2,128)} %param.14) | copy-start | bytes 196
  1.7 30.5 %collective-permute-start = (f32[2,256,256]{2,1,0:T(8,128)S(1)}, f32[2,256,256]{2,1,0:T(8,128)S(1)}, u32[]{:S(2)}, u32[]{:S(2)}) collective-permute-start(f32[2,256,256]{2,1,0:T(8,128)S(1)} %slice.68), channel_id=1, source_target_pairs={{1,0},{2,1},{3,2},{4,3},{5,4},{6,5},{7,6},{8,7},{9,8},{10,9},{11,1... | collective-permute-start | bytes 1572872 | tf_op jit(solution)/shard_map/ppermute | solution.py:20
  11.1 48.1 %collective-permute-start.5 = (f32[2,256,512]{2,1,0:T(8,128)S(1)}, f32[2,256,512]{2,1,0:T(8,128)}, u32[]{:S(2)}, u32[]{:S(2)}) collective-permute-start(f32[2,256,512]{2,1,0:T(8,128)S(1)} %slice.71), channel_id=1, source_target_pairs={{16,0},{32,16},{48,32},{64,48},{80,64},{96,80},{112,96},{128,112},... | collective-permute-start | bytes 3145736 | tf_op jit(solution)/shard_map/ppermute | solution.py:20
  13.5 11.6 %collective-permute-start.2 = (f32[2,128,256]{2,1,0:T(8,128)S(1)}, f32[2,128,256]{2,1,0:T(8,128)S(1)}, u32[]{:S(2)}, u32[]{:S(2)}) collective-permute-start(f32[2,128,256]{2,1,0:T(8,128)S(1)} %get-tuple-element.44), channel_id=1, source_target_pairs={{0,1},{1,2},{2,3},{3,0},{4,5},{5,6},{6,7},{7,4},{8,9},{9,10},{10,1... | collective-permute-start | bytes 786440 | tf_op jit(solution)/shard_map/ppermute | solution.py:332
  25.2 15.9 %collective-permute-start.3 = (f32[2,128,256]{2,1,0:T(8,128)S(1)}, f32[2,128,256]{2,1,0:T(8,128)S(1)}, u32[]{:S(2)}, u32[]{:S(2)}) collective-permute-start(f32[2,128,256]{2,1,0:T(8,128)S(1)} %collective-permute-done.2), channel_id=1, source_target_pairs={{0,1},{1,2},{2,3},{3,0},{4,5},{5,6},{6,7},{7,4},{8,9},{9,10},{10,1... | collective-permute-start | bytes 786440 | tf_op jit(solution)/shard_map/ppermute | solution.py:332
  32.3 26.9 %collective-permute-start.6 = (f32[2,256,256]{2,1,0:T(8,128)S(1)}, f32[2,256,256]{2,1,0:T(8,128)S(1)}, u32[]{:S(2)}, u32[]{:S(2)}) collective-permute-start(f32[2,256,256]{2,1,0:T(8,128)S(1)} %collective-permute-done.upper), channel_id=1, source_target_pairs={{16,0},{32,16},{48,32},{64,48},{80,64},{96,80},{112,96},{128,112},... | collective-permute-start | bytes 1572872 | tf_op jit(solution)/shard_map/ppermute | solution.py:20
  33.6 18.3 %collective-permute-start.1 = (f32[2,128,256]{2,1,0:T(8,128)S(1)}, f32[2,128,256]{2,1,0:T(8,128)S(1)}, u32[]{:S(2)}, u32[]{:S(2)}) collective-permute-start(f32[2,128,256]{2,1,0:T(8,128)S(1)} %get-tuple-element.45), channel_id=1, source_target_pairs={{1,0},{2,1},{3,2},{4,3},{5,4},{6,5},{7,6},{8,7},{9,8},{10,9},{11,1... | collective-permute-start | bytes 786440 | tf_op jit(solution)/shard_map/ppermute | solution.py:20
  41.0 18.2 %collective-permute-start.4 = (f32[2,128,256]{2,1,0:T(8,128)S(1)}, f32[2,128,256]{2,1,0:T(8,128)S(1)}, u32[]{:S(2)}, u32[]{:S(2)}) collective-permute-start(f32[2,128,256]{2,1,0:T(8,128)S(1)} %collective-permute-done.3), channel_id=1, source_target_pairs={{0,1},{1,2},{3,0},{4,5},{5,6},{6,3},{7,4},{8,9},{9,10},{10,7},{11,... | collective-permute-start | bytes 786440 | tf_op jit(solution)/shard_map/ppermute | solution.py:366
  43.7 15.6 %copy-start = (s32[8,2]{1,0:T(8,128)S(1)}, s32[8,2]{1,0:T(8,128)}, u32[]{:S(2)}) copy-start(s32[8,2]{1,0:T(8,128)} %copy.10.off) | copy-start | bytes 196
  78.9 0.8 copy-start.1
  79.7 42.1 %copy-start.2 = (f32[2,256,256]{2,1,0:T(8,128)S(1)}, f32[2,256,256]{2,1,0:T(8,128)}, u32[]{:S(2)}) copy-start(f32[2,256,256]{2,1,0:T(8,128)} %copy-done.1) | copy-start | bytes 1572868
  79.8 1.6 collective-permute-start.11
  81.5 4.9 %collective-permute-start.12 = (f32[64,256]{1,0:T(8,128)S(1)}, f32[64,256]{1,0:T(8,128)S(1)}, u32[]{:S(2)}, u32[]{:S(2)}) collective-permute-start(f32[64,256]{1,0:T(8,128)S(1)} %get-tuple-element.48), channel_id=1, source_target_pairs={{0,32},{16,48},{32,0},{48,16},{64,96},{80,112},{96,64},{112,80},{1... | collective-permute-start | bytes 196616 | tf_op jit(solution)/shard_map/ppermute | solution.py:288
  82.0 6.6 %collective-permute-start.13 = (f32[64,256]{1,0:T(8,128)S(1)}, f32[64,256]{1,0:T(8,128)S(1)}, u32[]{:S(2)}, u32[]{:S(2)}) collective-permute-start(f32[64,256]{1,0:T(8,128)S(1)} %get-tuple-element.50), channel_id=1, source_target_pairs={{0,64},{16,80},{32,96},{48,112},{64,0},{80,16},{96,32},{112,48},{1... | collective-permute-start | bytes 196616 | tf_op jit(solution)/shard_map/ppermute | solution.py:288
  85.0 5.5 %collective-permute-start.14 = (f32[64,256]{1,0:T(8,128)S(1)}, f32[64,256]{1,0:T(8,128)S(1)}, u32[]{:S(2)}, u32[]{:S(2)}) collective-permute-start(f32[64,256]{1,0:T(8,128)S(1)} %get-tuple-element.49), channel_id=1, source_target_pairs={{0,96},{16,112},{32,64},{48,80},{64,32},{80,48},{96,0},{112,16},{1... | collective-permute-start | bytes 196616 | tf_op jit(solution)/shard_map/ppermute | solution.py:288
  90.5 4.4 %collective-permute-start.15 = (f32[64,256]{1,0:T(8,128)S(1)}, f32[64,256]{1,0:T(8,128)S(1)}, u32[]{:S(2)}, u32[]{:S(2)}) collective-permute-start(f32[64,256]{1,0:T(8,128)S(1)} %add_add_fusion.2), channel_id=1, source_target_pairs={{0,4},{1,5},{2,6},{3,7},{4,0},{5,1},{6,2},{7,3},{8,12},{9,13},{10,... | collective-permute-start | bytes 196616 | tf_op jit(solution)/shard_map/ppermute | solution.py:288
  90.6 7.0 %collective-permute-start.16 = (f32[64,256]{1,0:T(8,128)S(1)}, f32[64,256]{1,0:T(8,128)S(1)}, u32[]{:S(2)}, u32[]{:S(2)}) collective-permute-start(f32[64,256]{1,0:T(8,128)S(1)} %add_add_fusion.2), channel_id=1, source_target_pairs={{0,8},{1,9},{2,10},{3,11},{4,12},{5,13},{6,14},{7,15},{8,0},{9,1},... | collective-permute-start | bytes 196616 | tf_op jit(solution)/shard_map/ppermute | solution.py:288
  94.8 4.3 %collective-permute-start.17 = (f32[64,256]{1,0:T(8,128)S(1)}, f32[64,256]{1,0:T(8,128)S(1)}, u32[]{:S(2)}, u32[]{:S(2)}) collective-permute-start(f32[64,256]{1,0:T(8,128)S(1)} %add_add_fusion.2), channel_id=1, source_target_pairs={{0,12},{1,13},{2,14},{3,15},{4,8},{5,9},{6,10},{7,11},{8,4},{9,5},... | collective-permute-start | bytes 196616 | tf_op jit(solution)/shard_map/ppermute | solution.py:288
  99.0 5.1 %collective-permute-start.18 = (f32[64,256]{1,0:T(8,128)S(1)}, f32[64,256]{1,0:T(8,128)S(1)}, u32[]{:S(2)}, u32[]{:S(2)}) collective-permute-start(f32[64,256]{1,0:T(8,128)S(1)} %add_add_fusion.1), channel_id=1, source_target_pairs={{0,128},{16,144},{32,160},{48,176},{64,192},{80,208},{96,224},{112... | collective-permute-start | bytes 196616 | tf_op jit(solution)/shard_map/ppermute | solution.py:288
  104.1 5.3 %collective-permute-start.19 = (f32[64,256]{1,0:T(8,128)S(1)}, f32[64,256]{1,0:T(8,128)S(1)}, u32[]{:S(2)}, u32[]{:S(2)}) collective-permute-start(f32[64,256]{1,0:T(8,128)S(1)} %add.80), channel_id=1, source_target_pairs={{0,3},{1,0},{2,1},{3,2},{4,7},{5,4},{6,5},{7,6},{8,11},{9,8},{10,9... | collective-permute-start | bytes 196616 | tf_op jit(solution)/shard_map/ppermute | solution.py:332
  109.4 6.4 %collective-permute-start.20 = (f32[64,256]{1,0:T(8,128)S(1)}, f32[64,256]{1,0:T(8,128)S(1)}, u32[]{:S(2)}, u32[]{:S(2)}) collective-permute-start(f32[64,256]{1,0:T(8,128)S(1)} %collective-permute-done.19), channel_id=1, source_target_pairs={{0,3},{1,0},{2,1},{3,2},{4,7},{5,4},{6,5},{7,6},{8,11},{9,8},{10,9... | collective-permute-start | bytes 196616 | tf_op jit(solution)/shard_map/ppermute | solution.py:332
  115.8 5.9 %collective-permute-start.21 = (f32[64,256]{1,0:T(8,128)S(1)}, f32[64,256]{1,0:T(8,128)S(1)}, u32[]{:S(2)}, u32[]{:S(2)}) collective-permute-start(f32[64,256]{1,0:T(8,128)S(1)} %collective-permute-done.20), channel_id=1, source_target_pairs={{0,3},{1,0},{2,1},{3,2},{4,7},{5,4},{6,5},{7,6},{8,11},{9,8},{10,9... | collective-permute-start | bytes 196616 | tf_op jit(solution)/shard_map/ppermute | solution.py:332
  118.5 37.2 %collective-permute-start.7 = (f32[2,256,512]{2,1,0:T(8,128)}, f32[2,256,512]{2,1,0:T(8,128)S(1)}, u32[]{:S(2)}, u32[]{:S(2)}) collective-permute-start(f32[2,256,512]{2,1,0:T(8,128)} %get-tuple-element.37), channel_id=1, source_target_pairs={{0,16},{16,32},{32,48},{48,64},{64,80},{80,96},{96,112},{112,128},... | collective-permute-start | bytes 3145736 | tf_op jit(solution)/shard_map/ppermute | solution.py:20
  121.7 34.0 %copy-start.3 = (f32[2,512,512]{2,1,0:T(8,128)S(1)}, f32[2,512,512]{2,1,0:T(8,128)}, u32[]{:S(2)}) copy-start(f32[2,512,512]{2,1,0:T(8,128)} %get-tuple-element.36) | copy-start | bytes 6291460
  121.7 9.1 %collective-permute-start.22 = (f32[64,256]{1,0:T(8,128)S(1)}, f32[64,256]{1,0:T(8,128)S(1)}, u32[]{:S(2)}, u32[]{:S(2)}) collective-permute-start(f32[64,256]{1,0:T(8,128)S(1)} %get-tuple-element.43), channel_id=1, source_target_pairs={{0,32},{16,48},{32,0},{48,16},{64,96},{80,112},{96,64},{112,80},{1... | collective-permute-start | bytes 196616 | tf_op jit(solution)/shard_map/ppermute | solution.py:288
  121.9 28.8 %collective-permute-start.8 = (f32[2,256,256]{2,1,0:T(8,128)S(1)}, f32[2,256,256]{2,1,0:T(8,128)S(1)}, u32[]{:S(2)}, u32[]{:S(2)}) collective-permute-start(f32[2,256,256]{2,1,0:T(8,128)S(1)} %copy-done.2), channel_id=1, source_target_pairs={{0,16},{16,32},{32,48},{48,64},{64,80},{80,96},{96,112},{112,128},... | collective-permute-start | bytes 1572872 | tf_op jit(solution)/shard_map/ppermute | solution.py:20
  123.6 10.0 %collective-permute-start.23 = (f32[64,256]{1,0:T(8,128)S(1)}, f32[64,256]{1,0:T(8,128)S(1)}, u32[]{:S(2)}, u32[]{:S(2)}) collective-permute-start(f32[64,256]{1,0:T(8,128)S(1)} %get-tuple-element.43), channel_id=1, source_target_pairs={{0,64},{16,80},{32,96},{48,112},{64,0},{80,16},{96,32},{112,48},{1... | collective-permute-start | bytes 196616 | tf_op jit(solution)/shard_map/ppermute | solution.py:288
  130.6 5.5 %collective-permute-start.24 = (f32[64,256]{1,0:T(8,128)S(1)}, f32[64,256]{1,0:T(8,128)S(1)}, u32[]{:S(2)}, u32[]{:S(2)}) collective-permute-start(f32[64,256]{1,0:T(8,128)S(1)} %get-tuple-element.43), channel_id=1, source_target_pairs={{0,96},{16,112},{32,64},{48,80},{64,32},{80,48},{96,0},{112,16},{1... | collective-permute-start | bytes 196616 | tf_op jit(solution)/shard_map/ppermute | solution.py:288
  136.1 18.8 %collective-permute-start.25 = (f32[256,256]{1,0:T(8,128)S(1)}, f32[256,256]{1,0:T(8,128)S(1)}, u32[]{:S(2)}, u32[]{:S(2)}) collective-permute-start(f32[256,256]{1,0:T(8,128)S(1)} %constant_dynamic-update-slice_fusion), channel_id=1, source_target_pairs={{0,16},{16,0},{32,48},{48,32},{64,80},{80,64},{96,112},{112,96},{1... | collective-permute-start | bytes 786440 | tf_op jit(solution)/shard_map/ppermute | solution.py:288
  148.7 34.6 %collective-permute-start.10 = (f32[2,256,256]{2,1,0:T(8,128)S(1)}, f32[2,256,256]{2,1,0:T(8,128)S(1)}, u32[]{:S(2)}, u32[]{:S(2)}) collective-permute-start(f32[2,256,256]{2,1,0:T(8,128)S(1)} %get-tuple-element.40), channel_id=1, source_target_pairs={{0,1},{1,2},{2,3},{3,4},{4,5},{5,6},{6,7},{7,8},{8,9},{9,10},{10,1... | collective-permute-start | bytes 1572872 | tf_op jit(solution)/shard_map/ppermute | solution.py:20
  150.8 50.2 %collective-permute-start.9 = (f32[2,256,256]{2,1,0:T(8,128)S(1)}, f32[2,256,256]{2,1,0:T(8,128)S(1)}, u32[]{:S(2)}, u32[]{:S(2)}) collective-permute-start(f32[2,256,256]{2,1,0:T(8,128)S(1)} %add.67), channel_id=1, source_target_pairs={{0,1},{1,2},{2,3},{3,4},{4,5},{5,6},{6,7},{7,8},{8,9},{9,10},{10,1... | collective-permute-start | bytes 1572872 | tf_op jit(solution)/shard_map/ppermute | solution.py:20
  201.3 1.3 copy-start.4

commit v5 on v4

--- a/solution.py
+++ b/solution.py
@@ -154,6 +154,8 @@
         put(a_high, a_low, 1, slice(at, at + step), upper_r - lower_r)
         put(a_high, a_low, 1, slice(half + at, half + at + step), upper_i - lower_i)
 
+    yield
+
     def left_product(table, odd):
         fine, rough = table[odd, 1], table[odd, 0]
         return dot(jnp.concatenate([rough, rough, fine], axis=1),
@@ -171,6 +173,7 @@
             rows = slice(odd * half + at, odd * half + at + step)
             put(x_high, x_low, 0, rows, jnp.concatenate([real[:, :half] + real[:, half:], imag[:, :half] + imag[:, half:]], axis=1))
             put(x_high, x_low, 1, rows, jnp.concatenate([real[:, :half] - real[:, half:], imag[:, :half] - imag[:, half:]], axis=1))
+    yield
     for odd in (0, 1):
         far = right_product(right_table, odd)
         for at in range(0, side, step):
@@ -178,6 +181,7 @@
             real, imag = far[rows, :half], far[rows, half:]
             keep = 1.0 - amp[odd, rows] * lax.rsqrt(jnp.maximum(real * real + imag * imag, 0.25))
             put(x_high, x_low, odd, rows, jnp.concatenate([real * keep, imag * keep], axis=1))
+    yield
     even, odd_part = right_product(left_table, 0), right_product(left_table, 1)
     for at in range(0, side, step):
         rows = slice(at, at + step)
@@ -185,6 +189,7 @@
         which, place = at // half, at % half
         put(a_high, a_low, which, slice(place, place + step), jnp.concatenate([total[:, :half], difference[:, :half]], axis=1))
         put(a_high, a_low, which, slice(half + place, half + place + step), jnp.concatenate([total[:, half:], difference[:, half:]], axis=1))
+    yield
     even, odd_part = left_product(right_table, 0), left_product(right_table, 1)
 
     def add(part, offset, term):
@@ -216,6 +221,7 @@
             add(part, at, term)
         view[0, rows] = unrolled(vr * cr + vi * ci, lane, 1)
         view[1, rows] = unrolled(vr * ci - vi * cr, lane, 1)
+    yield
     back = lax.rem(8 - row, 8)
     inside = lax.broadcasted_iota(jnp.int32, (8, side), 0) < 8 - row
     for part in (0, 1):
@@ -225,6 +231,12 @@
             after = opening if at + 8 == side else pltpu.roll(view[part, at + 8:at + 16], back, 0)
             probe_acc[part, at:at + 8] += jnp.where(inside, now, after)
             now = after
+
+
+def interleaved(patches):
+    running = list(patches)
+    while running:
+        running = [patch for patch in running if next(patch, running) is None]
 
 
 def patches_kernel(off, tile, upper, middle, lower, bottom, corner, probe, amp, left_table, right_table,
@@ -245,8 +257,11 @@
         grad[...] = jnp.zeros_like(grad)
         probe_out[...] = jnp.zeros_like(probe_out)
 
-    one_patch(off[number, 0], off[number, 1], amp.at[0], probe.at[0], left_table, right_table,
-              ext, grad, probe_out, *scratch)
+    together = amp.shape[0]
+    interleaved(
+        one_patch(off[number * together + which, 0], off[number * together + which, 1], amp.at[which], probe.at[which],
+                  left_table, right_table, ext, grad, probe_out, *[ref.at[which] for ref in scratch])
+        for which in range(together))
 
     @pl.when(number == pl.num_programs(0) - 1)
     def closing():
@@ -260,6 +275,7 @@
 
 def all_patches(off, tile, upper, middle, lower, bottom, corner, probe, amp, scale):
     count, side = amp.shape[0], upper.shape[2]
+    together = 2 if count % 2 == 0 else 1
     rows, cols = tile.shape[1], tile.shape[2]
     table = half_tables(side)
     tables = [jnp.asarray(split_table(table)), jnp.asarray(split_table(table.transpose(0, 2, 1)))]
@@ -268,15 +284,15 @@
     shape = lambda *dims: jax.ShapeDtypeStruct(dims, F32)
     return pl.pallas_call(
         functools.partial(patches_kernel, scale=scale),
-        grid=(count,),
+        grid=(count // together,),
         out_shape=(shape(2, rows, cols), shape(2, side, side), shape(2, rows - side, side), shape(2, side, cols),
                    shape(2, side, side), shape(2, side, side)),
         in_specs=[pl.BlockSpec(memory_space=pltpu.SMEM)] + [vmem] * 6
-                 + [pl.BlockSpec((1, 2, side, side), lambda i: (i, 0, 0, 0)),
-                    pl.BlockSpec((1, 2, side, side // 2), lambda i: (i, 0, 0, 0))] + [vmem] * 2,
+                 + [pl.BlockSpec((together, 2, side, side), lambda i: (i, 0, 0, 0)),
+                    pl.BlockSpec((together, 2, side, side // 2), lambda i: (i, 0, 0, 0))] + [vmem] * 2,
         out_specs=[vmem] * 6,
         scratch_shapes=[pltpu.VMEM((2, rows + side, cols + side), F32)] * 2
-                     + [pltpu.VMEM((2, side, side), F32)] + [pltpu.VMEM((2, side, side), BF16)] * 4,
+                     + [pltpu.VMEM((together, 2, side, side), F32)] + [pltpu.VMEM((together, 2, side, side), BF16)] * 4,
         compiler_params=pltpu.CompilerParams(vmem_limit_bytes=50 * 1024 * 1024),
     )(off, tile, upper, middle, lower, bottom, corner, probes, amps, *tables)
 
@@ -330,13 +346,6 @@
 def round_ring(value, step):
     size = lax.axis_size("col")
     return lax.ppermute(value, "col", [(i, i // 4 * 4 + (i + step) % 4) for i in range(size)])
-
-
-def ring_sum(value):
-    held = [value]
-    for _ in range(3):
-        held.append(round_ring(held[-1], -1))
-    return (held[0] + held[2]) + (held[1] + held[3])
 
 
 def summed_everywhere(value):
@@ -347,7 +356,7 @@
     value = scattered(value, chip, ACROSS, "row")
     value = everywhere(value, LINES, "col")
     value = value + exchanged([value], (8,), "row")[0]
-    value = ring_sum(value)
+    value = everywhere(value, (1, 2, 3), "col")
     value = gathered(value, chip, ACROSS, "row")
     value = doubled(value, 1, "row")
     return value.reshape(shape)

time: 203 us -> 187 us (0.921)
  the two profiles are of different devices: /device:TPU:8 before, /device:TPU:49 now
where the time goes in v5:
time: 187 us; the launch traced here: 186 us
  waiting for transfers between devices  87.3 us (47%)
  starting transfers between devices  66.2 us (35%)
  Pallas kernels  23.8 us (13%)
  local copies, waits for them, and re-layouts  6.33 us (3%)
    ppermute x8, waiting for transfers between devices, passed_along(): lax.ppermute(value, axis, [(source, source + steps) for source in range(f...  44.3 us
    ppermute x8, starting transfers between devices, passed_along(): lax.ppermute(value, axis, [(source, source + steps) for source in range(f...  39.9 us
    ppermute x15, starting transfers between devices, exchanged(): lax.ppermute(piece, axis, [(i, i ^ distance) for i in range(lax.axis_size...  23 us
    ppermute x15, waiting for transfers between devices, exchanged(): lax.ppermute(piece, axis, [(i, i ^ distance) for i in range(lax.axis_size...  22.8 us
    ppermute x2, waiting for transfers between devices, round_ring(): lax.ppermute(value, 'col', [(i, i // 4 * 4 + (i + step) % 4) for i in ran...  17.9 us
    pallas_call x1, Pallas kernels, all_patches(): pl.pallas_call(functools.partial(patches_kernel, scale=scale), grid=(coun...  15.6 us
    pallas_call x1, Pallas kernels, prepare(): pl.pallas_call(prepare_kernel, grid=(count,), out_shape=(jax.ShapeDtypeSt...  8.19 us
  transfers between devices with their start and end apart: 26, of which 14 were waited for; matrix products, arithmetic and copies ran while one was open for 2% of the time, Pallas kernels for 4%

profile of v5, /device:TPU:49, one launch (start us, length us, event | category | flops | bytes accessed | tf_op | source)
XLA Modules:
  0.0 186.2 jit_solution(13328641653367513308)
XLA Ops:
  1.7 6.9 %collective-permute-start = (f32[2,256,256]{2,1,0:T(8,128)S(1)}, f32[2,256,256]{2,1,0:T(8,128)S(1)}, u32[]{:S(2)}, u32[]{:S(2)}) collective-permute-start(f32[2,256,256]{2,1,0:T(8,128)S(1)} %slice.68), channel_id=1, source_target_pairs={{1,0},{2,1},{3,2},{4,3},{5,4},{6,5},{7,6},{8,7},{9,8},{10,9},{11,1... | collective-permute-start | bytes 1572872 | tf_op jit(solution)/shard_map/ppermute | solution.py:20
  8.7 1.3 slice.71
  10.0 2.9 %collective-permute-start.5 = (f32[2,256,512]{2,1,0:T(8,128)S(1)}, f32[2,256,512]{2,1,0:T(8,128)}, u32[]{:S(2)}, u32[]{:S(2)}) collective-permute-start(f32[2,256,512]{2,1,0:T(8,128)S(1)} %slice.71), channel_id=1, source_target_pairs={{16,0},{32,16},{48,32},{64,48},{80,64},{96,80},{112,96},{128,112},... | collective-permute-start | bytes 3145736 | tf_op jit(solution)/shard_map/ppermute | solution.py:20
  14.0 15.6 %collective-permute-done.2 = f32[2,128,256]{2,1,0:T(8,128)S(1)} collective-permute-done((f32[2,128,256]{2,1,0:T(8,128)S(1)}, f32[2,128,256]{2,1,0:T(8,128)S(1)}, u32[]{:S(2)}, u32[]{:S(2)}) %collective-permute-start.2) | collective-permute-done | bytes 262176 | tf_op jit(solution)/shard_map/ppermute | solution.py:348
  29.7 2.8 %collective-permute-start.6 = (f32[2,256,256]{2,1,0:T(8,128)S(1)}, f32[2,256,256]{2,1,0:T(8,128)S(1)}, u32[]{:S(2)}, u32[]{:S(2)}) collective-permute-start(f32[2,256,256]{2,1,0:T(8,128)S(1)} %collective-permute-done.upper), channel_id=1, source_target_pairs={{16,0},{32,16},{48,32},{64,48},{80,64},{96,80},{112,96},{128,112},... | collective-permute-start | bytes 1572872 | tf_op jit(solution)/shard_map/ppermute | solution.py:20
  32.5 7.2 %collective-permute-start.1 = (f32[2,128,256]{2,1,0:T(8,128)S(1)}, f32[2,128,256]{2,1,0:T(8,128)S(1)}, u32[]{:S(2)}, u32[]{:S(2)}) collective-permute-start(f32[2,128,256]{2,1,0:T(8,128)S(1)} %get-tuple-element.45), channel_id=1, source_target_pairs={{1,0},{2,1},{3,2},{4,3},{5,4},{6,5},{7,6},{8,7},{9,8},{10,9},{11,1... | collective-permute-start | bytes 786440 | tf_op jit(solution)/shard_map/ppermute | solution.py:20
  39.7 2.3 %collective-permute-done.3 = f32[2,128,256]{2,1,0:T(8,128)S(1)} collective-permute-done((f32[2,128,256]{2,1,0:T(8,128)S(1)}, f32[2,128,256]{2,1,0:T(8,128)S(1)}, u32[]{:S(2)}, u32[]{:S(2)}) %collective-permute-start.3) | collective-permute-done | bytes 262176 | tf_op jit(solution)/shard_map/ppermute | solution.py:348
  42.0 3.1 %collective-permute-start.4 = (f32[2,128,256]{2,1,0:T(8,128)S(1)}, f32[2,128,256]{2,1,0:T(8,128)S(1)}, u32[]{:S(2)}, u32[]{:S(2)}) collective-permute-start(f32[2,128,256]{2,1,0:T(8,128)S(1)} %collective-permute-done.3), channel_id=1, source_target_pairs={{0,1},{1,2},{3,0},{4,5},{5,6},{6,3},{7,4},{8,9},{9,10},{10,7},{11,... | collective-permute-start | bytes 786440 | tf_op jit(solution)/shard_map/ppermute | solution.py:375
  45.8 8.2 %shard_map.86 = (f32[8,2,256,128]{3,2,1,0:T(8,128)}, f32[8,2,256,256]{3,2,1,0:T(8,128)}) custom-call(s32[8,2]{1,0:T(8,128)} %copy.10.off, f32[8,256,256]{2,1,0:T(8,128)} %bitcast.7, f32[2,256,256]{2,1,0:T(8,128)} %probe.1, bf16[2,256,256]{2,1,0:T(8,128)(2,1)} %constant.78.clone.pick), custom_call_target="tpu_custom_call" | custom-call | tf_op jit(solution)/shard_map/pallas_call | solution.py:96
  54.0 2.3 %collective-permute-done.4.lower = f32[2,128,256]{2,1,0:T(8,128)S(1)} collective-permute-done((f32[2,128,256]{2,1,0:T(8,128)S(1)}, f32[2,128,256]{2,1,0:T(8,128)S(1)}, u32[]{:S(2)}, u32[]{:S(2)}) %collective-permute-start.4) | collective-permute-done | bytes 262176 | tf_op jit(solution)/shard_map/ppermute | solution.py:375
  56.3 15.6 %shard_map.87 = (f32[2,512,512]{2,1,0:T(8,128)}, f32[2,256,256]{2,1,0:T(8,128)S(1)}, f32[2,256,256]{2,1,0:T(8,128)S(1)}, f32[2,256,512]{2,1,0:T(8,128)}, f32[2,2...) custom-call(s32[8,2]{1,0:T(8,128)S(1)} %copy-done, f32[2,512,512]{2,1,0:T(8,128)} %tile.1, ...), custom_call_target="tpu_custom_call" | custom-call | tf_op jit(solution)/shard_map/pallas_call | solution.py:285
  72.8 4.1 %collective-permute-start.11 = (f32[256,256]{1,0:T(8,128)S(1)}, f32[256,256]{1,0:T(8,128)S(1)}, u32[]{:S(2)}, u32[]{:S(2)}) collective-permute-start(f32[256,256]{1,0:T(8,128)S(1)} %select_bitcast_fusion), channel_id=1, source_target_pairs={{0,16},{16,0},{32,48},{48,32},{64,80},{80,64},{96,112},{112,96},{1... | collective-permute-start | bytes 786440 | tf_op jit(solution)/shard_map/ppermute | solution.py:304
  78.2 2.1 %collective-permute-start.13 = (f32[64,256]{1,0:T(8,128)S(1)}, f32[64,256]{1,0:T(8,128)S(1)}, u32[]{:S(2)}, u32[]{:S(2)}) collective-permute-start(f32[64,256]{1,0:T(8,128)S(1)} %get-tuple-element.50), channel_id=1, source_target_pairs={{0,64},{16,80},{32,96},{48,112},{64,0},{80,16},{96,32},{112,48},{1... | collective-permute-start | bytes 196616 | tf_op jit(solution)/shard_map/ppermute | solution.py:304
  80.3 1.8 collective-permute-start.14
  82.0 1.9 collective-permute-done.13
  88.1 2.9 %collective-permute-done.16 = f32[64,256]{1,0:T(8,128)S(1)} collective-permute-done((f32[64,256]{1,0:T(8,128)S(1)}, f32[64,256]{1,0:T(8,128)S(1)}, u32[]{:S(2)}, u32[]{:S(2)}) %collective-permute-start.16) | collective-permute-done | bytes 65568 | tf_op jit(solution)/shard_map/ppermute | solution.py:304
  91.0 1.3 collective-permute-start.18
  92.4 1.9 %collective-permute-done.18 = f32[64,256]{1,0:T(8,128)S(1)} collective-permute-done((f32[64,256]{1,0:T(8,128)S(1)}, f32[64,256]{1,0:T(8,128)S(1)}, u32[]{:S(2)}, u32[]{:S(2)}) %collective-permute-start.18) | collective-permute-done | bytes 65568 | tf_op jit(solution)/shard_map/ppermute | solution.py:304
  94.3 2.1 %collective-permute-start.19 = (f32[64,256]{1,0:T(8,128)S(1)}, f32[64,256]{1,0:T(8,128)S(1)}, u32[]{:S(2)}, u32[]{:S(2)}) collective-permute-start(f32[64,256]{1,0:T(8,128)S(1)} %add.80), channel_id=1, source_target_pairs={{0,1},{1,0},{2,3},{3,2},{4,5},{5,4},{6,7},{7,6},{8,9},{9,8},{10,11... | collective-permute-start | bytes 196616 | tf_op jit(solution)/shard_map/ppermute | solution.py:304
  96.4 3.2 %collective-permute-start.20 = (f32[64,256]{1,0:T(8,128)S(1)}, f32[64,256]{1,0:T(8,128)S(1)}, u32[]{:S(2)}, u32[]{:S(2)}) collective-permute-start(f32[64,256]{1,0:T(8,128)S(1)} %add.80), channel_id=1, source_target_pairs={{0,2},{1,3},{2,0},{3,1},{4,6},{5,7},{6,4},{7,5},{8,10},{9,11},{10,... | collective-permute-start | bytes 196616 | tf_op jit(solution)/shard_map/ppermute | solution.py:304
  100.0 6.3 %collective-permute-start.7 = (f32[2,256,512]{2,1,0:T(8,128)}, f32[2,256,512]{2,1,0:T(8,128)S(1)}, u32[]{:S(2)}, u32[]{:S(2)}) collective-permute-start(f32[2,256,512]{2,1,0:T(8,128)} %get-tuple-element.37), channel_id=1, source_target_pairs={{0,16},{16,32},{32,48},{48,64},{64,80},{80,96},{96,112},{112,128},... | collective-permute-start | bytes 3145736 | tf_op jit(solution)/shard_map/ppermute | solution.py:20
  107.0 7.2 %collective-permute-start.8 = (f32[2,256,256]{2,1,0:T(8,128)S(1)}, f32[2,256,256]{2,1,0:T(8,128)S(1)}, u32[]{:S(2)}, u32[]{:S(2)}) collective-permute-start(f32[2,256,256]{2,1,0:T(8,128)S(1)} %copy-done.2), channel_id=1, source_target_pairs={{0,16},{16,32},{32,48},{48,64},{64,80},{80,96},{96,112},{112,128},... | collective-permute-start | bytes 1572872 | tf_op jit(solution)/shard_map/ppermute | solution.py:20
  114.2 1.9 collective-permute-start.23
  116.1 2.2 %collective-permute-start.24 = (f32[64,256]{1,0:T(8,128)S(1)}, f32[64,256]{1,0:T(8,128)S(1)}, u32[]{:S(2)}, u32[]{:S(2)}) collective-permute-start(f32[64,256]{1,0:T(8,128)S(1)} %get-tuple-element.43), channel_id=1, source_target_pairs={{0,96},{16,112},{32,64},{48,80},{64,32},{80,48},{96,0},{112,16},{1... | collective-permute-start | bytes 196616 | tf_op jit(solution)/shard_map/ppermute | solution.py:304
  118.3 2.1 %collective-permute-done.22 = f32[64,256]{1,0:T(8,128)S(1)} collective-permute-done((f32[64,256]{1,0:T(8,128)S(1)}, f32[64,256]{1,0:T(8,128)S(1)}, u32[]{:S(2)}, u32[]{:S(2)}) %collective-permute-start.22) | collective-permute-done | bytes 65568 | tf_op jit(solution)/shard_map/ppermute | solution.py:304
  120.4 9.9 %collective-permute-done.23 = f32[64,256]{1,0:T(8,128)S(1)} collective-permute-done((f32[64,256]{1,0:T(8,128)S(1)}, f32[64,256]{1,0:T(8,128)S(1)}, u32[]{:S(2)}, u32[]{:S(2)}) %collective-permute-start.23) | collective-permute-done | bytes 65568 | tf_op jit(solution)/shard_map/ppermute | solution.py:304
  130.3 1.5 collective-permute-done.24
  132.4 2.3 %collective-permute-start.10 = (f32[2,256,256]{2,1,0:T(8,128)S(1)}, f32[2,256,256]{2,1,0:T(8,128)S(1)}, u32[]{:S(2)}, u32[]{:S(2)}) collective-permute-start(f32[2,256,256]{2,1,0:T(8,128)S(1)} %get-tuple-element.40), channel_id=1, source_target_pairs={{0,1},{1,2},{2,3},{3,4},{4,5},{5,6},{6,7},{7,8},{8,9},{9,10},{10,1... | collective-permute-start | bytes 1572872 | tf_op jit(solution)/shard_map/ppermute | solution.py:20
  134.8 4.3 %collective-permute-start.9 = (f32[2,256,256]{2,1,0:T(8,128)S(1)}, f32[2,256,256]{2,1,0:T(8,128)S(1)}, u32[]{:S(2)}, u32[]{:S(2)}) collective-permute-start(f32[2,256,256]{2,1,0:T(8,128)S(1)} %add.67), channel_id=1, source_target_pairs={{0,1},{1,2},{2,3},{3,4},{4,5},{5,6},{6,7},{7,8},{8,9},{9,10},{10,1... | collective-permute-start | bytes 1572872 | tf_op jit(solution)/shard_map/ppermute | solution.py:20
  140.3 33.0 %collective-permute-done.10 = f32[2,256,256]{2,1,0:T(8,128)S(1)} collective-permute-done((f32[2,256,256]{2,1,0:T(8,128)S(1)}, f32[2,256,256]{2,1,0:T(8,128)S(1)}, u32[]{:S(2)}, u32[]{:S(2)}) %collective-permute-start.10) | collective-permute-done | bytes 524320 | tf_op jit(solution)/shard_map/ppermute | solution.py:20
  173.4 11.2 %collective-permute-done.9 = f32[2,256,256]{2,1,0:T(8,128)S(1)} collective-permute-done((f32[2,256,256]{2,1,0:T(8,128)S(1)}, f32[2,256,256]{2,1,0:T(8,128)S(1)}, u32[]{:S(2)}, u32[]{:S(2)}) %collective-permute-start.9) | collective-permute-done | bytes 524320 | tf_op jit(solution)/shard_map/ppermute | solution.py:20
  184.9 1.3 copy-done.4
  (54 shorter events, 12.5 us)
Async XLA Ops:
  0.6 44.5 %copy-start.5 = (s32[1,1,8,2]{2,3,1,0:T(2,128)S(1)}, s32[1,1,8,2]{2,3,1,0:T(2,128)}, u32[]{:S(2)}) copy-start(s32[1,1,8,2]{2,3,1,0:T(2,128)} %param.14) | copy-start | bytes 196
  1.7 27.9 %collective-permute-start = (f32[2,256,256]{2,1,0:T(8,128)S(1)}, f32[2,256,256]{2,1,0:T(8,128)S(1)}, u32[]{:S(2)}, u32[]{:S(2)}) collective-permute-start(f32[2,256,256]{2,1,0:T(8,128)S(1)} %slice.68), channel_id=1, source_target_pairs={{1,0},{2,1},{3,2},{4,3},{5,4},{6,5},{7,6},{8,7},{9,8},{10,9},{11,1... | collective-permute-start | bytes 1572872 | tf_op jit(solution)/shard_map/ppermute | solution.py:20
  10.0 46.3 %collective-permute-start.5 = (f32[2,256,512]{2,1,0:T(8,128)S(1)}, f32[2,256,512]{2,1,0:T(8,128)}, u32[]{:S(2)}, u32[]{:S(2)}) collective-permute-start(f32[2,256,512]{2,1,0:T(8,128)S(1)} %slice.71), channel_id=1, source_target_pairs={{16,0},{32,16},{48,32},{64,48},{80,64},{96,80},{112,96},{128,112},... | collective-permute-start | bytes 3145736 | tf_op jit(solution)/shard_map/ppermute | solution.py:20
  13.9 15.7 %collective-permute-start.2 = (f32[2,128,256]{2,1,0:T(8,128)S(1)}, f32[2,128,256]{2,1,0:T(8,128)S(1)}, u32[]{:S(2)}, u32[]{:S(2)}) collective-permute-start(f32[2,128,256]{2,1,0:T(8,128)S(1)} %get-tuple-element.44), channel_id=1, source_target_pairs={{0,1},{1,2},{2,3},{3,0},{4,5},{5,6},{6,7},{7,4},{8,9},{9,10},{10,1... | collective-permute-start | bytes 786440 | tf_op jit(solution)/shard_map/ppermute | solution.py:348
  29.6 12.3 %collective-permute-start.3 = (f32[2,128,256]{2,1,0:T(8,128)S(1)}, f32[2,128,256]{2,1,0:T(8,128)S(1)}, u32[]{:S(2)}, u32[]{:S(2)}) collective-permute-start(f32[2,128,256]{2,1,0:T(8,128)S(1)} %collective-permute-done.2), channel_id=1, source_target_pairs={{0,1},{1,2},{2,3},{3,0},{4,5},{5,6},{6,7},{7,4},{8,9},{9,10},{10,1... | collective-permute-start | bytes 786440 | tf_op jit(solution)/shard_map/ppermute | solution.py:348
  29.7 26.6 %collective-permute-start.6 = (f32[2,256,256]{2,1,0:T(8,128)S(1)}, f32[2,256,256]{2,1,0:T(8,128)S(1)}, u32[]{:S(2)}, u32[]{:S(2)}) collective-permute-start(f32[2,256,256]{2,1,0:T(8,128)S(1)} %collective-permute-done.upper), channel_id=1, source_target_pairs={{16,0},{32,16},{48,32},{64,48},{80,64},{96,80},{112,96},{128,112},... | collective-permute-start | bytes 1572872 | tf_op jit(solution)/shard_map/ppermute | solution.py:20
  32.5 21.5 %collective-permute-start.1 = (f32[2,128,256]{2,1,0:T(8,128)S(1)}, f32[2,128,256]{2,1,0:T(8,128)S(1)}, u32[]{:S(2)}, u32[]{:S(2)}) collective-permute-start(f32[2,128,256]{2,1,0:T(8,128)S(1)} %get-tuple-element.45), channel_id=1, source_target_pairs={{1,0},{2,1},{3,2},{4,3},{5,4},{6,5},{7,6},{8,7},{9,8},{10,9},{11,1... | collective-permute-start | bytes 786440 | tf_op jit(solution)/shard_map/ppermute | solution.py:20
  42.0 14.3 %collective-permute-start.4 = (f32[2,128,256]{2,1,0:T(8,128)S(1)}, f32[2,128,256]{2,1,0:T(8,128)S(1)}, u32[]{:S(2)}, u32[]{:S(2)}) collective-permute-start(f32[2,128,256]{2,1,0:T(8,128)S(1)} %collective-permute-done.3), channel_id=1, source_target_pairs={{0,1},{1,2},{3,0},{4,5},{5,6},{6,3},{7,4},{8,9},{9,10},{10,7},{11,... | collective-permute-start | bytes 786440 | tf_op jit(solution)/shard_map/ppermute | solution.py:375
  45.8 10.5 %copy-start = (s32[8,2]{1,0:T(8,128)S(1)}, s32[8,2]{1,0:T(8,128)}, u32[]{:S(2)}) copy-start(s32[8,2]{1,0:T(8,128)} %copy.10.off) | copy-start | bytes 196
  71.9 0.8 copy-start.1
  72.7 34.3 %copy-start.2 = (f32[2,256,256]{2,1,0:T(8,128)S(1)}, f32[2,256,256]{2,1,0:T(8,128)}, u32[]{:S(2)}) copy-start(f32[2,256,256]{2,1,0:T(8,128)} %copy-done.1) | copy-start | bytes 1572868
  72.8 5.2 %collective-permute-start.11 = (f32[256,256]{1,0:T(8,128)S(1)}, f32[256,256]{1,0:T(8,128)S(1)}, u32[]{:S(2)}, u32[]{:S(2)}) collective-permute-start(f32[256,256]{1,0:T(8,128)S(1)} %select_bitcast_fusion), channel_id=1, source_target_pairs={{0,16},{16,0},{32,48},{48,32},{64,80},{80,64},{96,112},{112,96},{1... | collective-permute-start | bytes 786440 | tf_op jit(solution)/shard_map/ppermute | solution.py:304
  78.1 3.9 %collective-permute-start.12 = (f32[64,256]{1,0:T(8,128)S(1)}, f32[64,256]{1,0:T(8,128)S(1)}, u32[]{:S(2)}, u32[]{:S(2)}) collective-permute-start(f32[64,256]{1,0:T(8,128)S(1)} %get-tuple-element.48), channel_id=1, source_target_pairs={{0,32},{16,48},{32,0},{48,16},{64,96},{80,112},{96,64},{112,80},{1... | collective-permute-start | bytes 196616 | tf_op jit(solution)/shard_map/ppermute | solution.py:304
  78.2 5.7 %collective-permute-start.13 = (f32[64,256]{1,0:T(8,128)S(1)}, f32[64,256]{1,0:T(8,128)S(1)}, u32[]{:S(2)}, u32[]{:S(2)}) collective-permute-start(f32[64,256]{1,0:T(8,128)S(1)} %get-tuple-element.50), channel_id=1, source_target_pairs={{0,64},{16,80},{32,96},{48,112},{64,0},{80,16},{96,32},{112,48},{1... | collective-permute-start | bytes 196616 | tf_op jit(solution)/shard_map/ppermute | solution.py:304
  80.3 4.6 %collective-permute-start.14 = (f32[64,256]{1,0:T(8,128)S(1)}, f32[64,256]{1,0:T(8,128)S(1)}, u32[]{:S(2)}, u32[]{:S(2)}) collective-permute-start(f32[64,256]{1,0:T(8,128)S(1)} %get-tuple-element.49), channel_id=1, source_target_pairs={{0,96},{16,112},{32,64},{48,80},{64,32},{80,48},{96,0},{112,16},{1... | collective-permute-start | bytes 196616 | tf_op jit(solution)/shard_map/ppermute | solution.py:304
  84.9 3.2 %collective-permute-start.15 = (f32[64,256]{1,0:T(8,128)S(1)}, f32[64,256]{1,0:T(8,128)S(1)}, u32[]{:S(2)}, u32[]{:S(2)}) collective-permute-start(f32[64,256]{1,0:T(8,128)S(1)} %add_add_fusion.2), channel_id=1, source_target_pairs={{0,4},{1,5},{2,6},{3,7},{4,0},{5,1},{6,2},{7,3},{8,12},{9,13},{10,... | collective-permute-start | bytes 196616 | tf_op jit(solution)/shard_map/ppermute | solution.py:304
  85.9 5.2 %collective-permute-start.16 = (f32[64,256]{1,0:T(8,128)S(1)}, f32[64,256]{1,0:T(8,128)S(1)}, u32[]{:S(2)}, u32[]{:S(2)}) collective-permute-start(f32[64,256]{1,0:T(8,128)S(1)} %add_add_fusion.2), channel_id=1, source_target_pairs={{0,8},{1,9},{2,10},{3,11},{4,12},{5,13},{6,14},{7,15},{8,0},{9,1},... | collective-permute-start | bytes 196616 | tf_op jit(solution)/shard_map/ppermute | solution.py:304
  86.6 4.4 %collective-permute-start.17 = (f32[64,256]{1,0:T(8,128)S(1)}, f32[64,256]{1,0:T(8,128)S(1)}, u32[]{:S(2)}, u32[]{:S(2)}) collective-permute-start(f32[64,256]{1,0:T(8,128)S(1)} %add_add_fusion.2), channel_id=1, source_target_pairs={{0,12},{1,13},{2,14},{3,15},{4,8},{5,9},{6,10},{7,11},{8,4},{9,5},... | collective-permute-start | bytes 196616 | tf_op jit(solution)/shard_map/ppermute | solution.py:304
  91.0 3.2 %collective-permute-start.18 = (f32[64,256]{1,0:T(8,128)S(1)}, f32[64,256]{1,0:T(8,128)S(1)}, u32[]{:S(2)}, u32[]{:S(2)}) collective-permute-start(f32[64,256]{1,0:T(8,128)S(1)} %add_add_fusion.1), channel_id=1, source_target_pairs={{0,128},{16,144},{32,160},{48,176},{64,192},{80,208},{96,224},{112... | collective-permute-start | bytes 196616 | tf_op jit(solution)/shard_map/ppermute | solution.py:304
  94.3 12.1 %collective-permute-start.19 = (f32[64,256]{1,0:T(8,128)S(1)}, f32[64,256]{1,0:T(8,128)S(1)}, u32[]{:S(2)}, u32[]{:S(2)}) collective-permute-start(f32[64,256]{1,0:T(8,128)S(1)} %add.80), channel_id=1, source_target_pairs={{0,1},{1,0},{2,3},{3,2},{4,5},{5,4},{6,7},{7,6},{8,9},{9,8},{10,11... | collective-permute-start | bytes 196616 | tf_op jit(solution)/shard_map/ppermute | solution.py:304
  96.4 10.0 %collective-permute-start.20 = (f32[64,256]{1,0:T(8,128)S(1)}, f32[64,256]{1,0:T(8,128)S(1)}, u32[]{:S(2)}, u32[]{:S(2)}) collective-permute-start(f32[64,256]{1,0:T(8,128)S(1)} %add.80), channel_id=1, source_target_pairs={{0,2},{1,3},{2,0},{3,1},{4,6},{5,7},{6,4},{7,5},{8,10},{9,11},{10,... | collective-permute-start | bytes 196616 | tf_op jit(solution)/shard_map/ppermute | solution.py:304
  99.6 6.8 %collective-permute-start.21 = (f32[64,256]{1,0:T(8,128)S(1)}, f32[64,256]{1,0:T(8,128)S(1)}, u32[]{:S(2)}, u32[]{:S(2)}) collective-permute-start(f32[64,256]{1,0:T(8,128)S(1)} %add.80), channel_id=1, source_target_pairs={{0,3},{1,2},{2,1},{3,0},{4,7},{5,6},{6,5},{7,4},{8,11},{9,10},{10,... | collective-permute-start | bytes 196616 | tf_op jit(solution)/shard_map/ppermute | solution.py:304
  100.0 40.0 %collective-permute-start.7 = (f32[2,256,512]{2,1,0:T(8,128)}, f32[2,256,512]{2,1,0:T(8,128)S(1)}, u32[]{:S(2)}, u32[]{:S(2)}) collective-permute-start(f32[2,256,512]{2,1,0:T(8,128)} %get-tuple-element.37), channel_id=1, source_target_pairs={{0,16},{16,32},{32,48},{48,64},{64,80},{80,96},{96,112},{112,128},... | collective-permute-start | bytes 3145736 | tf_op jit(solution)/shard_map/ppermute | solution.py:20
  106.4 33.6 %copy-start.3 = (f32[2,512,512]{2,1,0:T(8,128)S(1)}, f32[2,512,512]{2,1,0:T(8,128)}, u32[]{:S(2)}) copy-start(f32[2,512,512]{2,1,0:T(8,128)} %get-tuple-element.36) | copy-start | bytes 6291460
  106.4 13.9 %collective-permute-start.22 = (f32[64,256]{1,0:T(8,128)S(1)}, f32[64,256]{1,0:T(8,128)S(1)}, u32[]{:S(2)}, u32[]{:S(2)}) collective-permute-start(f32[64,256]{1,0:T(8,128)S(1)} %get-tuple-element.43), channel_id=1, source_target_pairs={{0,32},{16,48},{32,0},{48,16},{64,96},{80,112},{96,64},{112,80},{1... | collective-permute-start | bytes 196616 | tf_op jit(solution)/shard_map/ppermute | solution.py:304
  107.0 27.7 %collective-permute-start.8 = (f32[2,256,256]{2,1,0:T(8,128)S(1)}, f32[2,256,256]{2,1,0:T(8,128)S(1)}, u32[]{:S(2)}, u32[]{:S(2)}) collective-permute-start(f32[2,256,256]{2,1,0:T(8,128)S(1)} %copy-done.2), channel_id=1, source_target_pairs={{0,16},{16,32},{32,48},{48,64},{64,80},{80,96},{96,112},{112,128},... | collective-permute-start | bytes 1572872 | tf_op jit(solution)/shard_map/ppermute | solution.py:20
  114.2 16.1 %collective-permute-start.23 = (f32[64,256]{1,0:T(8,128)S(1)}, f32[64,256]{1,0:T(8,128)S(1)}, u32[]{:S(2)}, u32[]{:S(2)}) collective-permute-start(f32[64,256]{1,0:T(8,128)S(1)} %get-tuple-element.43), channel_id=1, source_target_pairs={{0,64},{16,80},{32,96},{48,112},{64,0},{80,16},{96,32},{112,48},{1... | collective-permute-start | bytes 196616 | tf_op jit(solution)/shard_map/ppermute | solution.py:304
  116.1 15.7 %collective-permute-start.24 = (f32[64,256]{1,0:T(8,128)S(1)}, f32[64,256]{1,0:T(8,128)S(1)}, u32[]{:S(2)}, u32[]{:S(2)}) collective-permute-start(f32[64,256]{1,0:T(8,128)S(1)} %get-tuple-element.43), channel_id=1, source_target_pairs={{0,96},{16,112},{32,64},{48,80},{64,32},{80,48},{96,0},{112,16},{1... | collective-permute-start | bytes 196616 | tf_op jit(solution)/shard_map/ppermute | solution.py:304
  131.8 7.3 %collective-permute-start.25 = (f32[256,256]{1,0:T(8,128)S(1)}, f32[256,256]{1,0:T(8,128)S(1)}, u32[]{:S(2)}, u32[]{:S(2)}) collective-permute-start(f32[256,256]{1,0:T(8,128)S(1)} %constant_dynamic-update-slice_fusion), channel_id=1, source_target_pairs={{0,16},{16,0},{32,48},{48,32},{64,80},{80,64},{96,112},{112,96},{1... | collective-permute-start | bytes 786440 | tf_op jit(solution)/shard_map/ppermute | solution.py:304
  132.4 41.0 %collective-permute-start.10 = (f32[2,256,256]{2,1,0:T(8,128)S(1)}, f32[2,256,256]{2,1,0:T(8,128)S(1)}, u32[]{:S(2)}, u32[]{:S(2)}) collective-permute-start(f32[2,256,256]{2,1,0:T(8,128)S(1)} %get-tuple-element.40), channel_id=1, source_target_pairs={{0,1},{1,2},{2,3},{3,4},{4,5},{5,6},{6,7},{7,8},{8,9},{9,10},{10,1... | collective-permute-start | bytes 1572872 | tf_op jit(solution)/shard_map/ppermute | solution.py:20
  134.8 49.8 %collective-permute-start.9 = (f32[2,256,256]{2,1,0:T(8,128)S(1)}, f32[2,256,256]{2,1,0:T(8,128)S(1)}, u32[]{:S(2)}, u32[]{:S(2)}) collective-permute-start(f32[2,256,256]{2,1,0:T(8,128)S(1)} %add.67), channel_id=1, source_target_pairs={{0,1},{1,2},{2,3},{3,4},{4,5},{5,6},{6,7},{7,8},{8,9},{9,10},{10,1... | collective-permute-start | bytes 1572872 | tf_op jit(solution)/shard_map/ppermute | solution.py:20
  184.9 1.3 copy-start.4

commit v6 on v5

--- a/solution.py
+++ b/solution.py
@@ -239,7 +239,7 @@
         running = [patch for patch in running if next(patch, running) is None]
 
 
-def patches_kernel(off, tile, upper, middle, lower, bottom, corner, probe, amp, left_table, right_table,
+def patches_kernel(off, tile, upper, middle, lower, bottom, relayed, corner, probe, amp, left_table, right_table,
                    main_out, upper_out, lower_out, bottom_out, corner_out, probe_out, ext, grad, *scratch, scale):
     side = upper.shape[2]
     rows, cols = tile.shape[1], tile.shape[2]
@@ -252,7 +252,7 @@
         ext[:, :side, cols:] = upper[...]
         ext[:, side:cut, cols:] = middle[...]
         ext[:, cut:rows, cols:] = lower[...]
-        ext[:, rows:, :cols] = bottom[...]
+        ext[:, rows:, :cols] = bottom[...] + relayed[...]
         ext[:, rows:, cols:] = corner[...]
         grad[...] = jnp.zeros_like(grad)
         probe_out[...] = jnp.zeros_like(probe_out)
@@ -273,7 +273,7 @@
         probe_out[...] *= scale
 
 
-def all_patches(off, tile, upper, middle, lower, bottom, corner, probe, amp, scale):
+def all_patches(off, tile, upper, middle, lower, bottom, relayed, corner, probe, amp, scale):
     count, side = amp.shape[0], upper.shape[2]
     together = 2 if count % 2 == 0 else 1
     rows, cols = tile.shape[1], tile.shape[2]
@@ -287,14 +287,14 @@
         grid=(count // together,),
         out_shape=(shape(2, rows, cols), shape(2, side, side), shape(2, rows - side, side), shape(2, side, cols),
                    shape(2, side, side), shape(2, side, side)),
-        in_specs=[pl.BlockSpec(memory_space=pltpu.SMEM)] + [vmem] * 6
+        in_specs=[pl.BlockSpec(memory_space=pltpu.SMEM)] + [vmem] * 7
                  + [pl.BlockSpec((together, 2, side, side), lambda i: (i, 0, 0, 0)),
                     pl.BlockSpec((together, 2, side, side // 2), lambda i: (i, 0, 0, 0))] + [vmem] * 2,
         out_specs=[vmem] * 6,
         scratch_shapes=[pltpu.VMEM((2, rows + side, cols + side), F32)] * 2
                      + [pltpu.VMEM((together, 2, side, side), F32)] + [pltpu.VMEM((together, 2, side, side), BF16)] * 4,
         compiler_params=pltpu.CompilerParams(vmem_limit_bytes=50 * 1024 * 1024),
-    )(off, tile, upper, middle, lower, bottom, corner, probes, amps, *tables)
+    )(off, tile, upper, middle, lower, bottom, relayed, corner, probes, amps, *tables)
 
 
 ACROSS, LINES = (2, 4, 6), (4, 8, 12)
@@ -375,17 +375,25 @@
     return lax.ppermute(value, "col", pairs)
 
 
+def bottom_rows(value):
+    count = lax.axis_size("row")
+    half = count // 2
+    relayed = lax.ppermute(value, "row", [(half, count - 2)])
+    bottom = lax.ppermute(value, "row", [(i, i - 1) for i in range(1, count) if i != half])
+    return bottom, lax.ppermute(relayed, "row", [(count - 2, half - 1)])
+
+
 def shards_body(object_field, probe, amplitude, offsets):
     side = probe.shape[1]
-    cut = object_field.shape[1] - side // 2
+    cut = object_field.shape[1] - side * 7 // 16
     lower = long_way(object_field[:, cut:, :side])
     upper = passed_along(object_field[:, :side, :side], "col", -1)
     middle = passed_along(object_field[:, side:cut, :side], "col", -1)
-    bottom = passed_along(object_field[:, :side, :], "row", -1)
+    bottom, relayed = bottom_rows(object_field[:, :side, :])
     corner = passed_along(upper, "row", -1)
     count = amplitude.shape[2] * lax.axis_size("row") * lax.axis_size("col")
     main, upper, lower, bottom, corner, probe_acc = all_patches(
-        offsets[0, 0], object_field, upper, middle, lower, bottom, corner, probe, amplitude[0, 0], 1.0 / count)
+        offsets[0, 0], object_field, upper, middle, lower, bottom, relayed, corner, probe, amplitude[0, 0], 1.0 / count)
     corner_back = passed_along(corner, "row", 1)
     lower_back = passed_along(lower, "col", 1)
     bottom_back = passed_along(bottom, "row", 1)

time: 187 us -> 199 us (1.064)
  the two profiles are of different devices: /device:TPU:49 before, /device:TPU:24 now
where the time goes in v6:
time: 199 us; the launch traced here: 198 us
  waiting for transfers between devices  92.1 us (46%)
  starting transfers between devices  72.9 us (37%)
  Pallas kernels  24.3 us (12%)
  local copies, waits for them, and re-layouts  6.45 us (3%)
    ppermute x7, waiting for transfers between devices, passed_along(): lax.ppermute(value, axis, [(source, source + steps) for source in range(f...  65.7 us
    ppermute x15, starting transfers between devices, exchanged(): lax.ppermute(piece, axis, [(i, i ^ distance) for i in range(lax.axis_size...  35.7 us
    ppermute x7, starting transfers between devices, passed_along(): lax.ppermute(value, axis, [(source, source + steps) for source in range(f...  27 us
    ppermute x15, waiting for transfers between devices, exchanged(): lax.ppermute(piece, axis, [(i, i ^ distance) for i in range(lax.axis_size...  20.1 us
    pallas_call x1, Pallas kernels, all_patches(): pl.pallas_call(functools.partial(patches_kernel, scale=scale), grid=(coun...  16.1 us
    pallas_call x1, Pallas kernels, prepare(): pl.pallas_call(prepare_kernel, grid=(count,), out_shape=(jax.ShapeDtypeSt...  8.19 us
    ppermute x1, starting transfers between devices, long_way(): return lax.ppermute(value, 'col', pairs)  5.44 us
    ppermute x2, waiting for transfers between devices, round_ring(): lax.ppermute(value, 'col', [(i, i // 4 * 4 + (i + step) % 4) for i in ran...  4.46 us
  transfers between devices with their start and end apart: 28, of which 15 were waited for; matrix products, arithmetic and copies ran while one was open for 1% of the time, Pallas kernels for 4%

profile of v6, /device:TPU:24, one launch (start us, length us, event | category | flops | bytes accessed | tf_op | source)
XLA Modules:
  0.0 198.3 jit_solution(7010435222444656547)
XLA Ops:
  0.7 2.4 %slice.71 = f32[2,256,512]{2,1,0:T(8,128)} slice(f32[2,512,512]{2,1,0:T(8,128)} %tile.1), slice={[0:2], [0:256], [0:512]} | slice | bytes 2097152 | tf_op jit(solution)/shard_map/slice | solution.py:392
  3.1 1.7 collective-permute-start.6
  6.1 8.4 %collective-permute-start = (f32[2,256,256]{2,1,0:T(8,128)S(1)}, f32[2,256,256]{2,1,0:T(8,128)S(1)}, u32[]{:S(2)}, u32[]{:S(2)}) collective-permute-start(f32[2,256,256]{2,1,0:T(8,128)S(1)} %slice.68), channel_id=1, source_target_pairs={{1,0},{2,1},{3,2},{4,3},{5,4},{6,5},{7,6},{8,7},{9,8},{10,9},{11,1... | collective-permute-start | bytes 1572872 | tf_op jit(solution)/shard_map/ppermute | solution.py:20
  14.5 1.6 collective-permute-start.7
  16.3 21.6 %collective-permute-done.upper = f32[2,256,256]{2,1,0:T(8,128)S(1)} collective-permute-done((f32[2,256,256]{2,1,0:T(8,128)S(1)}, f32[2,256,256]{2,1,0:T(8,128)S(1)}, u32[]{:S(2)}, u32[]{:S(2)}) %collective-permute-start) | collective-permute-done | bytes 524320 | tf_op jit(solution)/shard_map/ppermute | solution.py:20
  39.3 7.4 %collective-permute-start.1 = (f32[2,144,256]{2,1,0:T(8,128)S(1)}, f32[2,144,256]{2,1,0:T(8,128)S(1)}, u32[]{:S(2)}, u32[]{:S(2)}) collective-permute-start(f32[2,144,256]{2,1,0:T(8,128)S(1)} %slice.69), channel_id=1, source_target_pairs={{1,0},{2,1},{3,2},{4,3},{5,4},{6,5},{7,6},{8,7},{9,8},{10,9},{11,1... | collective-permute-start | bytes 884744 | tf_op jit(solution)/shard_map/ppermute | solution.py:20
  46.7 4.5 %collective-permute-done.3 = f32[2,112,256]{2,1,0:T(8,128)S(1)} collective-permute-done((f32[2,112,256]{2,1,0:T(8,128)S(1)}, f32[2,112,256]{2,1,0:T(8,128)S(1)}, u32[]{:S(2)}, u32[]{:S(2)}) %collective-permute-start.3) | collective-permute-done | bytes 229408 | tf_op jit(solution)/shard_map/ppermute | solution.py:348
  51.2 5.4 %collective-permute-start.4 = (f32[2,112,256]{2,1,0:T(8,128)S(1)}, f32[2,112,256]{2,1,0:T(8,128)S(1)}, u32[]{:S(2)}, u32[]{:S(2)}) collective-permute-start(f32[2,112,256]{2,1,0:T(8,128)S(1)} %collective-permute-done.3), channel_id=1, source_target_pairs={{0,1},{1,2},{3,0},{4,5},{5,6},{6,3},{7,4},{8,9},{9,10},{10,7},{11,... | collective-permute-start | bytes 688136 | tf_op jit(solution)/shard_map/ppermute | solution.py:375
  57.3 8.2 %shard_map.86 = (f32[8,2,256,128]{3,2,1,0:T(8,128)}, f32[8,2,256,256]{3,2,1,0:T(8,128)}) custom-call(s32[8,2]{1,0:T(8,128)} %copy.10.off, f32[8,256,256]{2,1,0:T(8,128)} %bitcast.7, f32[2,256,256]{2,1,0:T(8,128)} %probe.1, bf16[2,256,256]{2,1,0:T(8,128)(2,1)} %constant.78.clone.pick), custom_call_target="tpu_custom_call" | custom-call | tf_op jit(solution)/shard_map/pallas_call | solution.py:96
  65.5 1.7 collective-permute-done.4.lower
  68.3 16.1 %shard_map.87 = (f32[2,512,512]{2,1,0:T(8,128)}, f32[2,256,256]{2,1,0:T(8,128)S(1)}, f32[2,256,256]{2,1,0:T(8,128)S(1)}, f32[2,256,512]{2,1,0:T(8,128)}, f32[2,2...) custom-call(s32[8,2]{1,0:T(8,128)S(1)} %copy-done, f32[2,512,512]{2,1,0:T(8,128)} %tile.1, ...), custom_call_target="tpu_custom_call" | custom-call | tf_op jit(solution)/shard_map/pallas_call | solution.py:285
  85.4 1.5 collective-permute-done.13
  87.0 2.1 %collective-permute-start.14 = (f32[64,256]{1,0:T(8,128)S(1)}, f32[64,256]{1,0:T(8,128)S(1)}, u32[]{:S(2)}, u32[]{:S(2)}) collective-permute-start(f32[64,256]{1,0:T(8,128)S(1)} %get-tuple-element.46), channel_id=1, source_target_pairs={{0,32},{16,48},{32,0},{48,16},{64,96},{80,112},{96,64},{112,80},{1... | collective-permute-start | bytes 196616 | tf_op jit(solution)/shard_map/ppermute | solution.py:304
  89.0 2.2 %collective-permute-start.15 = (f32[64,256]{1,0:T(8,128)S(1)}, f32[64,256]{1,0:T(8,128)S(1)}, u32[]{:S(2)}, u32[]{:S(2)}) collective-permute-start(f32[64,256]{1,0:T(8,128)S(1)} %get-tuple-element.48), channel_id=1, source_target_pairs={{0,64},{16,80},{32,96},{48,112},{64,0},{80,16},{96,32},{112,48},{1... | collective-permute-start | bytes 196616 | tf_op jit(solution)/shard_map/ppermute | solution.py:304
  91.8 3.1 %collective-permute-done.15 = f32[64,256]{1,0:T(8,128)S(1)} collective-permute-done((f32[64,256]{1,0:T(8,128)S(1)}, f32[64,256]{1,0:T(8,128)S(1)}, u32[]{:S(2)}, u32[]{:S(2)}) %collective-permute-start.15) | collective-permute-done | bytes 65568 | tf_op jit(solution)/shard_map/ppermute | solution.py:304
  94.9 1.8 collective-permute-done.16
  96.8 4.6 %collective-permute-start.17 = (f32[64,256]{1,0:T(8,128)S(1)}, f32[64,256]{1,0:T(8,128)S(1)}, u32[]{:S(2)}, u32[]{:S(2)}) collective-permute-start(f32[64,256]{1,0:T(8,128)S(1)} %add_add_fusion.2), channel_id=1, source_target_pairs={{0,4},{1,5},{2,6},{3,7},{4,0},{5,1},{6,2},{7,3},{8,12},{9,13},{10,... | collective-permute-start | bytes 196616 | tf_op jit(solution)/shard_map/ppermute | solution.py:304
  102.0 2.2 %collective-permute-start.19 = (f32[64,256]{1,0:T(8,128)S(1)}, f32[64,256]{1,0:T(8,128)S(1)}, u32[]{:S(2)}, u32[]{:S(2)}) collective-permute-start(f32[64,256]{1,0:T(8,128)S(1)} %add_add_fusion.2), channel_id=1, source_target_pairs={{0,12},{1,13},{2,14},{3,15},{4,8},{5,9},{6,10},{7,11},{8,4},{9,5},... | collective-permute-start | bytes 196616 | tf_op jit(solution)/shard_map/ppermute | solution.py:304
  104.2 3.0 %collective-permute-done.18 = f32[64,256]{1,0:T(8,128)S(1)} collective-permute-done((f32[64,256]{1,0:T(8,128)S(1)}, f32[64,256]{1,0:T(8,128)S(1)}, u32[]{:S(2)}, u32[]{:S(2)}) %collective-permute-start.18) | collective-permute-done | bytes 65568 | tf_op jit(solution)/shard_map/ppermute | solution.py:304
  108.6 3.6 %collective-permute-done.20 = f32[64,256]{1,0:T(8,128)S(1)} collective-permute-done((f32[64,256]{1,0:T(8,128)S(1)}, f32[64,256]{1,0:T(8,128)S(1)}, u32[]{:S(2)}, u32[]{:S(2)}) %collective-permute-start.20) | collective-permute-done | bytes 65568 | tf_op jit(solution)/shard_map/ppermute | solution.py:304
  112.3 3.4 %collective-permute-start.22 = (f32[64,256]{1,0:T(8,128)S(1)}, f32[64,256]{1,0:T(8,128)S(1)}, u32[]{:S(2)}, u32[]{:S(2)}) collective-permute-start(f32[64,256]{1,0:T(8,128)S(1)} %add.80), channel_id=1, source_target_pairs={{0,2},{1,3},{2,0},{3,1},{4,6},{5,7},{6,4},{7,5},{8,10},{9,11},{10,... | collective-permute-start | bytes 196616 | tf_op jit(solution)/shard_map/ppermute | solution.py:304
  115.8 3.0 %collective-permute-start.23 = (f32[64,256]{1,0:T(8,128)S(1)}, f32[64,256]{1,0:T(8,128)S(1)}, u32[]{:S(2)}, u32[]{:S(2)}) collective-permute-start(f32[64,256]{1,0:T(8,128)S(1)} %add.80), channel_id=1, source_target_pairs={{0,3},{1,2},{2,1},{3,0},{4,7},{5,6},{6,5},{7,4},{8,11},{9,10},{10,... | collective-permute-start | bytes 196616 | tf_op jit(solution)/shard_map/ppermute | solution.py:304
  120.8 1.5 collective-permute-done.23
  122.7 1.4 collective-permute-start.10
  124.1 3.8 %collective-permute-start.25 = (f32[64,256]{1,0:T(8,128)S(1)}, f32[64,256]{1,0:T(8,128)S(1)}, u32[]{:S(2)}, u32[]{:S(2)}) collective-permute-start(f32[64,256]{1,0:T(8,128)S(1)} %get-tuple-element.43), channel_id=1, source_target_pairs={{0,64},{16,80},{32,96},{48,112},{64,0},{80,16},{96,32},{112,48},{1... | collective-permute-start | bytes 196616 | tf_op jit(solution)/shard_map/ppermute | solution.py:304
  129.2 1.8 collective-permute-done.25
  130.9 2.5 %collective-permute-done.26 = f32[64,256]{1,0:T(8,128)S(1)} collective-permute-done((f32[64,256]{1,0:T(8,128)S(1)}, f32[64,256]{1,0:T(8,128)S(1)}, u32[]{:S(2)}, u32[]{:S(2)}) %collective-permute-start.26) | collective-permute-done | bytes 65568 | tf_op jit(solution)/shard_map/ppermute | solution.py:304
  133.5 10.7 %collective-permute-start.27 = (f32[256,256]{1,0:T(8,128)S(1)}, f32[256,256]{1,0:T(8,128)S(1)}, u32[]{:S(2)}, u32[]{:S(2)}) collective-permute-start(f32[256,256]{1,0:T(8,128)S(1)} %constant_dynamic-update-slice_fusion), channel_id=1, source_target_pairs={{0,16},{16,0},{32,48},{48,32},{64,80},{80,64},{96,112},{112,96},{1... | collective-permute-start | bytes 786440 | tf_op jit(solution)/shard_map/ppermute | solution.py:304
  144.2 2.2 %collective-permute-start.12 = (f32[2,256,256]{2,1,0:T(8,128)S(1)}, f32[2,256,256]{2,1,0:T(8,128)S(1)}, u32[]{:S(2)}, u32[]{:S(2)}) collective-permute-start(f32[2,256,256]{2,1,0:T(8,128)S(1)} %get-tuple-element.40), channel_id=1, source_target_pairs={{0,1},{1,2},{2,3},{3,4},{4,5},{5,6},{6,7},{7,8},{8,9},{9,10},{10,1... | collective-permute-start | bytes 1572872 | tf_op jit(solution)/shard_map/ppermute | solution.py:20
  146.4 4.9 %collective-permute-start.11 = (f32[2,256,256]{2,1,0:T(8,128)S(1)}, f32[2,256,256]{2,1,0:T(8,128)S(1)}, u32[]{:S(2)}, u32[]{:S(2)}) collective-permute-start(f32[2,256,256]{2,1,0:T(8,128)S(1)} %add.67), channel_id=1, source_target_pairs={{0,1},{1,2},{2,3},{3,4},{4,5},{5,6},{6,7},{7,8},{8,9},{9,10},{10,1... | collective-permute-start | bytes 1572872 | tf_op jit(solution)/shard_map/ppermute | solution.py:20
  152.6 11.4 %collective-permute-done.12 = f32[2,256,256]{2,1,0:T(8,128)S(1)} collective-permute-done((f32[2,256,256]{2,1,0:T(8,128)S(1)}, f32[2,256,256]{2,1,0:T(8,128)S(1)}, u32[]{:S(2)}, u32[]{:S(2)}) %collective-permute-start.12) | collective-permute-done | bytes 524320 | tf_op jit(solution)/shard_map/ppermute | solution.py:20
  164.0 32.7 %collective-permute-done.11 = f32[2,256,256]{2,1,0:T(8,128)S(1)} collective-permute-done((f32[2,256,256]{2,1,0:T(8,128)S(1)}, f32[2,256,256]{2,1,0:T(8,128)S(1)}, u32[]{:S(2)}, u32[]{:S(2)}) %collective-permute-start.11) | collective-permute-done | bytes 524320 | tf_op jit(solution)/shard_map/ppermute | solution.py:20
  (63 shorter events, 14.7 us)
Async XLA Ops:
  0.6 56.0 %copy-start.7 = (s32[1,1,8,2]{2,3,1,0:T(2,128)S(1)}, s32[1,1,8,2]{2,3,1,0:T(2,128)}, u32[]{:S(2)}) copy-start(s32[1,1,8,2]{2,3,1,0:T(2,128)} %param.14) | copy-start | bytes 196
  3.1 11.4 %collective-permute-start.6 = (f32[2,256,512]{2,1,0:T(8,128)}, f32[2,256,512]{2,1,0:T(8,128)}, u32[]{:S(2)}, u32[]{:S(2)}) collective-permute-start(f32[2,256,512]{2,1,0:T(8,128)} %slice.71), channel_id=1, source_target_pairs={{128,224},{129,225},{130,226},{131,227},{132,228},{133,229},{134,2... | collective-permute-start | bytes 3145736 | tf_op jit(solution)/shard_map/ppermute | solution.py:381
  4.8 62.5 %collective-permute-start.5 = (f32[2,256,512]{2,1,0:T(8,128)}, f32[2,256,512]{2,1,0:T(8,128)S(1)}, u32[]{:S(2)}, u32[]{:S(2)}) collective-permute-start(f32[2,256,512]{2,1,0:T(8,128)} %slice.71), channel_id=1, source_target_pairs={{16,0},{32,16},{48,32},{64,48},{80,64},{96,80},{112,96},{144,128},... | collective-permute-start | bytes 3145736 | tf_op jit(solution)/shard_map/ppermute | solution.py:382
  6.1 31.8 %collective-permute-start = (f32[2,256,256]{2,1,0:T(8,128)S(1)}, f32[2,256,256]{2,1,0:T(8,128)S(1)}, u32[]{:S(2)}, u32[]{:S(2)}) collective-permute-start(f32[2,256,256]{2,1,0:T(8,128)S(1)} %slice.68), channel_id=1, source_target_pairs={{1,0},{2,1},{3,2},{4,3},{5,4},{6,5},{7,6},{8,7},{9,8},{10,9},{11,1... | collective-permute-start | bytes 1572872 | tf_op jit(solution)/shard_map/ppermute | solution.py:20
  14.5 52.7 %collective-permute-start.7 = (f32[2,256,512]{2,1,0:T(8,128)}, f32[2,256,512]{2,1,0:T(8,128)}, u32[]{:S(2)}, u32[]{:S(2)}) collective-permute-start(f32[2,256,512]{2,1,0:T(8,128)} %collective-permute-done.6), channel_id=1, source_target_pairs={{224,112},{225,113},{226,114},{227,115},{228,116},{229,117},{230,1... | collective-permute-start | bytes 3145736 | tf_op jit(solution)/shard_map/ppermute | solution.py:383
  16.2 23.0 %collective-permute-start.2 = (f32[2,112,256]{2,1,0:T(8,128)S(1)}, f32[2,112,256]{2,1,0:T(8,128)S(1)}, u32[]{:S(2)}, u32[]{:S(2)}) collective-permute-start(f32[2,112,256]{2,1,0:T(8,128)S(1)} %slice.70), channel_id=1, source_target_pairs={{0,1},{1,2},{2,3},{3,0},{4,5},{5,6},{6,7},{7,4},{8,9},{9,10},{10,1... | collective-permute-start | bytes 688136 | tf_op jit(solution)/shard_map/ppermute | solution.py:348
  37.9 29.4 %collective-permute-start.8 = (f32[2,256,256]{2,1,0:T(8,128)S(1)}, f32[2,256,256]{2,1,0:T(8,128)S(1)}, u32[]{:S(2)}, u32[]{:S(2)}) collective-permute-start(f32[2,256,256]{2,1,0:T(8,128)S(1)} %collective-permute-done.upper), channel_id=1, source_target_pairs={{16,0},{32,16},{48,32},{64,48},{80,64},{96,80},{112,96},{128,112},... | collective-permute-start | bytes 1572872 | tf_op jit(solution)/shard_map/ppermute | solution.py:20
  39.2 12.0 %collective-permute-start.3 = (f32[2,112,256]{2,1,0:T(8,128)S(1)}, f32[2,112,256]{2,1,0:T(8,128)S(1)}, u32[]{:S(2)}, u32[]{:S(2)}) collective-permute-start(f32[2,112,256]{2,1,0:T(8,128)S(1)} %collective-permute-done.2), channel_id=1, source_target_pairs={{0,1},{1,2},{2,3},{3,0},{4,5},{5,6},{6,7},{7,4},{8,9},{9,10},{10,1... | collective-permute-start | bytes 688136 | tf_op jit(solution)/shard_map/ppermute | solution.py:348
  39.3 26.2 %collective-permute-start.1 = (f32[2,144,256]{2,1,0:T(8,128)S(1)}, f32[2,144,256]{2,1,0:T(8,128)S(1)}, u32[]{:S(2)}, u32[]{:S(2)}) collective-permute-start(f32[2,144,256]{2,1,0:T(8,128)S(1)} %slice.69), channel_id=1, source_target_pairs={{1,0},{2,1},{3,2},{4,3},{5,4},{6,5},{7,6},{8,7},{9,8},{10,9},{11,1... | collective-permute-start | bytes 884744 | tf_op jit(solution)/shard_map/ppermute | solution.py:20
  51.2 16.1 %collective-permute-start.4 = (f32[2,112,256]{2,1,0:T(8,128)S(1)}, f32[2,112,256]{2,1,0:T(8,128)S(1)}, u32[]{:S(2)}, u32[]{:S(2)}) collective-permute-start(f32[2,112,256]{2,1,0:T(8,128)S(1)} %collective-permute-done.3), channel_id=1, source_target_pairs={{0,1},{1,2},{3,0},{4,5},{5,6},{6,3},{7,4},{8,9},{9,10},{10,7},{11,... | collective-permute-start | bytes 688136 | tf_op jit(solution)/shard_map/ppermute | solution.py:375
  57.3 11.0 %copy-start = (s32[8,2]{1,0:T(8,128)S(1)}, s32[8,2]{1,0:T(8,128)}, u32[]{:S(2)}) copy-start(s32[8,2]{1,0:T(8,128)} %copy.10.off) | copy-start | bytes 196
  85.2 37.5 %copy-start.2 = (f32[2,256,256]{2,1,0:T(8,128)S(1)}, f32[2,256,256]{2,1,0:T(8,128)}, u32[]{:S(2)}) copy-start(f32[2,256,256]{2,1,0:T(8,128)} %copy-done.1) | copy-start | bytes 1572868
  85.3 1.6 collective-permute-start.13
  87.0 4.8 %collective-permute-start.14 = (f32[64,256]{1,0:T(8,128)S(1)}, f32[64,256]{1,0:T(8,128)S(1)}, u32[]{:S(2)}, u32[]{:S(2)}) collective-permute-start(f32[64,256]{1,0:T(8,128)S(1)} %get-tuple-element.46), channel_id=1, source_target_pairs={{0,32},{16,48},{32,0},{48,16},{64,96},{80,112},{96,64},{112,80},{1... | collective-permute-start | bytes 196616 | tf_op jit(solution)/shard_map/ppermute | solution.py:304
  89.0 5.9 %collective-permute-start.15 = (f32[64,256]{1,0:T(8,128)S(1)}, f32[64,256]{1,0:T(8,128)S(1)}, u32[]{:S(2)}, u32[]{:S(2)}) collective-permute-start(f32[64,256]{1,0:T(8,128)S(1)} %get-tuple-element.48), channel_id=1, source_target_pairs={{0,64},{16,80},{32,96},{48,112},{64,0},{80,16},{96,32},{112,48},{1... | collective-permute-start | bytes 196616 | tf_op jit(solution)/shard_map/ppermute | solution.py:304
  91.3 5.5 %collective-permute-start.16 = (f32[64,256]{1,0:T(8,128)S(1)}, f32[64,256]{1,0:T(8,128)S(1)}, u32[]{:S(2)}, u32[]{:S(2)}) collective-permute-start(f32[64,256]{1,0:T(8,128)S(1)} %get-tuple-element.47), channel_id=1, source_target_pairs={{0,96},{16,112},{32,64},{48,80},{64,32},{80,48},{96,0},{112,16},{1... | collective-permute-start | bytes 196616 | tf_op jit(solution)/shard_map/ppermute | solution.py:304
  96.8 7.4 %collective-permute-start.17 = (f32[64,256]{1,0:T(8,128)S(1)}, f32[64,256]{1,0:T(8,128)S(1)}, u32[]{:S(2)}, u32[]{:S(2)}) collective-permute-start(f32[64,256]{1,0:T(8,128)S(1)} %add_add_fusion.2), channel_id=1, source_target_pairs={{0,4},{1,5},{2,6},{3,7},{4,0},{5,1},{6,2},{7,3},{8,12},{9,13},{10,... | collective-permute-start | bytes 196616 | tf_op jit(solution)/shard_map/ppermute | solution.py:304
  101.4 5.8 %collective-permute-start.18 = (f32[64,256]{1,0:T(8,128)S(1)}, f32[64,256]{1,0:T(8,128)S(1)}, u32[]{:S(2)}, u32[]{:S(2)}) collective-permute-start(f32[64,256]{1,0:T(8,128)S(1)} %add_add_fusion.2), channel_id=1, source_target_pairs={{0,8},{1,9},{2,10},{3,11},{4,12},{5,13},{6,14},{7,15},{8,0},{9,1},... | collective-permute-start | bytes 196616 | tf_op jit(solution)/shard_map/ppermute | solution.py:304
  102.0 5.9 %collective-permute-start.19 = (f32[64,256]{1,0:T(8,128)S(1)}, f32[64,256]{1,0:T(8,128)S(1)}, u32[]{:S(2)}, u32[]{:S(2)}) collective-permute-start(f32[64,256]{1,0:T(8,128)S(1)} %add_add_fusion.2), channel_id=1, source_target_pairs={{0,12},{1,13},{2,14},{3,15},{4,8},{5,9},{6,10},{7,11},{8,4},{9,5},... | collective-permute-start | bytes 196616 | tf_op jit(solution)/shard_map/ppermute | solution.py:304
  107.9 4.4 %collective-permute-start.20 = (f32[64,256]{1,0:T(8,128)S(1)}, f32[64,256]{1,0:T(8,128)S(1)}, u32[]{:S(2)}, u32[]{:S(2)}) collective-permute-start(f32[64,256]{1,0:T(8,128)S(1)} %add_add_fusion.1), channel_id=1, source_target_pairs={{0,128},{16,144},{32,160},{48,176},{64,192},{80,208},{96,224},{112... | collective-permute-start | bytes 196616 | tf_op jit(solution)/shard_map/ppermute | solution.py:304
  112.2 7.9 %collective-permute-start.21 = (f32[64,256]{1,0:T(8,128)S(1)}, f32[64,256]{1,0:T(8,128)S(1)}, u32[]{:S(2)}, u32[]{:S(2)}) collective-permute-start(f32[64,256]{1,0:T(8,128)S(1)} %add.80), channel_id=1, source_target_pairs={{0,1},{1,0},{2,3},{3,2},{4,5},{5,4},{6,7},{7,6},{8,9},{9,8},{10,11... | collective-permute-start | bytes 196616 | tf_op jit(solution)/shard_map/ppermute | solution.py:304
  112.3 8.5 %collective-permute-start.22 = (f32[64,256]{1,0:T(8,128)S(1)}, f32[64,256]{1,0:T(8,128)S(1)}, u32[]{:S(2)}, u32[]{:S(2)}) collective-permute-start(f32[64,256]{1,0:T(8,128)S(1)} %add.80), channel_id=1, source_target_pairs={{0,2},{1,3},{2,0},{3,1},{4,6},{5,7},{6,4},{7,5},{8,10},{9,11},{10,... | collective-permute-start | bytes 196616 | tf_op jit(solution)/shard_map/ppermute | solution.py:304
  115.8 6.5 %collective-permute-start.23 = (f32[64,256]{1,0:T(8,128)S(1)}, f32[64,256]{1,0:T(8,128)S(1)}, u32[]{:S(2)}, u32[]{:S(2)}) collective-permute-start(f32[64,256]{1,0:T(8,128)S(1)} %add.80), channel_id=1, source_target_pairs={{0,3},{1,2},{2,1},{3,0},{4,7},{5,6},{6,5},{7,4},{8,11},{9,10},{10,... | collective-permute-start | bytes 196616 | tf_op jit(solution)/shard_map/ppermute | solution.py:304
  118.8 33.5 %collective-permute-start.9 = (f32[2,256,512]{2,1,0:T(8,128)}, f32[2,256,512]{2,1,0:T(8,128)S(1)}, u32[]{:S(2)}, u32[]{:S(2)}) collective-permute-start(f32[2,256,512]{2,1,0:T(8,128)} %get-tuple-element.37), channel_id=1, source_target_pairs={{0,16},{16,32},{32,48},{48,64},{64,80},{80,96},{96,112},{112,128},... | collective-permute-start | bytes 3145736 | tf_op jit(solution)/shard_map/ppermute | solution.py:20
  122.3 29.9 %copy-start.4 = (f32[2,512,512]{2,1,0:T(8,128)S(1)}, f32[2,512,512]{2,1,0:T(8,128)}, u32[]{:S(2)}) copy-start(f32[2,512,512]{2,1,0:T(8,128)} %get-tuple-element.36) | copy-start | bytes 6291460
  122.3 6.8 %collective-permute-start.24 = (f32[64,256]{1,0:T(8,128)S(1)}, f32[64,256]{1,0:T(8,128)S(1)}, u32[]{:S(2)}, u32[]{:S(2)}) collective-permute-start(f32[64,256]{1,0:T(8,128)S(1)} %get-tuple-element.43), channel_id=1, source_target_pairs={{0,32},{16,48},{32,0},{48,16},{64,96},{80,112},{96,64},{112,80},{1... | collective-permute-start | bytes 196616 | tf_op jit(solution)/shard_map/ppermute | solution.py:304
  122.7 23.7 %collective-permute-start.10 = (f32[2,256,256]{2,1,0:T(8,128)S(1)}, f32[2,256,256]{2,1,0:T(8,128)S(1)}, u32[]{:S(2)}, u32[]{:S(2)}) collective-permute-start(f32[2,256,256]{2,1,0:T(8,128)S(1)} %copy-done.2), channel_id=1, source_target_pairs={{0,16},{16,32},{32,48},{48,64},{64,80},{80,96},{96,112},{112,128},... | collective-permute-start | bytes 1572872 | tf_op jit(solution)/shard_map/ppermute | solution.py:20
  124.1 6.8 %collective-permute-start.25 = (f32[64,256]{1,0:T(8,128)S(1)}, f32[64,256]{1,0:T(8,128)S(1)}, u32[]{:S(2)}, u32[]{:S(2)}) collective-permute-start(f32[64,256]{1,0:T(8,128)S(1)} %get-tuple-element.43), channel_id=1, source_target_pairs={{0,64},{16,80},{32,96},{48,112},{64,0},{80,16},{96,32},{112,48},{1... | collective-permute-start | bytes 196616 | tf_op jit(solution)/shard_map/ppermute | solution.py:304
  128.0 5.5 %collective-permute-start.26 = (f32[64,256]{1,0:T(8,128)S(1)}, f32[64,256]{1,0:T(8,128)S(1)}, u32[]{:S(2)}, u32[]{:S(2)}) collective-permute-start(f32[64,256]{1,0:T(8,128)S(1)} %get-tuple-element.43), channel_id=1, source_target_pairs={{0,96},{16,112},{32,64},{48,80},{64,32},{80,48},{96,0},{112,16},{1... | collective-permute-start | bytes 196616 | tf_op jit(solution)/shard_map/ppermute | solution.py:304
  133.5 17.9 %collective-permute-start.27 = (f32[256,256]{1,0:T(8,128)S(1)}, f32[256,256]{1,0:T(8,128)S(1)}, u32[]{:S(2)}, u32[]{:S(2)}) collective-permute-start(f32[256,256]{1,0:T(8,128)S(1)} %constant_dynamic-update-slice_fusion), channel_id=1, source_target_pairs={{0,16},{16,0},{32,48},{48,32},{64,80},{80,64},{96,112},{112,96},{1... | collective-permute-start | bytes 786440 | tf_op jit(solution)/shard_map/ppermute | solution.py:304
  144.2 19.8 %collective-permute-start.12 = (f32[2,256,256]{2,1,0:T(8,128)S(1)}, f32[2,256,256]{2,1,0:T(8,128)S(1)}, u32[]{:S(2)}, u32[]{:S(2)}) collective-permute-start(f32[2,256,256]{2,1,0:T(8,128)S(1)} %get-tuple-element.40), channel_id=1, source_target_pairs={{0,1},{1,2},{2,3},{3,4},{4,5},{5,6},{6,7},{7,8},{8,9},{9,10},{10,1... | collective-permute-start | bytes 1572872 | tf_op jit(solution)/shard_map/ppermute | solution.py:20
  146.4 50.2 %collective-permute-start.11 = (f32[2,256,256]{2,1,0:T(8,128)S(1)}, f32[2,256,256]{2,1,0:T(8,128)S(1)}, u32[]{:S(2)}, u32[]{:S(2)}) collective-permute-start(f32[2,256,256]{2,1,0:T(8,128)S(1)} %add.67), channel_id=1, source_target_pairs={{0,1},{1,2},{2,3},{3,4},{4,5},{5,6},{6,7},{7,8},{8,9},{9,10},{10,1... | collective-permute-start | bytes 1572872 | tf_op jit(solution)/shard_map/ppermute | solution.py:20
  (4 other events, 8.6 us)

commit v7 on v5

--- a/solution.py
+++ b/solution.py
@@ -239,7 +239,7 @@
         running = [patch for patch in running if next(patch, running) is None]
 
 
-def patches_kernel(off, tile, upper, middle, lower, bottom, corner, probe, amp, left_table, right_table,
+def patches_kernel(off, tile, upper, middle, lower, bottom, deeper, relayed, corner, probe, amp, left_table, right_table,
                    main_out, upper_out, lower_out, bottom_out, corner_out, probe_out, ext, grad, *scratch, scale):
     side = upper.shape[2]
     rows, cols = tile.shape[1], tile.shape[2]
@@ -252,7 +252,8 @@
         ext[:, :side, cols:] = upper[...]
         ext[:, side:cut, cols:] = middle[...]
         ext[:, cut:rows, cols:] = lower[...]
-        ext[:, rows:, :cols] = bottom[...]
+        ext[:, rows:rows + side // 2, :cols] = bottom[...]
+        ext[:, rows + side // 2:, :cols] = deeper[...] + relayed[...]
         ext[:, rows:, cols:] = corner[...]
         grad[...] = jnp.zeros_like(grad)
         probe_out[...] = jnp.zeros_like(probe_out)
@@ -273,7 +274,7 @@
         probe_out[...] *= scale
 
 
-def all_patches(off, tile, upper, middle, lower, bottom, corner, probe, amp, scale):
+def all_patches(off, tile, upper, middle, lower, bottom, deeper, relayed, corner, probe, amp, scale):
     count, side = amp.shape[0], upper.shape[2]
     together = 2 if count % 2 == 0 else 1
     rows, cols = tile.shape[1], tile.shape[2]
@@ -287,14 +288,14 @@
         grid=(count // together,),
         out_shape=(shape(2, rows, cols), shape(2, side, side), shape(2, rows - side, side), shape(2, side, cols),
                    shape(2, side, side), shape(2, side, side)),
-        in_specs=[pl.BlockSpec(memory_space=pltpu.SMEM)] + [vmem] * 6
+        in_specs=[pl.BlockSpec(memory_space=pltpu.SMEM)] + [vmem] * 8
                  + [pl.BlockSpec((together, 2, side, side), lambda i: (i, 0, 0, 0)),
                     pl.BlockSpec((together, 2, side, side // 2), lambda i: (i, 0, 0, 0))] + [vmem] * 2,
         out_specs=[vmem] * 6,
         scratch_shapes=[pltpu.VMEM((2, rows + side, cols + side), F32)] * 2
                      + [pltpu.VMEM((together, 2, side, side), F32)] + [pltpu.VMEM((together, 2, side, side), BF16)] * 4,
         compiler_params=pltpu.CompilerParams(vmem_limit_bytes=50 * 1024 * 1024),
-    )(off, tile, upper, middle, lower, bottom, corner, probes, amps, *tables)
+    )(off, tile, upper, middle, lower, bottom, deeper, relayed, corner, probes, amps, *tables)
 
 
 ACROSS, LINES = (2, 4, 6), (4, 8, 12)
@@ -375,17 +376,26 @@
     return lax.ppermute(value, "col", pairs)
 
 
+def deeper_rows(value):
+    count = lax.axis_size("row")
+    half = count // 2
+    relayed = lax.ppermute(value, "row", [(half, count - 2)])
+    deeper = lax.ppermute(value, "row", [(i, i - 1) for i in range(1, count) if i != half])
+    return deeper, lax.ppermute(relayed, "row", [(count - 2, half - 1)])
+
+
 def shards_body(object_field, probe, amplitude, offsets):
     side = probe.shape[1]
     cut = object_field.shape[1] - side // 2
     lower = long_way(object_field[:, cut:, :side])
     upper = passed_along(object_field[:, :side, :side], "col", -1)
     middle = passed_along(object_field[:, side:cut, :side], "col", -1)
-    bottom = passed_along(object_field[:, :side, :], "row", -1)
+    bottom = passed_along(object_field[:, :side // 2, :], "row", -1)
+    deeper, relayed = deeper_rows(object_field[:, side // 2:side, :])
     corner = passed_along(upper, "row", -1)
     count = amplitude.shape[2] * lax.axis_size("row") * lax.axis_size("col")
     main, upper, lower, bottom, corner, probe_acc = all_patches(
-        offsets[0, 0], object_field, upper, middle, lower, bottom, corner, probe, amplitude[0, 0], 1.0 / count)
+        offsets[0, 0], object_field, upper, middle, lower, bottom, deeper, relayed, corner, probe, amplitude[0, 0], 1.0 / count)
     corner_back = passed_along(corner, "row", 1)
     lower_back = passed_along(lower, "col", 1)
     bottom_back = passed_along(bottom, "row", 1)

time: 187 us -> 205 us (1.096)
  the two profiles are of different devices: /device:TPU:49 before, /device:TPU:24 now
where the time goes in v7:
time: 205 us
  waiting for transfers between devices  98.4 us (48%)
  starting transfers between devices  73.4 us (36%)
  Pallas kernels  24 us (12%)
  local copies, waits for them, and re-layouts  6.44 us (3%)
    ppermute x8, waiting for transfers between devices, passed_along(): lax.ppermute(value, axis, [(source, source + steps) for source in range(f...  61.1 us
    ppermute x15, starting transfers between devices, exchanged(): lax.ppermute(piece, axis, [(i, i ^ distance) for i in range(lax.axis_size...  35.4 us
    ppermute x8, starting transfers between devices, passed_along(): lax.ppermute(value, axis, [(source, source + steps) for source in range(f...  27.1 us
    ppermute x15, waiting for transfers between devices, exchanged(): lax.ppermute(piece, axis, [(i, i ^ distance) for i in range(lax.axis_size...  20.6 us
    ppermute x2, waiting for transfers between devices, round_ring(): lax.ppermute(value, 'col', [(i, i // 4 * 4 + (i + step) % 4) for i in ran...  16.7 us
    pallas_call x1, Pallas kernels, all_patches(): pl.pallas_call(functools.partial(patches_kernel, scale=scale), grid=(coun...  15.9 us
    pallas_call x1, Pallas kernels, prepare(): pl.pallas_call(prepare_kernel, grid=(count,), out_shape=(jax.ShapeDtypeSt...  8.18 us
    ppermute x1, starting transfers between devices, long_way(): return lax.ppermute(value, 'col', pairs)  5.28 us
  transfers between devices with their start and end apart: 29, of which 15 were waited for; matrix products, arithmetic and copies ran while one was open for 1% of the time, Pallas kernels for 4%

profile of v7, /device:TPU:24, one launch (start us, length us, event | category | flops | bytes accessed | tf_op | source)
XLA Modules:
  0.0 204.9 jit_solution(1539951876571545782)
XLA Ops:
  0.7 2.4 %fusion.1 = (f32[2,128,512]{2,1,0:T(8,128)}, f32[2,128,512]{2,1,0:T(8,128)}) fusion(f32[2,512,512]{2,1,0:T(8,128)} %tile.1), kind=kLoop, calls=%fused_computation.18 | loop fusion | bytes 2097152 | tf_op jit(solution)/shard_map/slice | solution.py:394
  3.0 1.5 collective-permute-start.7
  4.6 8.4 %collective-permute-start = (f32[2,256,256]{2,1,0:T(8,128)S(1)}, f32[2,256,256]{2,1,0:T(8,128)S(1)}, u32[]{:S(2)}, u32[]{:S(2)}) collective-permute-start(f32[2,256,256]{2,1,0:T(8,128)S(1)} %slice.71), channel_id=1, source_target_pairs={{1,0},{2,1},{3,2},{4,3},{5,4},{6,5},{7,6},{8,7},{9,8},{10,9},{11,1... | collective-permute-start | bytes 1572872 | tf_op jit(solution)/shard_map/ppermute | solution.py:20
  13.1 5.9 %collective-permute-start.1 = (f32[2,128,256]{2,1,0:T(8,128)S(1)}, f32[2,128,256]{2,1,0:T(8,128)S(1)}, u32[]{:S(2)}, u32[]{:S(2)}) collective-permute-start(f32[2,128,256]{2,1,0:T(8,128)S(1)} %get-tuple-element.47), channel_id=1, source_target_pairs={{1,0},{2,1},{3,2},{4,3},{5,4},{6,5},{7,6},{8,7},{9,8},{10,9},{11,1... | collective-permute-start | bytes 786440 | tf_op jit(solution)/shard_map/ppermute | solution.py:20
  20.3 7.8 %collective-permute-done.2 = f32[2,128,256]{2,1,0:T(8,128)S(1)} collective-permute-done((f32[2,128,256]{2,1,0:T(8,128)S(1)}, f32[2,128,256]{2,1,0:T(8,128)S(1)}, u32[]{:S(2)}, u32[]{:S(2)}) %collective-permute-start.2) | collective-permute-done | bytes 262176 | tf_op jit(solution)/shard_map/ppermute | solution.py:349
  29.4 17.2 %collective-permute-done.1.middle = f32[2,128,256]{2,1,0:T(8,128)S(1)} collective-permute-done((f32[2,128,256]{2,1,0:T(8,128)S(1)}, f32[2,128,256]{2,1,0:T(8,128)S(1)}, u32[]{:S(2)}, u32[]{:S(2)}) %collective-permute-start.1) | collective-permute-done | bytes 262176 | tf_op jit(solution)/shard_map/ppermute | solution.py:20
  46.6 2.1 %collective-permute-start.3 = (f32[2,128,256]{2,1,0:T(8,128)S(1)}, f32[2,128,256]{2,1,0:T(8,128)S(1)}, u32[]{:S(2)}, u32[]{:S(2)}) collective-permute-start(f32[2,128,256]{2,1,0:T(8,128)S(1)} %collective-permute-done.2), channel_id=1, source_target_pairs={{0,1},{1,2},{2,3},{3,0},{4,5},{5,6},{6,7},{7,4},{8,9},{9,10},{10,1... | collective-permute-start | bytes 786440 | tf_op jit(solution)/shard_map/ppermute | solution.py:349
  50.7 8.9 %collective-permute-done.3 = f32[2,128,256]{2,1,0:T(8,128)S(1)} collective-permute-done((f32[2,128,256]{2,1,0:T(8,128)S(1)}, f32[2,128,256]{2,1,0:T(8,128)S(1)}, u32[]{:S(2)}, u32[]{:S(2)}) %collective-permute-start.3) | collective-permute-done | bytes 262176 | tf_op jit(solution)/shard_map/ppermute | solution.py:349
  59.6 5.3 %collective-permute-start.4 = (f32[2,128,256]{2,1,0:T(8,128)S(1)}, f32[2,128,256]{2,1,0:T(8,128)S(1)}, u32[]{:S(2)}, u32[]{:S(2)}) collective-permute-start(f32[2,128,256]{2,1,0:T(8,128)S(1)} %collective-permute-done.3), channel_id=1, source_target_pairs={{0,1},{1,2},{3,0},{4,5},{5,6},{6,3},{7,4},{8,9},{9,10},{10,7},{11,... | collective-permute-start | bytes 786440 | tf_op jit(solution)/shard_map/ppermute | solution.py:376
  65.6 8.2 %shard_map.86 = (f32[8,2,256,128]{3,2,1,0:T(8,128)}, f32[8,2,256,256]{3,2,1,0:T(8,128)}) custom-call(s32[8,2]{1,0:T(8,128)} %copy.10.off, f32[8,256,256]{2,1,0:T(8,128)} %bitcast.7, f32[2,256,256]{2,1,0:T(8,128)} %probe.1, bf16[2,256,256]{2,1,0:T(8,128)(2,1)} %constant.78.clone.pick), custom_call_target="tpu_custom_call" | custom-call | tf_op jit(solution)/shard_map/pallas_call | solution.py:96
  75.0 15.9 %shard_map.87 = (f32[2,512,512]{2,1,0:T(8,128)}, f32[2,256,256]{2,1,0:T(8,128)S(1)}, f32[2,256,256]{2,1,0:T(8,128)S(1)}, f32[2,256,512]{2,1,0:T(8,128)}, f32[2,2...) custom-call(s32[8,2]{1,0:T(8,128)S(1)} %copy-done, f32[2,512,512]{2,1,0:T(8,128)} %tile.1, ...), custom_call_target="tpu_custom_call" | custom-call | tf_op jit(solution)/shard_map/pallas_call | solution.py:286
  91.8 1.5 collective-permute-done.14
  94.7 2.9 %collective-permute-start.16 = (f32[64,256]{1,0:T(8,128)S(1)}, f32[64,256]{1,0:T(8,128)S(1)}, u32[]{:S(2)}, u32[]{:S(2)}) collective-permute-start(f32[64,256]{1,0:T(8,128)S(1)} %get-tuple-element.52), channel_id=1, source_target_pairs={{0,64},{16,80},{32,96},{48,112},{64,0},{80,16},{96,32},{112,48},{1... | collective-permute-start | bytes 196616 | tf_op jit(solution)/shard_map/ppermute | solution.py:305
  98.2 2.9 %collective-permute-done.16 = f32[64,256]{1,0:T(8,128)S(1)} collective-permute-done((f32[64,256]{1,0:T(8,128)S(1)}, f32[64,256]{1,0:T(8,128)S(1)}, u32[]{:S(2)}, u32[]{:S(2)}) %collective-permute-start.16) | collective-permute-done | bytes 65568 | tf_op jit(solution)/shard_map/ppermute | solution.py:305
  101.1 2.0 collective-permute-done.17
  103.0 4.6 %collective-permute-start.18 = (f32[64,256]{1,0:T(8,128)S(1)}, f32[64,256]{1,0:T(8,128)S(1)}, u32[]{:S(2)}, u32[]{:S(2)}) collective-permute-start(f32[64,256]{1,0:T(8,128)S(1)} %add_add_fusion.2), channel_id=1, source_target_pairs={{0,4},{1,5},{2,6},{3,7},{4,0},{5,1},{6,2},{7,3},{8,12},{9,13},{10,... | collective-permute-start | bytes 196616 | tf_op jit(solution)/shard_map/ppermute | solution.py:305
  107.7 2.0 collective-permute-start.19
  110.4 3.0 %collective-permute-done.19 = f32[64,256]{1,0:T(8,128)S(1)} collective-permute-done((f32[64,256]{1,0:T(8,128)S(1)}, f32[64,256]{1,0:T(8,128)S(1)}, u32[]{:S(2)}, u32[]{:S(2)}) %collective-permute-start.19) | collective-permute-done | bytes 65568 | tf_op jit(solution)/shard_map/ppermute | solution.py:305
  113.4 1.7 collective-permute-done.20
  115.6 3.9 %collective-permute-done.21 = f32[64,256]{1,0:T(8,128)S(1)} collective-permute-done((f32[64,256]{1,0:T(8,128)S(1)}, f32[64,256]{1,0:T(8,128)S(1)}, u32[]{:S(2)}, u32[]{:S(2)}) %collective-permute-start.21) | collective-permute-done | bytes 65568 | tf_op jit(solution)/shard_map/ppermute | solution.py:305
  119.6 2.1 %collective-permute-start.23 = (f32[64,256]{1,0:T(8,128)S(1)}, f32[64,256]{1,0:T(8,128)S(1)}, u32[]{:S(2)}, u32[]{:S(2)}) collective-permute-start(f32[64,256]{1,0:T(8,128)S(1)} %add.80), channel_id=1, source_target_pairs={{0,2},{1,3},{2,0},{3,1},{4,6},{5,7},{6,4},{7,5},{8,10},{9,11},{10,... | collective-permute-start | bytes 196616 | tf_op jit(solution)/shard_map/ppermute | solution.py:305
  121.7 4.4 %collective-permute-start.24 = (f32[64,256]{1,0:T(8,128)S(1)}, f32[64,256]{1,0:T(8,128)S(1)}, u32[]{:S(2)}, u32[]{:S(2)}) collective-permute-start(f32[64,256]{1,0:T(8,128)S(1)} %add.80), channel_id=1, source_target_pairs={{0,3},{1,2},{2,1},{3,0},{4,7},{5,6},{6,5},{7,4},{8,11},{9,10},{10,... | collective-permute-start | bytes 196616 | tf_op jit(solution)/shard_map/ppermute | solution.py:305
  126.1 1.3 collective-permute-start.10
  130.0 1.5 collective-permute-start.11
  131.5 3.1 %collective-permute-start.26 = (f32[64,256]{1,0:T(8,128)S(1)}, f32[64,256]{1,0:T(8,128)S(1)}, u32[]{:S(2)}, u32[]{:S(2)}) collective-permute-start(f32[64,256]{1,0:T(8,128)S(1)} %get-tuple-element.43), channel_id=1, source_target_pairs={{0,64},{16,80},{32,96},{48,112},{64,0},{80,16},{96,32},{112,48},{1... | collective-permute-start | bytes 196616 | tf_op jit(solution)/shard_map/ppermute | solution.py:305
  134.5 2.2 %collective-permute-start.27 = (f32[64,256]{1,0:T(8,128)S(1)}, f32[64,256]{1,0:T(8,128)S(1)}, u32[]{:S(2)}, u32[]{:S(2)}) collective-permute-start(f32[64,256]{1,0:T(8,128)S(1)} %get-tuple-element.43), channel_id=1, source_target_pairs={{0,96},{16,112},{32,64},{48,80},{64,32},{80,48},{96,0},{112,16},{1... | collective-permute-start | bytes 196616 | tf_op jit(solution)/shard_map/ppermute | solution.py:305
  138.1 2.0 collective-permute-done.27
  140.0 10.8 %collective-permute-start.28 = (f32[256,256]{1,0:T(8,128)S(1)}, f32[256,256]{1,0:T(8,128)S(1)}, u32[]{:S(2)}, u32[]{:S(2)}) collective-permute-start(f32[256,256]{1,0:T(8,128)S(1)} %constant_dynamic-update-slice_fusion), channel_id=1, source_target_pairs={{0,16},{16,0},{32,48},{48,32},{64,80},{80,64},{96,112},{112,96},{1... | collective-permute-start | bytes 786440 | tf_op jit(solution)/shard_map/ppermute | solution.py:305
  150.8 2.2 %collective-permute-start.13 = (f32[2,256,256]{2,1,0:T(8,128)S(1)}, f32[2,256,256]{2,1,0:T(8,128)S(1)}, u32[]{:S(2)}, u32[]{:S(2)}) collective-permute-start(f32[2,256,256]{2,1,0:T(8,128)S(1)} %get-tuple-element.40), channel_id=1, source_target_pairs={{0,1},{1,2},{2,3},{3,4},{4,5},{5,6},{6,7},{7,8},{8,9},{9,10},{10,1... | collective-permute-start | bytes 1572872 | tf_op jit(solution)/shard_map/ppermute | solution.py:20
  153.1 5.2 %collective-permute-start.12 = (f32[2,256,256]{2,1,0:T(8,128)S(1)}, f32[2,256,256]{2,1,0:T(8,128)S(1)}, u32[]{:S(2)}, u32[]{:S(2)}) collective-permute-start(f32[2,256,256]{2,1,0:T(8,128)S(1)} %add.67), channel_id=1, source_target_pairs={{0,1},{1,2},{2,3},{3,4},{4,5},{5,6},{6,7},{7,8},{8,9},{9,10},{10,1... | collective-permute-start | bytes 1572872 | tf_op jit(solution)/shard_map/ppermute | solution.py:20
  159.5 11.4 %collective-permute-done.13 = f32[2,256,256]{2,1,0:T(8,128)S(1)} collective-permute-done((f32[2,256,256]{2,1,0:T(8,128)S(1)}, f32[2,256,256]{2,1,0:T(8,128)S(1)}, u32[]{:S(2)}, u32[]{:S(2)}) %collective-permute-start.13) | collective-permute-done | bytes 524320 | tf_op jit(solution)/shard_map/ppermute | solution.py:20
  170.9 32.4 %collective-permute-done.12 = f32[2,256,256]{2,1,0:T(8,128)S(1)} collective-permute-done((f32[2,256,256]{2,1,0:T(8,128)S(1)}, f32[2,256,256]{2,1,0:T(8,128)S(1)}, u32[]{:S(2)}, u32[]{:S(2)}) %collective-permute-start.12) | collective-permute-done | bytes 524320 | tf_op jit(solution)/shard_map/ppermute | solution.py:20
  (68 shorter events, 17.5 us)
Async XLA Ops:
  0.6 64.3 %copy-start.9 = (s32[1,1,8,2]{2,3,1,0:T(2,128)S(1)}, s32[1,1,8,2]{2,3,1,0:T(2,128)}, u32[]{:S(2)}) copy-start(s32[1,1,8,2]{2,3,1,0:T(2,128)} %param.14) | copy-start | bytes 196
  3.0 45.7 %collective-permute-start.7 = (f32[2,128,512]{2,1,0:T(8,128)}, f32[2,128,512]{2,1,0:T(8,128)}, u32[]{:S(2)}, u32[]{:S(2)}) collective-permute-start(f32[2,128,512]{2,1,0:T(8,128)} %get-tuple-element.44), channel_id=1, source_target_pairs={{128,224},{129,225},{130,226},{131,227},{132,228},{133,229},{134,2... | collective-permute-start | bytes 1572872 | tf_op jit(solution)/shard_map/ppermute | solution.py:382
  4.6 44.8 %collective-permute-start = (f32[2,256,256]{2,1,0:T(8,128)S(1)}, f32[2,256,256]{2,1,0:T(8,128)S(1)}, u32[]{:S(2)}, u32[]{:S(2)}) collective-permute-start(f32[2,256,256]{2,1,0:T(8,128)S(1)} %slice.71), channel_id=1, source_target_pairs={{1,0},{2,1},{3,2},{4,3},{5,4},{6,5},{7,6},{8,7},{9,8},{10,9},{11,1... | collective-permute-start | bytes 1572872 | tf_op jit(solution)/shard_map/ppermute | solution.py:20
  13.0 15.1 %collective-permute-start.2 = (f32[2,128,256]{2,1,0:T(8,128)S(1)}, f32[2,128,256]{2,1,0:T(8,128)S(1)}, u32[]{:S(2)}, u32[]{:S(2)}) collective-permute-start(f32[2,128,256]{2,1,0:T(8,128)S(1)} %get-tuple-element.46), channel_id=1, source_target_pairs={{0,1},{1,2},{2,3},{3,0},{4,5},{5,6},{6,7},{7,4},{8,9},{9,10},{10,1... | collective-permute-start | bytes 786440 | tf_op jit(solution)/shard_map/ppermute | solution.py:349
  13.1 33.5 %collective-permute-start.1 = (f32[2,128,256]{2,1,0:T(8,128)S(1)}, f32[2,128,256]{2,1,0:T(8,128)S(1)}, u32[]{:S(2)}, u32[]{:S(2)}) collective-permute-start(f32[2,128,256]{2,1,0:T(8,128)S(1)} %get-tuple-element.47), channel_id=1, source_target_pairs={{1,0},{2,1},{3,2},{4,3},{5,4},{6,5},{7,6},{8,7},{9,8},{10,9},{11,1... | collective-permute-start | bytes 786440 | tf_op jit(solution)/shard_map/ppermute | solution.py:20
  19.0 54.8 %collective-permute-start.6 = (f32[2,128,512]{2,1,0:T(8,128)}, f32[2,128,512]{2,1,0:T(8,128)S(1)}, u32[]{:S(2)}, u32[]{:S(2)}) collective-permute-start(f32[2,128,512]{2,1,0:T(8,128)} %get-tuple-element.44), channel_id=1, source_target_pairs={{16,0},{32,16},{48,32},{64,48},{80,64},{96,80},{112,96},{144,128},... | collective-permute-start | bytes 1572872 | tf_op jit(solution)/shard_map/ppermute | solution.py:383
  28.1 45.7 %collective-permute-start.5 = (f32[2,128,512]{2,1,0:T(8,128)}, f32[2,128,512]{2,1,0:T(8,128)S(1)}, u32[]{:S(2)}, u32[]{:S(2)}) collective-permute-start(f32[2,128,512]{2,1,0:T(8,128)} %get-tuple-element.45), channel_id=1, source_target_pairs={{16,0},{32,16},{48,32},{64,48},{80,64},{96,80},{112,96},{128,112},... | collective-permute-start | bytes 1572872 | tf_op jit(solution)/shard_map/ppermute | solution.py:20
  46.6 13.0 %collective-permute-start.3 = (f32[2,128,256]{2,1,0:T(8,128)S(1)}, f32[2,128,256]{2,1,0:T(8,128)S(1)}, u32[]{:S(2)}, u32[]{:S(2)}) collective-permute-start(f32[2,128,256]{2,1,0:T(8,128)S(1)} %collective-permute-done.2), channel_id=1, source_target_pairs={{0,1},{1,2},{2,3},{3,0},{4,5},{5,6},{6,7},{7,4},{8,9},{9,10},{10,1... | collective-permute-start | bytes 786440 | tf_op jit(solution)/shard_map/ppermute | solution.py:349
  48.7 25.1 %collective-permute-start.8 = (f32[2,128,512]{2,1,0:T(8,128)}, f32[2,128,512]{2,1,0:T(8,128)S(1)}, u32[]{:S(2)}, u32[]{:S(2)}) collective-permute-start(f32[2,128,512]{2,1,0:T(8,128)} %collective-permute-done.7), channel_id=1, source_target_pairs={{224,112},{225,113},{226,114},{227,115},{228,116},{229,117},{230,1... | collective-permute-start | bytes 1572872 | tf_op jit(solution)/shard_map/ppermute | solution.py:384
  49.4 24.4 %collective-permute-start.9 = (f32[2,256,256]{2,1,0:T(8,128)S(1)}, f32[2,256,256]{2,1,0:T(8,128)S(1)}, u32[]{:S(2)}, u32[]{:S(2)}) collective-permute-start(f32[2,256,256]{2,1,0:T(8,128)S(1)} %collective-permute-done.upper), channel_id=1, source_target_pairs={{16,0},{32,16},{48,32},{64,48},{80,64},{96,80},{112,96},{128,112},... | collective-permute-start | bytes 1572872 | tf_op jit(solution)/shard_map/ppermute | solution.py:20
  59.6 14.2 %collective-permute-start.4 = (f32[2,128,256]{2,1,0:T(8,128)S(1)}, f32[2,128,256]{2,1,0:T(8,128)S(1)}, u32[]{:S(2)}, u32[]{:S(2)}) collective-permute-start(f32[2,128,256]{2,1,0:T(8,128)S(1)} %collective-permute-done.3), channel_id=1, source_target_pairs={{0,1},{1,2},{3,0},{4,5},{5,6},{6,3},{7,4},{8,9},{9,10},{10,7},{11,... | collective-permute-start | bytes 786440 | tf_op jit(solution)/shard_map/ppermute | solution.py:376
  91.6 38.4 %copy-start.2 = (f32[2,256,256]{2,1,0:T(8,128)S(1)}, f32[2,256,256]{2,1,0:T(8,128)}, u32[]{:S(2)}) copy-start(f32[2,256,256]{2,1,0:T(8,128)} %copy-done.1) | copy-start | bytes 1572868
  91.7 1.6 collective-permute-start.14
  93.4 4.8 %collective-permute-start.15 = (f32[64,256]{1,0:T(8,128)S(1)}, f32[64,256]{1,0:T(8,128)S(1)}, u32[]{:S(2)}, u32[]{:S(2)}) collective-permute-start(f32[64,256]{1,0:T(8,128)S(1)} %get-tuple-element.50), channel_id=1, source_target_pairs={{0,32},{16,48},{32,0},{48,16},{64,96},{80,112},{96,64},{112,80},{1... | collective-permute-start | bytes 196616 | tf_op jit(solution)/shard_map/ppermute | solution.py:305
  94.7 6.4 %collective-permute-start.16 = (f32[64,256]{1,0:T(8,128)S(1)}, f32[64,256]{1,0:T(8,128)S(1)}, u32[]{:S(2)}, u32[]{:S(2)}) collective-permute-start(f32[64,256]{1,0:T(8,128)S(1)} %get-tuple-element.52), channel_id=1, source_target_pairs={{0,64},{16,80},{32,96},{48,112},{64,0},{80,16},{96,32},{112,48},{1... | collective-permute-start | bytes 196616 | tf_op jit(solution)/shard_map/ppermute | solution.py:305
  97.6 5.5 %collective-permute-start.17 = (f32[64,256]{1,0:T(8,128)S(1)}, f32[64,256]{1,0:T(8,128)S(1)}, u32[]{:S(2)}, u32[]{:S(2)}) collective-permute-start(f32[64,256]{1,0:T(8,128)S(1)} %get-tuple-element.51), channel_id=1, source_target_pairs={{0,96},{16,112},{32,64},{48,80},{64,32},{80,48},{96,0},{112,16},{1... | collective-permute-start | bytes 196616 | tf_op jit(solution)/shard_map/ppermute | solution.py:305
  103.0 7.4 %collective-permute-start.18 = (f32[64,256]{1,0:T(8,128)S(1)}, f32[64,256]{1,0:T(8,128)S(1)}, u32[]{:S(2)}, u32[]{:S(2)}) collective-permute-start(f32[64,256]{1,0:T(8,128)S(1)} %add_add_fusion.2), channel_id=1, source_target_pairs={{0,4},{1,5},{2,6},{3,7},{4,0},{5,1},{6,2},{7,3},{8,12},{9,13},{10,... | collective-permute-start | bytes 196616 | tf_op jit(solution)/shard_map/ppermute | solution.py:305
  107.7 5.8 %collective-permute-start.19 = (f32[64,256]{1,0:T(8,128)S(1)}, f32[64,256]{1,0:T(8,128)S(1)}, u32[]{:S(2)}, u32[]{:S(2)}) collective-permute-start(f32[64,256]{1,0:T(8,128)S(1)} %add_add_fusion.2), channel_id=1, source_target_pairs={{0,8},{1,9},{2,10},{3,11},{4,12},{5,13},{6,14},{7,15},{8,0},{9,1},... | collective-permute-start | bytes 196616 | tf_op jit(solution)/shard_map/ppermute | solution.py:305
  109.6 5.5 %collective-permute-start.20 = (f32[64,256]{1,0:T(8,128)S(1)}, f32[64,256]{1,0:T(8,128)S(1)}, u32[]{:S(2)}, u32[]{:S(2)}) collective-permute-start(f32[64,256]{1,0:T(8,128)S(1)} %add_add_fusion.2), channel_id=1, source_target_pairs={{0,12},{1,13},{2,14},{3,15},{4,8},{5,9},{6,10},{7,11},{8,4},{9,5},... | collective-permute-start | bytes 196616 | tf_op jit(solution)/shard_map/ppermute | solution.py:305
  115.1 4.4 %collective-permute-start.21 = (f32[64,256]{1,0:T(8,128)S(1)}, f32[64,256]{1,0:T(8,128)S(1)}, u32[]{:S(2)}, u32[]{:S(2)}) collective-permute-start(f32[64,256]{1,0:T(8,128)S(1)} %add_add_fusion.1), channel_id=1, source_target_pairs={{0,128},{16,144},{32,160},{48,176},{64,192},{80,208},{96,224},{112... | collective-permute-start | bytes 196616 | tf_op jit(solution)/shard_map/ppermute | solution.py:305
  119.5 7.9 %collective-permute-start.22 = (f32[64,256]{1,0:T(8,128)S(1)}, f32[64,256]{1,0:T(8,128)S(1)}, u32[]{:S(2)}, u32[]{:S(2)}) collective-permute-start(f32[64,256]{1,0:T(8,128)S(1)} %add.80), channel_id=1, source_target_pairs={{0,1},{1,0},{2,3},{3,2},{4,5},{5,4},{6,7},{7,6},{8,9},{9,8},{10,11... | collective-permute-start | bytes 196616 | tf_op jit(solution)/shard_map/ppermute | solution.py:305
  119.6 9.2 %collective-permute-start.23 = (f32[64,256]{1,0:T(8,128)S(1)}, f32[64,256]{1,0:T(8,128)S(1)}, u32[]{:S(2)}, u32[]{:S(2)}) collective-permute-start(f32[64,256]{1,0:T(8,128)S(1)} %add.80), channel_id=1, source_target_pairs={{0,2},{1,3},{2,0},{3,1},{4,6},{5,7},{6,4},{7,5},{8,10},{9,11},{10,... | collective-permute-start | bytes 196616 | tf_op jit(solution)/shard_map/ppermute | solution.py:305
  121.7 8.1 %collective-permute-start.24 = (f32[64,256]{1,0:T(8,128)S(1)}, f32[64,256]{1,0:T(8,128)S(1)}, u32[]{:S(2)}, u32[]{:S(2)}) collective-permute-start(f32[64,256]{1,0:T(8,128)S(1)} %add.80), channel_id=1, source_target_pairs={{0,3},{1,2},{2,1},{3,0},{4,7},{5,6},{6,5},{7,4},{8,11},{9,10},{10,... | collective-permute-start | bytes 196616 | tf_op jit(solution)/shard_map/ppermute | solution.py:305
  126.1 33.1 %collective-permute-start.10 = (f32[2,256,512]{2,1,0:T(8,128)}, f32[2,256,512]{2,1,0:T(8,128)S(1)}, u32[]{:S(2)}, u32[]{:S(2)}) collective-permute-start(f32[2,256,512]{2,1,0:T(8,128)} %get-tuple-element.37), channel_id=1, source_target_pairs={{0,16},{16,32},{32,48},{48,64},{64,80},{80,96},{96,112},{112,128},... | collective-permute-start | bytes 3145736 | tf_op jit(solution)/shard_map/ppermute | solution.py:20
  129.9 29.3 %copy-start.4 = (f32[2,512,512]{2,1,0:T(8,128)S(1)}, f32[2,512,512]{2,1,0:T(8,128)}, u32[]{:S(2)}) copy-start(f32[2,512,512]{2,1,0:T(8,128)} %get-tuple-element.36) | copy-start | bytes 6291460
  129.9 6.8 %collective-permute-start.25 = (f32[64,256]{1,0:T(8,128)S(1)}, f32[64,256]{1,0:T(8,128)S(1)}, u32[]{:S(2)}, u32[]{:S(2)}) collective-permute-start(f32[64,256]{1,0:T(8,128)S(1)} %get-tuple-element.43), channel_id=1, source_target_pairs={{0,32},{16,48},{32,0},{48,16},{64,96},{80,112},{96,64},{112,80},{1... | collective-permute-start | bytes 196616 | tf_op jit(solution)/shard_map/ppermute | solution.py:305
  130.0 23.0 %collective-permute-start.11 = (f32[2,256,256]{2,1,0:T(8,128)S(1)}, f32[2,256,256]{2,1,0:T(8,128)S(1)}, u32[]{:S(2)}, u32[]{:S(2)}) collective-permute-start(f32[2,256,256]{2,1,0:T(8,128)S(1)} %copy-done.2), channel_id=1, source_target_pairs={{0,16},{16,32},{32,48},{48,64},{64,80},{80,96},{96,112},{112,128},... | collective-permute-start | bytes 1572872 | tf_op jit(solution)/shard_map/ppermute | solution.py:20
  131.5 6.6 %collective-permute-start.26 = (f32[64,256]{1,0:T(8,128)S(1)}, f32[64,256]{1,0:T(8,128)S(1)}, u32[]{:S(2)}, u32[]{:S(2)}) collective-permute-start(f32[64,256]{1,0:T(8,128)S(1)} %get-tuple-element.43), channel_id=1, source_target_pairs={{0,64},{16,80},{32,96},{48,112},{64,0},{80,16},{96,32},{112,48},{1... | collective-permute-start | bytes 196616 | tf_op jit(solution)/shard_map/ppermute | solution.py:305
  134.5 5.5 %collective-permute-start.27 = (f32[64,256]{1,0:T(8,128)S(1)}, f32[64,256]{1,0:T(8,128)S(1)}, u32[]{:S(2)}, u32[]{:S(2)}) collective-permute-start(f32[64,256]{1,0:T(8,128)S(1)} %get-tuple-element.43), channel_id=1, source_target_pairs={{0,96},{16,112},{32,64},{48,80},{64,32},{80,48},{96,0},{112,16},{1... | collective-permute-start | bytes 196616 | tf_op jit(solution)/shard_map/ppermute | solution.py:305
  140.0 18.3 %collective-permute-start.28 = (f32[256,256]{1,0:T(8,128)S(1)}, f32[256,256]{1,0:T(8,128)S(1)}, u32[]{:S(2)}, u32[]{:S(2)}) collective-permute-start(f32[256,256]{1,0:T(8,128)S(1)} %constant_dynamic-update-slice_fusion), channel_id=1, source_target_pairs={{0,16},{16,0},{32,48},{48,32},{64,80},{80,64},{96,112},{112,96},{1... | collective-permute-start | bytes 786440 | tf_op jit(solution)/shard_map/ppermute | solution.py:305
  150.8 20.1 %collective-permute-start.13 = (f32[2,256,256]{2,1,0:T(8,128)S(1)}, f32[2,256,256]{2,1,0:T(8,128)S(1)}, u32[]{:S(2)}, u32[]{:S(2)}) collective-permute-start(f32[2,256,256]{2,1,0:T(8,128)S(1)} %get-tuple-element.40), channel_id=1, source_target_pairs={{0,1},{1,2},{2,3},{3,4},{4,5},{5,6},{6,7},{7,8},{8,9},{9,10},{10,1... | collective-permute-start | bytes 1572872 | tf_op jit(solution)/shard_map/ppermute | solution.py:20
  153.1 50.3 %collective-permute-start.12 = (f32[2,256,256]{2,1,0:T(8,128)S(1)}, f32[2,256,256]{2,1,0:T(8,128)S(1)}, u32[]{:S(2)}, u32[]{:S(2)}) collective-permute-start(f32[2,256,256]{2,1,0:T(8,128)S(1)} %add.67), channel_id=1, source_target_pairs={{0,1},{1,2},{2,3},{3,4},{4,5},{5,6},{6,7},{7,8},{8,9},{9,10},{10,1... | collective-permute-start | bytes 1572872 | tf_op jit(solution)/shard_map/ppermute | solution.py:20
  (7 other events, 18.3 us)

commit v8 on v7

--- a/solution.py
+++ b/solution.py
@@ -240,7 +240,7 @@
 
 
 def patches_kernel(off, tile, upper, middle, lower, bottom, deeper, relayed, corner, probe, amp, left_table, right_table,
-                   main_out, upper_out, lower_out, bottom_out, corner_out, probe_out, ext, grad, *scratch, scale):
+                   main_out, upper_out, lower_out, bottom_out, deeper_out, corner_out, probe_out, ext, grad, *scratch, scale):
     side = upper.shape[2]
     rows, cols = tile.shape[1], tile.shape[2]
     cut = rows - lower.shape[1]
@@ -269,7 +269,8 @@
         main_out[...] = grad[:, :rows, :cols]
         upper_out[...] = grad[:, :side, cols:]
         lower_out[...] = grad[:, side:rows, cols:]
-        bottom_out[...] = grad[:, rows:, :cols]
+        bottom_out[...] = grad[:, rows:rows + side // 2, :cols]
+        deeper_out[...] = grad[:, rows + side // 2:, :cols]
         corner_out[...] = grad[:, rows:, cols:]
         probe_out[...] *= scale
 
@@ -286,12 +287,13 @@
     return pl.pallas_call(
         functools.partial(patches_kernel, scale=scale),
         grid=(count // together,),
-        out_shape=(shape(2, rows, cols), shape(2, side, side), shape(2, rows - side, side), shape(2, side, cols),
+        out_shape=(shape(2, rows, cols), shape(2, side, side), shape(2, rows - side, side),
+                   shape(2, side // 2, cols), shape(2, side // 2, cols),
                    shape(2, side, side), shape(2, side, side)),
         in_specs=[pl.BlockSpec(memory_space=pltpu.SMEM)] + [vmem] * 8
                  + [pl.BlockSpec((together, 2, side, side), lambda i: (i, 0, 0, 0)),
                     pl.BlockSpec((together, 2, side, side // 2), lambda i: (i, 0, 0, 0))] + [vmem] * 2,
-        out_specs=[vmem] * 6,
+        out_specs=[vmem] * 7,
         scratch_shapes=[pltpu.VMEM((2, rows + side, cols + side), F32)] * 2
                      + [pltpu.VMEM((together, 2, side, side), F32)] + [pltpu.VMEM((together, 2, side, side), BF16)] * 4,
         compiler_params=pltpu.CompilerParams(vmem_limit_bytes=50 * 1024 * 1024),
@@ -384,6 +386,14 @@
     return deeper, lax.ppermute(relayed, "row", [(count - 2, half - 1)])
 
 
+def deeper_returned(value):
+    count = lax.axis_size("row")
+    half = count // 2
+    relayed = lax.ppermute(value, "row", [(half - 1, 1)])
+    deeper = lax.ppermute(value, "row", [(i, i + 1) for i in range(count - 1) if i != half - 1])
+    return deeper + lax.ppermute(relayed, "row", [(1, half)])
+
+
 def shards_body(object_field, probe, amplitude, offsets):
     side = probe.shape[1]
     cut = object_field.shape[1] - side // 2
@@ -394,15 +404,17 @@
     deeper, relayed = deeper_rows(object_field[:, side // 2:side, :])
     corner = passed_along(upper, "row", -1)
     count = amplitude.shape[2] * lax.axis_size("row") * lax.axis_size("col")
-    main, upper, lower, bottom, corner, probe_acc = all_patches(
+    main, upper, lower, bottom, deeper, corner, probe_acc = all_patches(
         offsets[0, 0], object_field, upper, middle, lower, bottom, deeper, relayed, corner, probe, amplitude[0, 0], 1.0 / count)
     corner_back = passed_along(corner, "row", 1)
     lower_back = passed_along(lower, "col", 1)
     bottom_back = passed_along(bottom, "row", 1)
+    deeper_back = deeper_returned(deeper)
     upper_back = passed_along(upper + corner_back, "col", 1)
     probe_total = summed_everywhere(probe_acc)
     right_back = jnp.concatenate([upper_back, lower_back], axis=1)
-    main = main.at[:, :side, :].add(bottom_back)
+    below = jnp.concatenate([bottom_back, deeper_back], axis=1)
+    main = main.at[:, :side, :].add(below)
     object_grad = main.at[:, :, :side].add(right_back)
     return (object_grad, probe_total)
 

time: 205 us -> 210 us (1.024)
  the two profiles are of different devices: /device:TPU:24 before, /device:TPU:31 now
where the time goes in v8:
time: 210 us; the launch traced here: 206 us
  starting transfers between devices  93.3 us (44%)
  waiting for transfers between devices  78.1 us (37%)
  Pallas kernels  23.9 us (11%)
  local copies, waits for them, and re-layouts  6.7 us (3%)
  other arithmetic  2.67 us (1%)
    ppermute x8, waiting for transfers between devices, passed_along(): lax.ppermute(value, axis, [(source, source + steps) for source in range(f...  55.9 us
    ppermute x8, starting transfers between devices, passed_along(): lax.ppermute(value, axis, [(source, source + steps) for source in range(f...  48.6 us
    ppermute x15, starting transfers between devices, exchanged(): lax.ppermute(piece, axis, [(i, i ^ distance) for i in range(lax.axis_size...  24.7 us
    ppermute x15, waiting for transfers between devices, exchanged(): lax.ppermute(piece, axis, [(i, i ^ distance) for i in range(lax.axis_size...  18.4 us
    pallas_call x1, Pallas kernels, all_patches(): pl.pallas_call(functools.partial(patches_kernel, scale=scale), grid=(coun...  15.7 us
    pallas_call x1, Pallas kernels, prepare(): pl.pallas_call(prepare_kernel, grid=(count,), out_shape=(jax.ShapeDtypeSt...  8.18 us
    ppermute x1, starting transfers between devices, long_way(): return lax.ppermute(value, 'col', pairs)  5 us
    ppermute x2, starting transfers between devices, round_ring(): lax.ppermute(value, 'col', [(i, i // 4 * 4 + (i + step) % 4) for i in ran...  4.32 us
  transfers between devices with their start and end apart: 32, of which 16 were waited for; matrix products, arithmetic and copies ran while one was open for 1% of the time, Pallas kernels for 4%

profile of v8, /device:TPU:31, one launch (start us, length us, event | category | flops | bytes accessed | tf_op | source)
XLA Modules:
  0.0 205.7 jit_solution(15706962827357484804)
XLA Ops:
  0.7 2.5 %fusion.2 = (f32[2,128,512]{2,1,0:T(8,128)}, f32[2,128,512]{2,1,0:T(8,128)}) fusion(f32[2,512,512]{2,1,0:T(8,128)} %tile.1), kind=kLoop, calls=%fused_computation.19 | loop fusion | bytes 2097152 | tf_op jit(solution)/shard_map/slice | solution.py:404
  4.6 8.1 %collective-permute-start = (f32[2,256,256]{2,1,0:T(8,128)S(1)}, f32[2,256,256]{2,1,0:T(8,128)S(1)}, u32[]{:S(2)}, u32[]{:S(2)}) collective-permute-start(f32[2,256,256]{2,1,0:T(8,128)S(1)} %slice.71), channel_id=1, source_target_pairs={{1,0},{2,1},{3,2},{4,3},{5,4},{6,5},{7,6},{8,7},{9,8},{10,9},{11,1... | collective-permute-start | bytes 1572872 | tf_op jit(solution)/shard_map/ppermute | solution.py:20
  12.9 5.3 %collective-permute-start.1 = (f32[2,128,256]{2,1,0:T(8,128)S(1)}, f32[2,128,256]{2,1,0:T(8,128)S(1)}, u32[]{:S(2)}, u32[]{:S(2)}) collective-permute-start(f32[2,128,256]{2,1,0:T(8,128)S(1)} %get-tuple-element.49), channel_id=1, source_target_pairs={{1,0},{2,1},{3,2},{4,3},{5,4},{6,5},{7,6},{8,7},{9,8},{10,9},{11,1... | collective-permute-start | bytes 786440 | tf_op jit(solution)/shard_map/ppermute | solution.py:20
  18.2 3.5 %collective-permute-start.6 = (f32[2,128,512]{2,1,0:T(8,128)}, f32[2,128,512]{2,1,0:T(8,128)S(1)}, u32[]{:S(2)}, u32[]{:S(2)}) collective-permute-start(f32[2,128,512]{2,1,0:T(8,128)} %get-tuple-element.46), channel_id=1, source_target_pairs={{16,0},{32,16},{48,32},{64,48},{80,64},{96,80},{112,96},{144,128},... | collective-permute-start | bytes 1572872 | tf_op jit(solution)/shard_map/ppermute | solution.py:385
  21.7 1.7 collective-permute-done.2
  23.4 7.3 %collective-permute-start.5 = (f32[2,128,512]{2,1,0:T(8,128)}, f32[2,128,512]{2,1,0:T(8,128)S(1)}, u32[]{:S(2)}, u32[]{:S(2)}) collective-permute-start(f32[2,128,512]{2,1,0:T(8,128)} %get-tuple-element.47), channel_id=1, source_target_pairs={{16,0},{32,16},{48,32},{64,48},{80,64},{96,80},{112,96},{128,112},... | collective-permute-start | bytes 1572872 | tf_op jit(solution)/shard_map/ppermute | solution.py:20
  30.8 12.8 %collective-permute-done.1.middle = f32[2,128,256]{2,1,0:T(8,128)S(1)} collective-permute-done((f32[2,128,256]{2,1,0:T(8,128)S(1)}, f32[2,128,256]{2,1,0:T(8,128)S(1)}, u32[]{:S(2)}, u32[]{:S(2)}) %collective-permute-start.1) | collective-permute-done | bytes 262176 | tf_op jit(solution)/shard_map/ppermute | solution.py:20
  43.6 4.2 %collective-permute-start.3 = (f32[2,128,256]{2,1,0:T(8,128)S(1)}, f32[2,128,256]{2,1,0:T(8,128)S(1)}, u32[]{:S(2)}, u32[]{:S(2)}) collective-permute-start(f32[2,128,256]{2,1,0:T(8,128)S(1)} %collective-permute-done.2), channel_id=1, source_target_pairs={{0,1},{1,2},{2,3},{3,0},{4,5},{5,6},{6,7},{7,4},{8,9},{9,10},{10,1... | collective-permute-start | bytes 786440 | tf_op jit(solution)/shard_map/ppermute | solution.py:351
  49.2 2.8 %collective-permute-start.9 = (f32[2,256,256]{2,1,0:T(8,128)S(1)}, f32[2,256,256]{2,1,0:T(8,128)S(1)}, u32[]{:S(2)}, u32[]{:S(2)}) collective-permute-start(f32[2,256,256]{2,1,0:T(8,128)S(1)} %collective-permute-done.upper), channel_id=1, source_target_pairs={{16,0},{32,16},{48,32},{64,48},{80,64},{96,80},{112,96},{128,112},... | collective-permute-start | bytes 1572872 | tf_op jit(solution)/shard_map/ppermute | solution.py:20
  52.0 2.0 collective-permute-done.3
  54.0 5.0 %collective-permute-start.4 = (f32[2,128,256]{2,1,0:T(8,128)S(1)}, f32[2,128,256]{2,1,0:T(8,128)S(1)}, u32[]{:S(2)}, u32[]{:S(2)}) collective-permute-start(f32[2,128,256]{2,1,0:T(8,128)S(1)} %collective-permute-done.3), channel_id=1, source_target_pairs={{0,1},{1,2},{3,0},{4,5},{5,6},{6,3},{7,4},{8,9},{9,10},{10,7},{11,... | collective-permute-start | bytes 786440 | tf_op jit(solution)/shard_map/ppermute | solution.py:378
  59.6 8.2 %shard_map.86 = (f32[8,2,256,128]{3,2,1,0:T(8,128)}, f32[8,2,256,256]{3,2,1,0:T(8,128)}) custom-call(s32[8,2]{1,0:T(8,128)} %copy.10.off, f32[8,256,256]{2,1,0:T(8,128)} %bitcast.7, f32[2,256,256]{2,1,0:T(8,128)} %probe.1, bf16[2,256,256]{2,1,0:T(8,128)(2,1)} %constant.78.clone.pick), custom_call_target="tpu_custom_call" | custom-call | tf_op jit(solution)/shard_map/pallas_call | solution.py:96
  69.2 15.7 %shard_map.87 = (f32[2,512,512]{2,1,0:T(8,128)}, f32[2,256,256]{2,1,0:T(8,128)S(1)}, f32[2,256,256]{2,1,0:T(8,128)S(1)}, f32[2,128,512]{2,1,0:T(8,128)S(1)}, f32...) custom-call(s32[8,2]{1,0:T(8,128)S(1)} %copy-done, f32[2,512,512]{2,1,0:T(8,128)} %tile.1, ...), custom_call_target="tpu_custom_call" | custom-call | tf_op jit(solution)/shard_map/pallas_call | solution.py:287
  85.8 6.8 %collective-permute-start.17 = (f32[256,256]{1,0:T(8,128)S(1)}, f32[256,256]{1,0:T(8,128)}, u32[]{:S(2)}, u32[]{:S(2)}) collective-permute-start(f32[256,256]{1,0:T(8,128)S(1)} %select_bitcast_fusion), channel_id=1, source_target_pairs={{0,16},{16,0},{32,48},{48,32},{64,80},{80,64},{96,112},{112,96},{1... | collective-permute-start | bytes 786440 | tf_op jit(solution)/shard_map/ppermute | solution.py:307
  96.5 2.3 %collective-permute-start.20 = (f32[64,256]{1,0:T(8,128)S(1)}, f32[64,256]{1,0:T(8,128)S(1)}, u32[]{:S(2)}, u32[]{:S(2)}) collective-permute-start(f32[64,256]{1,0:T(8,128)S(1)} %get-tuple-element.53), channel_id=1, source_target_pairs={{0,96},{16,112},{32,64},{48,80},{64,32},{80,48},{96,0},{112,16},{1... | collective-permute-start | bytes 196616 | tf_op jit(solution)/shard_map/ppermute | solution.py:307
  100.1 1.7 collective-permute-done.20
  101.9 4.4 %collective-permute-start.21 = (f32[64,256]{1,0:T(8,128)S(1)}, f32[64,256]{1,0:T(8,128)S(1)}, u32[]{:S(2)}, u32[]{:S(2)}) collective-permute-start(f32[64,256]{1,0:T(8,128)S(1)} %add_add_fusion.2), channel_id=1, source_target_pairs={{0,4},{1,5},{2,6},{3,7},{4,0},{5,1},{6,2},{7,3},{8,12},{9,13},{10,... | collective-permute-start | bytes 196616 | tf_op jit(solution)/shard_map/ppermute | solution.py:307
  106.2 1.9 collective-permute-start.22
  108.7 2.7 %collective-permute-done.22 = f32[64,256]{1,0:T(8,128)S(1)} collective-permute-done((f32[64,256]{1,0:T(8,128)S(1)}, f32[64,256]{1,0:T(8,128)S(1)}, u32[]{:S(2)}, u32[]{:S(2)}) %collective-permute-start.22) | collective-permute-done | bytes 65568 | tf_op jit(solution)/shard_map/ppermute | solution.py:307
  111.4 1.7 collective-permute-done.23
  113.2 3.1 %collective-permute-done.24 = f32[64,256]{1,0:T(8,128)S(1)} collective-permute-done((f32[64,256]{1,0:T(8,128)S(1)}, f32[64,256]{1,0:T(8,128)S(1)}, u32[]{:S(2)}, u32[]{:S(2)}) %collective-permute-start.24) | collective-permute-done | bytes 65568 | tf_op jit(solution)/shard_map/ppermute | solution.py:307
  116.5 1.6 collective-permute-start.26
  118.0 4.1 %collective-permute-start.27 = (f32[64,256]{1,0:T(8,128)S(1)}, f32[64,256]{1,0:T(8,128)S(1)}, u32[]{:S(2)}, u32[]{:S(2)}) collective-permute-start(f32[64,256]{1,0:T(8,128)S(1)} %add.84), channel_id=1, source_target_pairs={{0,3},{1,2},{2,1},{3,0},{4,7},{5,6},{6,5},{7,4},{8,11},{9,10},{10,... | collective-permute-start | bytes 196616 | tf_op jit(solution)/shard_map/ppermute | solution.py:307
  122.1 2.5 %collective-permute-start.12 = (f32[2,128,512]{2,1,0:T(8,128)S(1)}, f32[2,128,512]{2,1,0:T(8,128)S(1)}, u32[]{:S(2)}, u32[]{:S(2)}) collective-permute-start(f32[2,128,512]{2,1,0:T(8,128)S(1)} %get-tuple-element.39), channel_id=1, source_target_pairs={{112,16},{113,17},{114,18},{115,19},{116,20},{117,21},{118,22},{11... | collective-permute-start | bytes 1572872 | tf_op jit(solution)/shard_map/ppermute | solution.py:392
  126.0 9.4 %collective-permute-start.14 = (f32[2,256,256]{2,1,0:T(8,128)S(1)}, f32[2,256,256]{2,1,0:T(8,128)S(1)}, u32[]{:S(2)}, u32[]{:S(2)}) collective-permute-start(f32[2,256,256]{2,1,0:T(8,128)S(1)} %copy-done.2), channel_id=1, source_target_pairs={{0,16},{16,32},{32,48},{48,64},{64,80},{80,96},{96,112},{112,128},... | collective-permute-start | bytes 1572872 | tf_op jit(solution)/shard_map/ppermute | solution.py:20
  135.7 4.4 %collective-permute-done.29 = f32[64,256]{1,0:T(8,128)S(1)} collective-permute-done((f32[64,256]{1,0:T(8,128)S(1)}, f32[64,256]{1,0:T(8,128)S(1)}, u32[]{:S(2)}, u32[]{:S(2)}) %collective-permute-start.29) | collective-permute-done | bytes 65568 | tf_op jit(solution)/shard_map/ppermute | solution.py:307
  144.0 10.6 %collective-permute-start.10 = (f32[2,128,512]{2,1,0:T(8,128)S(1)}, f32[2,128,512]{2,1,0:T(8,128)S(1)}, u32[]{:S(2)}, u32[]{:S(2)}) collective-permute-start(f32[2,128,512]{2,1,0:T(8,128)S(1)} %get-tuple-element.38), channel_id=1, source_target_pairs={{0,16},{16,32},{32,48},{48,64},{64,80},{80,96},{96,112},{112,128},... | collective-permute-start | bytes 1572872 | tf_op jit(solution)/shard_map/ppermute | solution.py:20
  154.6 1.9 collective-permute-start.16
  156.6 3.1 %collective-permute-start.15 = (f32[2,256,256]{2,1,0:T(8,128)S(1)}, f32[2,256,256]{2,1,0:T(8,128)S(1)}, u32[]{:S(2)}, u32[]{:S(2)}) collective-permute-start(f32[2,256,256]{2,1,0:T(8,128)S(1)} %add.71), channel_id=1, source_target_pairs={{0,1},{1,2},{2,3},{3,4},{4,5},{5,6},{6,7},{7,8},{8,9},{9,10},{10,1... | collective-permute-start | bytes 1572872 | tf_op jit(solution)/shard_map/ppermute | solution.py:20
  160.7 5.6 %collective-permute-done.10 = f32[2,128,512]{2,1,0:T(8,128)S(1)} collective-permute-done((f32[2,128,512]{2,1,0:T(8,128)S(1)}, f32[2,128,512]{2,1,0:T(8,128)S(1)}, u32[]{:S(2)}, u32[]{:S(2)}) %collective-permute-start.10) | collective-permute-done | bytes 524320 | tf_op jit(solution)/shard_map/ppermute | solution.py:20
  166.6 31.9 %collective-permute-done.16 = f32[2,256,256]{2,1,0:T(8,128)S(1)} collective-permute-done((f32[2,256,256]{2,1,0:T(8,128)S(1)}, f32[2,256,256]{2,1,0:T(8,128)S(1)}, u32[]{:S(2)}, u32[]{:S(2)}) %collective-permute-start.16) | collective-permute-done | bytes 524320 | tf_op jit(solution)/shard_map/ppermute | solution.py:20
  198.5 5.6 %collective-permute-done.15 = f32[2,256,256]{2,1,0:T(8,128)S(1)} collective-permute-done((f32[2,256,256]{2,1,0:T(8,128)S(1)}, f32[2,256,256]{2,1,0:T(8,128)S(1)}, u32[]{:S(2)}, u32[]{:S(2)}) %collective-permute-start.15) | collective-permute-done | bytes 524320 | tf_op jit(solution)/shard_map/ppermute | solution.py:20
  (79 shorter events, 20.1 us)
Async XLA Ops:
  3.1 44.7 %collective-permute-start.7 = (f32[2,128,512]{2,1,0:T(8,128)}, f32[2,128,512]{2,1,0:T(8,128)}, u32[]{:S(2)}, u32[]{:S(2)}) collective-permute-start(f32[2,128,512]{2,1,0:T(8,128)} %get-tuple-element.46), channel_id=1, source_target_pairs={{128,224},{129,225},{130,226},{131,227},{132,228},{133,229},{134,2... | collective-permute-start | bytes 1572872 | tf_op jit(solution)/shard_map/ppermute | solution.py:384
  4.6 44.5 %collective-permute-start = (f32[2,256,256]{2,1,0:T(8,128)S(1)}, f32[2,256,256]{2,1,0:T(8,128)S(1)}, u32[]{:S(2)}, u32[]{:S(2)}) collective-permute-start(f32[2,256,256]{2,1,0:T(8,128)S(1)} %slice.71), channel_id=1, source_target_pairs={{1,0},{2,1},{3,2},{4,3},{5,4},{6,5},{7,6},{8,7},{9,8},{10,9},{11,1... | collective-permute-start | bytes 1572872 | tf_op jit(solution)/shard_map/ppermute | solution.py:20
  12.8 10.6 %collective-permute-start.2 = (f32[2,128,256]{2,1,0:T(8,128)S(1)}, f32[2,128,256]{2,1,0:T(8,128)S(1)}, u32[]{:S(2)}, u32[]{:S(2)}) collective-permute-start(f32[2,128,256]{2,1,0:T(8,128)S(1)} %get-tuple-element.48), channel_id=1, source_target_pairs={{0,1},{1,2},{2,3},{3,0},{4,5},{5,6},{6,7},{7,4},{8,9},{9,10},{10,1... | collective-permute-start | bytes 786440 | tf_op jit(solution)/shard_map/ppermute | solution.py:351
  12.9 30.7 %collective-permute-start.1 = (f32[2,128,256]{2,1,0:T(8,128)S(1)}, f32[2,128,256]{2,1,0:T(8,128)S(1)}, u32[]{:S(2)}, u32[]{:S(2)}) collective-permute-start(f32[2,128,256]{2,1,0:T(8,128)S(1)} %get-tuple-element.49), channel_id=1, source_target_pairs={{1,0},{2,1},{3,2},{4,3},{5,4},{6,5},{7,6},{8,7},{9,8},{10,9},{11,1... | collective-permute-start | bytes 786440 | tf_op jit(solution)/shard_map/ppermute | solution.py:20
  18.2 49.6 %collective-permute-start.6 = (f32[2,128,512]{2,1,0:T(8,128)}, f32[2,128,512]{2,1,0:T(8,128)S(1)}, u32[]{:S(2)}, u32[]{:S(2)}) collective-permute-start(f32[2,128,512]{2,1,0:T(8,128)} %get-tuple-element.46), channel_id=1, source_target_pairs={{16,0},{32,16},{48,32},{64,48},{80,64},{96,80},{112,96},{144,128},... | collective-permute-start | bytes 1572872 | tf_op jit(solution)/shard_map/ppermute | solution.py:385
  23.4 44.4 %collective-permute-start.5 = (f32[2,128,512]{2,1,0:T(8,128)}, f32[2,128,512]{2,1,0:T(8,128)S(1)}, u32[]{:S(2)}, u32[]{:S(2)}) collective-permute-start(f32[2,128,512]{2,1,0:T(8,128)} %get-tuple-element.47), channel_id=1, source_target_pairs={{16,0},{32,16},{48,32},{64,48},{80,64},{96,80},{112,96},{128,112},... | collective-permute-start | bytes 1572872 | tf_op jit(solution)/shard_map/ppermute | solution.py:20
  43.6 10.3 %collective-permute-start.3 = (f32[2,128,256]{2,1,0:T(8,128)S(1)}, f32[2,128,256]{2,1,0:T(8,128)S(1)}, u32[]{:S(2)}, u32[]{:S(2)}) collective-permute-start(f32[2,128,256]{2,1,0:T(8,128)S(1)} %collective-permute-done.2), channel_id=1, source_target_pairs={{0,1},{1,2},{2,3},{3,0},{4,5},{5,6},{6,7},{7,4},{8,9},{9,10},{10,1... | collective-permute-start | bytes 786440 | tf_op jit(solution)/shard_map/ppermute | solution.py:351
  47.9 20.0 %collective-permute-start.8 = (f32[2,128,512]{2,1,0:T(8,128)}, f32[2,128,512]{2,1,0:T(8,128)S(1)}, u32[]{:S(2)}, u32[]{:S(2)}) collective-permute-start(f32[2,128,512]{2,1,0:T(8,128)} %collective-permute-done.7), channel_id=1, source_target_pairs={{224,112},{225,113},{226,114},{227,115},{228,116},{229,117},{230,1... | collective-permute-start | bytes 1572872 | tf_op jit(solution)/shard_map/ppermute | solution.py:386
  49.2 18.7 %collective-permute-start.9 = (f32[2,256,256]{2,1,0:T(8,128)S(1)}, f32[2,256,256]{2,1,0:T(8,128)S(1)}, u32[]{:S(2)}, u32[]{:S(2)}) collective-permute-start(f32[2,256,256]{2,1,0:T(8,128)S(1)} %collective-permute-done.upper), channel_id=1, source_target_pairs={{16,0},{32,16},{48,32},{64,48},{80,64},{96,80},{112,96},{128,112},... | collective-permute-start | bytes 1572872 | tf_op jit(solution)/shard_map/ppermute | solution.py:20
  54.0 13.9 %collective-permute-start.4 = (f32[2,128,256]{2,1,0:T(8,128)S(1)}, f32[2,128,256]{2,1,0:T(8,128)S(1)}, u32[]{:S(2)}, u32[]{:S(2)}) collective-permute-start(f32[2,128,256]{2,1,0:T(8,128)S(1)} %collective-permute-done.3), channel_id=1, source_target_pairs={{0,1},{1,2},{3,0},{4,5},{5,6},{6,3},{7,4},{8,9},{9,10},{10,7},{11,... | collective-permute-start | bytes 786440 | tf_op jit(solution)/shard_map/ppermute | solution.py:378
  85.8 8.1 %collective-permute-start.17 = (f32[256,256]{1,0:T(8,128)S(1)}, f32[256,256]{1,0:T(8,128)}, u32[]{:S(2)}, u32[]{:S(2)}) collective-permute-start(f32[256,256]{1,0:T(8,128)S(1)} %select_bitcast_fusion), channel_id=1, source_target_pairs={{0,16},{16,0},{32,48},{48,32},{64,80},{80,64},{96,112},{112,96},{1... | collective-permute-start | bytes 786440 | tf_op jit(solution)/shard_map/ppermute | solution.py:307
  94.9 4.0 %collective-permute-start.18 = (f32[64,256]{1,0:T(8,128)S(1)}, f32[64,256]{1,0:T(8,128)S(1)}, u32[]{:S(2)}, u32[]{:S(2)}) collective-permute-start(f32[64,256]{1,0:T(8,128)S(1)} %get-tuple-element.52), channel_id=1, source_target_pairs={{0,32},{16,48},{32,0},{48,16},{64,96},{80,112},{96,64},{112,80},{1... | collective-permute-start | bytes 196616 | tf_op jit(solution)/shard_map/ppermute | solution.py:307
  95.5 4.6 %collective-permute-start.19 = (f32[64,256]{1,0:T(8,128)S(1)}, f32[64,256]{1,0:T(8,128)S(1)}, u32[]{:S(2)}, u32[]{:S(2)}) collective-permute-start(f32[64,256]{1,0:T(8,128)S(1)} %get-tuple-element.54), channel_id=1, source_target_pairs={{0,64},{16,80},{32,96},{48,112},{64,0},{80,16},{96,32},{112,48},{1... | collective-permute-start | bytes 196616 | tf_op jit(solution)/shard_map/ppermute | solution.py:307
  96.5 5.3 %collective-permute-start.20 = (f32[64,256]{1,0:T(8,128)S(1)}, f32[64,256]{1,0:T(8,128)S(1)}, u32[]{:S(2)}, u32[]{:S(2)}) collective-permute-start(f32[64,256]{1,0:T(8,128)S(1)} %get-tuple-element.53), channel_id=1, source_target_pairs={{0,96},{16,112},{32,64},{48,80},{64,32},{80,48},{96,0},{112,16},{1... | collective-permute-start | bytes 196616 | tf_op jit(solution)/shard_map/ppermute | solution.py:307
  101.9 6.9 %collective-permute-start.21 = (f32[64,256]{1,0:T(8,128)S(1)}, f32[64,256]{1,0:T(8,128)S(1)}, u32[]{:S(2)}, u32[]{:S(2)}) collective-permute-start(f32[64,256]{1,0:T(8,128)S(1)} %add_add_fusion.2), channel_id=1, source_target_pairs={{0,4},{1,5},{2,6},{3,7},{4,0},{5,1},{6,2},{7,3},{8,12},{9,13},{10,... | collective-permute-start | bytes 196616 | tf_op jit(solution)/shard_map/ppermute | solution.py:307
  106.2 5.2 %collective-permute-start.22 = (f32[64,256]{1,0:T(8,128)S(1)}, f32[64,256]{1,0:T(8,128)S(1)}, u32[]{:S(2)}, u32[]{:S(2)}) collective-permute-start(f32[64,256]{1,0:T(8,128)S(1)} %add_add_fusion.2), channel_id=1, source_target_pairs={{0,8},{1,9},{2,10},{3,11},{4,12},{5,13},{6,14},{7,15},{8,0},{9,1},... | collective-permute-start | bytes 196616 | tf_op jit(solution)/shard_map/ppermute | solution.py:307
  108.2 4.9 %collective-permute-start.23 = (f32[64,256]{1,0:T(8,128)S(1)}, f32[64,256]{1,0:T(8,128)S(1)}, u32[]{:S(2)}, u32[]{:S(2)}) collective-permute-start(f32[64,256]{1,0:T(8,128)S(1)} %add_add_fusion.2), channel_id=1, source_target_pairs={{0,12},{1,13},{2,14},{3,15},{4,8},{5,9},{6,10},{7,11},{8,4},{9,5},... | collective-permute-start | bytes 196616 | tf_op jit(solution)/shard_map/ppermute | solution.py:307
  113.1 3.2 %collective-permute-start.24 = (f32[64,256]{1,0:T(8,128)S(1)}, f32[64,256]{1,0:T(8,128)S(1)}, u32[]{:S(2)}, u32[]{:S(2)}) collective-permute-start(f32[64,256]{1,0:T(8,128)S(1)} %add_add_fusion.1), channel_id=1, source_target_pairs={{0,128},{16,144},{32,160},{48,176},{64,192},{80,208},{96,224},{112... | collective-permute-start | bytes 196616 | tf_op jit(solution)/shard_map/ppermute | solution.py:307
  116.4 8.3 %collective-permute-start.25 = (f32[64,256]{1,0:T(8,128)S(1)}, f32[64,256]{1,0:T(8,128)S(1)}, u32[]{:S(2)}, u32[]{:S(2)}) collective-permute-start(f32[64,256]{1,0:T(8,128)S(1)} %add.84), channel_id=1, source_target_pairs={{0,1},{1,0},{2,3},{3,2},{4,5},{5,4},{6,7},{7,6},{8,9},{9,8},{10,11... | collective-permute-start | bytes 196616 | tf_op jit(solution)/shard_map/ppermute | solution.py:307
  116.5 8.4 %collective-permute-start.26 = (f32[64,256]{1,0:T(8,128)S(1)}, f32[64,256]{1,0:T(8,128)S(1)}, u32[]{:S(2)}, u32[]{:S(2)}) collective-permute-start(f32[64,256]{1,0:T(8,128)S(1)} %add.84), channel_id=1, source_target_pairs={{0,2},{1,3},{2,0},{3,1},{4,6},{5,7},{6,4},{7,5},{8,10},{9,11},{10,... | collective-permute-start | bytes 196616 | tf_op jit(solution)/shard_map/ppermute | solution.py:307
  118.0 7.8 %collective-permute-start.27 = (f32[64,256]{1,0:T(8,128)S(1)}, f32[64,256]{1,0:T(8,128)S(1)}, u32[]{:S(2)}, u32[]{:S(2)}) collective-permute-start(f32[64,256]{1,0:T(8,128)S(1)} %add.84), channel_id=1, source_target_pairs={{0,3},{1,2},{2,1},{3,0},{4,7},{5,6},{6,5},{7,4},{8,11},{9,10},{10,... | collective-permute-start | bytes 196616 | tf_op jit(solution)/shard_map/ppermute | solution.py:307
  122.1 21.2 %collective-permute-start.12 = (f32[2,128,512]{2,1,0:T(8,128)S(1)}, f32[2,128,512]{2,1,0:T(8,128)S(1)}, u32[]{:S(2)}, u32[]{:S(2)}) collective-permute-start(f32[2,128,512]{2,1,0:T(8,128)S(1)} %get-tuple-element.39), channel_id=1, source_target_pairs={{112,16},{113,17},{114,18},{115,19},{116,20},{117,21},{118,22},{11... | collective-permute-start | bytes 1572872 | tf_op jit(solution)/shard_map/ppermute | solution.py:392
  125.8 9.9 %collective-permute-start.28 = (f32[64,256]{1,0:T(8,128)S(1)}, f32[64,256]{1,0:T(8,128)S(1)}, u32[]{:S(2)}, u32[]{:S(2)}) collective-permute-start(f32[64,256]{1,0:T(8,128)S(1)} %get-tuple-element.45), channel_id=1, source_target_pairs={{0,32},{16,48},{32,0},{48,16},{64,96},{80,112},{96,64},{112,80},{1... | collective-permute-start | bytes 196616 | tf_op jit(solution)/shard_map/ppermute | solution.py:307
  126.0 28.6 %collective-permute-start.14 = (f32[2,256,256]{2,1,0:T(8,128)S(1)}, f32[2,256,256]{2,1,0:T(8,128)S(1)}, u32[]{:S(2)}, u32[]{:S(2)}) collective-permute-start(f32[2,256,256]{2,1,0:T(8,128)S(1)} %copy-done.2), channel_id=1, source_target_pairs={{0,16},{16,32},{32,48},{48,64},{64,80},{80,96},{96,112},{112,128},... | collective-permute-start | bytes 1572872 | tf_op jit(solution)/shard_map/ppermute | solution.py:20
  135.3 4.8 %collective-permute-start.29 = (f32[64,256]{1,0:T(8,128)S(1)}, f32[64,256]{1,0:T(8,128)S(1)}, u32[]{:S(2)}, u32[]{:S(2)}) collective-permute-start(f32[64,256]{1,0:T(8,128)S(1)} %get-tuple-element.45), channel_id=1, source_target_pairs={{0,64},{16,80},{32,96},{48,112},{64,0},{80,16},{96,32},{112,48},{1... | collective-permute-start | bytes 196616 | tf_op jit(solution)/shard_map/ppermute | solution.py:307
  135.4 5.8 %collective-permute-start.30 = (f32[64,256]{1,0:T(8,128)S(1)}, f32[64,256]{1,0:T(8,128)S(1)}, u32[]{:S(2)}, u32[]{:S(2)}) collective-permute-start(f32[64,256]{1,0:T(8,128)S(1)} %get-tuple-element.45), channel_id=1, source_target_pairs={{0,96},{16,112},{32,64},{48,80},{64,32},{80,48},{96,0},{112,16},{1... | collective-permute-start | bytes 196616 | tf_op jit(solution)/shard_map/ppermute | solution.py:307
  141.3 15.4 %collective-permute-start.31 = (f32[256,256]{1,0:T(8,128)S(1)}, f32[256,256]{1,0:T(8,128)S(1)}, u32[]{:S(2)}, u32[]{:S(2)}) collective-permute-start(f32[256,256]{1,0:T(8,128)S(1)} %constant_dynamic-update-slice_fusion), channel_id=1, source_target_pairs={{0,16},{16,0},{32,48},{48,32},{64,80},{80,64},{96,112},{112,96},{1... | collective-permute-start | bytes 786440 | tf_op jit(solution)/shard_map/ppermute | solution.py:307
  142.0 18.6 %collective-permute-start.11 = (f32[2,128,512]{2,1,0:T(8,128)S(1)}, f32[2,128,512]{2,1,0:T(8,128)S(1)}, u32[]{:S(2)}, u32[]{:S(2)}) collective-permute-start(f32[2,128,512]{2,1,0:T(8,128)S(1)} %get-tuple-element.39), channel_id=1, source_target_pairs={{0,16},{16,32},{32,48},{48,64},{64,80},{80,96},{96,112},{128,144},... | collective-permute-start | bytes 1572872 | tf_op jit(solution)/shard_map/ppermute | solution.py:393
  143.3 17.3 %collective-permute-start.13 = (f32[2,128,512]{2,1,0:T(8,128)S(1)}, f32[2,128,512]{2,1,0:T(8,128)S(1)}, u32[]{:S(2)}, u32[]{:S(2)}) collective-permute-start(f32[2,128,512]{2,1,0:T(8,128)S(1)} %collective-permute-done.12), channel_id=1, source_target_pairs={{16,128},{17,129},{18,130},{19,131},{20,132},{21,133},{22,134},{23... | collective-permute-start | bytes 1572872 | tf_op jit(solution)/shard_map/ppermute | solution.py:394
  144.0 22.3 %collective-permute-start.10 = (f32[2,128,512]{2,1,0:T(8,128)S(1)}, f32[2,128,512]{2,1,0:T(8,128)S(1)}, u32[]{:S(2)}, u32[]{:S(2)}) collective-permute-start(f32[2,128,512]{2,1,0:T(8,128)S(1)} %get-tuple-element.38), channel_id=1, source_target_pairs={{0,16},{16,32},{32,48},{48,64},{64,80},{80,96},{96,112},{112,128},... | collective-permute-start | bytes 1572872 | tf_op jit(solution)/shard_map/ppermute | solution.py:20
  154.6 43.9 %collective-permute-start.16 = (f32[2,256,256]{2,1,0:T(8,128)S(1)}, f32[2,256,256]{2,1,0:T(8,128)S(1)}, u32[]{:S(2)}, u32[]{:S(2)}) collective-permute-start(f32[2,256,256]{2,1,0:T(8,128)S(1)} %get-tuple-element.42), channel_id=1, source_target_pairs={{0,1},{1,2},{2,3},{3,4},{4,5},{5,6},{6,7},{7,8},{8,9},{9,10},{10,1... | collective-permute-start | bytes 1572872 | tf_op jit(solution)/shard_map/ppermute | solution.py:20
  156.6 47.5 %collective-permute-start.15 = (f32[2,256,256]{2,1,0:T(8,128)S(1)}, f32[2,256,256]{2,1,0:T(8,128)S(1)}, u32[]{:S(2)}, u32[]{:S(2)}) collective-permute-start(f32[2,256,256]{2,1,0:T(8,128)S(1)} %add.71), channel_id=1, source_target_pairs={{0,1},{1,2},{2,3},{3,4},{4,5},{5,6},{6,7},{7,8},{8,9},{9,10},{10,1... | collective-permute-start | bytes 1572872 | tf_op jit(solution)/shard_map/ppermute | solution.py:20
  (12 other events, 146.9 us)
